TPU v7x, 32 devices: a whole 2x2x4 slice. The times are simulated.
32 devices in a mesh: tp: 2 (over x), dp: 16 (over z, y, core).
Axes of the slice: x: 2, y: 2, z: 4, core: 2. Of those that a mesh axis runs over, the one named last changes fastest.
Arguments:
- layer_input: bfloat16 [2, 16, 64, 2048], P(None, 'dp', 'tp'), may hold values from -6 to 6
- query_weight: bfloat16 [2048, 2048], P('dp', 'tp'), may hold values from -0.125 to 0.125
- key_matrix: bfloat16 [2048, 1024], P('dp', 'tp'), may hold values from -0.125 to 0.125
- value_matrix: bfloat16 [2048, 1024], P('dp', 'tp'), may hold values from -0.125 to 0.125
- output_weight: bfloat16 [2048, 2048], P('tp', 'dp'), may hold values from -2 to 2
- gate_weight: bfloat16 [2048, 6144], P('dp', 'tp'), may hold values from -0.125 to 0.125
- up_weight: bfloat16 [2048, 6144], P('dp', 'tp'), may hold values from -0.125 to 0.125
- down_weight: bfloat16 [6144, 2048], P('tp', 'dp'), may hold values from -0.078125 to 0.078125
- attn_gain: float32 [2048], replicated, may hold values from 0.1 to 1.9
- mlp_gain: float32 [2048], replicated, may hold values from 0.1 to 1.9
- query_gain: float32 [128], replicated, may hold values from 0.8 to 1.8
- key_gain: float32 [128], replicated, may hold values from 0.8 to 1.8
- cotangent: bfloat16 [2, 16, 64, 2048], P(None, 'dp', 'tp'), may hold values from -6 to 6
Outputs:
- layer_output: bfloat16 [2, 16, 64, 2048], P(None, 'dp', 'tp')
- input_grad: bfloat16 [2, 16, 64, 2048], P(None, 'dp', 'tp')
- query_grad: float32 [2048, 2048], P('dp', 'tp')
- key_grad: float32 [2048, 1024], P('dp', 'tp')
- value_grad: float32 [2048, 1024], P('dp', 'tp')
- output_grad: float32 [2048, 2048], P('tp', 'dp')
- gate_grad: float32 [2048, 6144], P('dp', 'tp')
- up_grad: float32 [2048, 6144], P('dp', 'tp')
- down_grad: float32 [6144, 2048], P('tp', 'dp')
- attn_gain_grad: float32 [2048], replicated
- mlp_gain_grad: float32 [2048], replicated
- query_gain_grad: float32 [128], replicated
- key_gain_grad: float32 [128], replicated
All inputs are finite; a program needn't handle non-finite values.
Results may differ from a plain program's by a relative error of at most 0.018.
Values may be sent and summed in bfloat16 or wider, within the bound.
No kernel may reach another device: no remote copies, remote signals or barrier semaphores. Data moves between devices by JAX's collectives and lax.ppermute only.
A program may use at most 448 MiB of HBM per device.

v0:
```python
import jax
import jax.numpy as jnp
from jax import lax
from jax.sharding import PartitionSpec as P

HEAD_SIZE = 128
ROWS_DEV = 64
SEGMENTS = 2
SCORE_BLOCK_ROWS = 512


EPSILON = 1e-06
ROPE_BASE = 1000000.0
MASKED = -1e30


def norm_rows(value_rows, gain_vec):
    return (
        value_rows
        * lax.rsqrt(jnp.mean(value_rows * value_rows, axis=-1, keepdims=True) + EPSILON)
        * gain_vec
    )


def rotate(value_rows, cosine_table, sine_table):
    half_width = value_rows.shape[-1] // 2
    turned = jnp.concatenate([-value_rows[..., half_width:], value_rows[..., :half_width]], axis=-1)
    return value_rows * cosine_table + turned * sine_table


def tables(positions, head_width):
    half_width = head_width // 2
    inverse = ROPE_BASE ** (-(jnp.arange(half_width, dtype=jnp.float32) * 2.0 / head_width))
    angles = positions.astype(jnp.float32)[:, None] * inverse[None, :]
    angles = jnp.concatenate([angles, angles], axis=-1)[:, None, :]
    return (jnp.cos(angles), jnp.sin(angles))


def local(
    layer_input,
    query_weight,
    key_matrix,
    value_matrix,
    output_weight,
    gate_weight,
    up_weight,
    down_weight,
    attn_gain,
    mlp_gain,
    query_gain,
    key_gain,
    cotangent,
):
    data_ways = lax.axis_size("dp")
    place = lax.axis_index("dp")
    local_rows = ROWS_DEV
    segment_rows = local_rows * data_ways
    heads_q = query_weight.shape[1] // HEAD_SIZE
    heads_kv = key_matrix.shape[1] // HEAD_SIZE
    group_size = heads_q // heads_kv
    score_scale = HEAD_SIZE ** (-0.5)
    qwidth = heads_q * HEAD_SIZE
    kwidth = heads_kv * HEAD_SIZE
    ff_local = gate_weight.shape[1]
    full_width = gate_weight.shape[0] * data_ways

    def fetch_weights():
        return (
            lax.all_gather(query_weight, "dp", axis=0, tiled=True),
            lax.all_gather(key_matrix, "dp", axis=0, tiled=True),
            lax.all_gather(value_matrix, "dp", axis=0, tiled=True),
            lax.all_gather(output_weight, "dp", axis=1, tiled=True),
            lax.all_gather(gate_weight, "dp", axis=0, tiled=True),
            lax.all_gather(up_weight, "dp", axis=0, tiled=True),
            lax.all_gather(down_weight, "dp", axis=1, tiled=True),
        )

    def scores_at(query_rows, key_block, query_pos, key_index):
        offset = key_index * SCORE_BLOCK_ROWS
        raw_scores = (
            jnp.einsum("qkgd,skd->kgqs", query_rows, key_block, preferred_element_type=jnp.float32)
            * score_scale
        )
        key_pos = offset + jnp.arange(SCORE_BLOCK_ROWS, dtype=jnp.int32)
        return jnp.where(key_pos[None, :] <= query_pos[:, None], raw_scores, MASKED)

    cache_k = jnp.zeros((SEGMENTS * segment_rows, heads_kv, HEAD_SIZE), jnp.bfloat16)
    cache_v = jnp.zeros((SEGMENTS * segment_rows, heads_kv, HEAD_SIZE), jnp.bfloat16)
    outputs = []
    stored = []
    for segment in range(SEGMENTS):
        gathered = fetch_weights()
        q_full, k_full, v_full, o_full, gate_full, up_full, down_full = gathered
        resident = layer_input[segment, 0].astype(jnp.float32)
        normalized_rows = norm_rows(resident, attn_gain).astype(jnp.bfloat16)
        normed_all = lax.all_gather(normalized_rows, "tp", axis=0, tiled=True)
        query_pos = (
            segment * segment_rows + place * local_rows + jnp.arange(local_rows, dtype=jnp.int32)
        )
        cosine_table, sine_table = tables(query_pos, HEAD_SIZE)
        q_raw = jnp.dot(normed_all, q_full, preferred_element_type=jnp.float32).reshape(
            local_rows, heads_q, HEAD_SIZE
        )
        key_unrotated = jnp.dot(normed_all, k_full, preferred_element_type=jnp.float32).reshape(
            local_rows, heads_kv, HEAD_SIZE
        )
        value_rows = (
            jnp.dot(normed_all, v_full, preferred_element_type=jnp.float32)
            .astype(jnp.bfloat16)
            .reshape(local_rows, heads_kv, HEAD_SIZE)
        )
        query_rows = (
            rotate(norm_rows(q_raw, query_gain), cosine_table, sine_table)
            .astype(jnp.bfloat16)
            .reshape(local_rows, heads_kv, group_size, HEAD_SIZE)
        )
        key_rows = rotate(norm_rows(key_unrotated, key_gain), cosine_table, sine_table).astype(
            jnp.bfloat16
        )
        keys_all, values_all = (
            lax.all_gather(key_rows, "dp", axis=0, tiled=True),
            lax.all_gather(value_rows, "dp", axis=0, tiled=True),
        )
        cache_k = cache_k.at[segment * segment_rows : (segment + 1) * segment_rows].set(keys_all)
        cache_v = cache_v.at[segment * segment_rows : (segment + 1) * segment_rows].set(values_all)
        block_count = (
            segment * segment_rows + (place + 1) * local_rows + SCORE_BLOCK_ROWS - 1
        ) // SCORE_BLOCK_ROWS

        def stat_step(
            key_index, state_pair, query_rows=query_rows, query_pos=query_pos, cache_k=cache_k
        ):
            highest, summed = state_pair
            key_block = lax.dynamic_slice_in_dim(
                cache_k, key_index * SCORE_BLOCK_ROWS, SCORE_BLOCK_ROWS, 0
            )
            scores = scores_at(query_rows, key_block, query_pos, key_index)
            new_high = jnp.maximum(highest, jnp.max(scores, axis=-1))
            summed = summed * jnp.exp(highest - new_high) + jnp.sum(
                jnp.exp(scores - new_high[..., None]), axis=-1
            )
            return (new_high, summed)

        stat_shape = (heads_kv, group_size, local_rows)
        highest, summed = lax.fori_loop(
            0,
            block_count,
            stat_step,
            (jnp.full(stat_shape, MASKED, jnp.float32), jnp.zeros(stat_shape, jnp.float32)),
        )
        log_total = highest + jnp.log(summed)

        def value_step(
            key_index,
            accumulated,
            query_rows=query_rows,
            query_pos=query_pos,
            cache_k=cache_k,
            cache_v=cache_v,
            log_total=log_total,
        ):
            key_block = lax.dynamic_slice_in_dim(
                cache_k, key_index * SCORE_BLOCK_ROWS, SCORE_BLOCK_ROWS, 0
            )
            value_block = lax.dynamic_slice_in_dim(
                cache_v, key_index * SCORE_BLOCK_ROWS, SCORE_BLOCK_ROWS, 0
            )
            scores = scores_at(query_rows, key_block, query_pos, key_index)
            prob_rows = jnp.exp(scores - log_total[..., None]).astype(jnp.bfloat16)
            return accumulated + jnp.einsum(
                "kgqs,skd->qkgd", prob_rows, value_block, preferred_element_type=jnp.float32
            )

        attended = lax.fori_loop(
            0,
            block_count,
            value_step,
            jnp.zeros((local_rows, heads_kv, group_size, HEAD_SIZE), jnp.float32),
        )
        head_out = attended.astype(jnp.bfloat16).reshape(local_rows, qwidth)
        branch = lax.psum_scatter(
            jnp.dot(head_out, o_full, preferred_element_type=jnp.float32).astype(jnp.bfloat16),
            "tp",
            scatter_dimension=0,
            tiled=True,
        ).astype(jnp.float32)
        middle = resident + branch
        normed2 = norm_rows(middle, mlp_gain).astype(jnp.bfloat16)
        normed2_all = lax.all_gather(normed2, "tp", axis=0, tiled=True)
        gate_pre = jnp.dot(normed2_all, gate_full, preferred_element_type=jnp.float32)
        up_pre = jnp.dot(normed2_all, up_full, preferred_element_type=jnp.float32)
        active = (jax.nn.silu(gate_pre) * up_pre).astype(jnp.bfloat16)
        mlp_out = lax.psum_scatter(
            jnp.dot(active, down_full, preferred_element_type=jnp.float32).astype(jnp.bfloat16),
            "tp",
            scatter_dimension=0,
            tiled=True,
        ).astype(jnp.float32)
        outputs.append((middle + mlp_out).astype(jnp.bfloat16))
        stored.append(
            (
                resident,
                normed_all,
                q_raw,
                key_unrotated,
                query_rows,
                log_total,
                attended,
                head_out,
                middle,
                normed2_all,
                gate_pre,
                up_pre,
                active,
                query_pos,
                block_count,
            )
        )
    local_attn = jnp.zeros((full_width, 2 * qwidth + 2 * kwidth), jnp.float32)
    local_mlp = jnp.zeros((full_width, 3 * ff_local), jnp.float32)
    sum_attn_gain = jnp.zeros_like(attn_gain)
    sum_mlp_gain = jnp.zeros_like(mlp_gain)
    sum_query_gain = jnp.zeros_like(query_gain)
    sum_key_gain = jnp.zeros_like(key_gain)
    acc_k = jnp.zeros((SEGMENTS * segment_rows, heads_kv, HEAD_SIZE), jnp.float32)
    acc_v = jnp.zeros((SEGMENTS * segment_rows, heads_kv, HEAD_SIZE), jnp.float32)
    input_rows = [None] * SEGMENTS
    for segment in reversed(range(SEGMENTS)):
        gathered = fetch_weights()
        q_full, k_full, v_full, o_full, gate_full, up_full, down_full = gathered
        (
            resident,
            normed_all,
            q_raw,
            key_unrotated,
            query_rows,
            log_total,
            attended,
            head_out,
            middle,
            normed2_all,
            gate_pre,
            up_pre,
            active,
            query_pos,
            block_count,
        ) = stored[segment]
        incoming = cotangent[segment, 0]
        incoming_all = lax.all_gather(incoming, "tp", axis=0, tiled=True)
        d_active = jnp.einsum(
            "rd,fd->rf", incoming_all, down_full, preferred_element_type=jnp.float32
        )
        sigma = jax.nn.sigmoid(gate_pre)
        d_gate = (d_active * up_pre * sigma * (1.0 + gate_pre * (1.0 - sigma))).astype(jnp.bfloat16)
        d_upper = (d_active * gate_pre * sigma).astype(jnp.bfloat16)
        d_mlp_in = jnp.einsum(
            "rf,df->rd", d_gate, gate_full, preferred_element_type=jnp.float32
        ) + jnp.einsum("rf,df->rd", d_upper, up_full, preferred_element_type=jnp.float32)
        d_normed2 = lax.psum_scatter(
            d_mlp_in.astype(jnp.bfloat16), "tp", scatter_dimension=0, tiled=True
        ).astype(jnp.float32)
        gate_pair = jnp.concatenate([d_gate, d_upper], axis=1)

        def mlp_term(
            offset,
            extent,
            normed2_all=normed2_all,
            incoming_all=incoming_all,
            gate_pair=gate_pair,
            active=active,
        ):
            return jnp.concatenate(
                [
                    jnp.einsum(
                        "rc,rf->cf", normed2_all, gate_pair, preferred_element_type=jnp.float32
                    ),
                    jnp.einsum(
                        "rc,rf->cf", incoming_all, active, preferred_element_type=jnp.float32
                    ),
                ],
                axis=1,
            )

        local_mlp = local_mlp + mlp_term(0, full_width)
        _, pull_mlp = jax.vjp(norm_rows, middle, mlp_gain)
        d_mid_norm, d_mlp_gain = pull_mlp(d_normed2)
        sum_mlp_gain = sum_mlp_gain + d_mlp_gain
        d_middle = incoming.astype(jnp.float32) + d_mid_norm
        d_branch_all = lax.all_gather(d_middle.astype(jnp.bfloat16), "tp", axis=0, tiled=True)
        d_heads = (
            jnp.einsum("rd,hd->rh", d_branch_all, o_full, preferred_element_type=jnp.float32)
            .astype(jnp.bfloat16)
            .reshape(local_rows, heads_kv, group_size, HEAD_SIZE)
        )
        row_delta = jnp.sum(d_heads.astype(jnp.float32) * attended, axis=-1).transpose(1, 2, 0)

        def back_step(
            key_index,
            state_triple,
            query_rows=query_rows,
            query_pos=query_pos,
            log_total=log_total,
            d_heads=d_heads,
            row_delta=row_delta,
        ):
            d_query, grad_k, grad_v = state_triple
            offset = key_index * SCORE_BLOCK_ROWS
            key_block = lax.dynamic_slice_in_dim(cache_k, offset, SCORE_BLOCK_ROWS, 0)
            value_block = lax.dynamic_slice_in_dim(cache_v, offset, SCORE_BLOCK_ROWS, 0)
            scores = scores_at(query_rows, key_block, query_pos, key_index)
            prob_rows = jnp.exp(scores - log_total[..., None])
            d_probs = jnp.einsum(
                "qkgd,skd->kgqs", d_heads, value_block, preferred_element_type=jnp.float32
            )
            d_scores = (prob_rows * (d_probs - row_delta[..., None])).astype(jnp.bfloat16)
            d_query = d_query + jnp.einsum(
                "kgqs,skd->qkgd", d_scores, key_block, preferred_element_type=jnp.float32
            )
            key_part = jnp.einsum(
                "kgqs,qkgd->skd", d_scores, query_rows, preferred_element_type=jnp.float32
            )
            value_part = jnp.einsum(
                "kgqs,qkgd->skd",
                prob_rows.astype(jnp.bfloat16),
                d_heads,
                preferred_element_type=jnp.float32,
            )
            grad_k = lax.dynamic_update_slice_in_dim(
                grad_k,
                lax.dynamic_slice_in_dim(grad_k, offset, SCORE_BLOCK_ROWS, 0) + key_part,
                offset,
                0,
            )
            grad_v = lax.dynamic_update_slice_in_dim(
                grad_v,
                lax.dynamic_slice_in_dim(grad_v, offset, SCORE_BLOCK_ROWS, 0) + value_part,
                offset,
                0,
            )
            return (d_query, grad_k, grad_v)

        d_query, acc_k, acc_v = lax.fori_loop(
            0,
            block_count,
            back_step,
            (jnp.zeros((local_rows, heads_kv, group_size, HEAD_SIZE), jnp.float32), acc_k, acc_v),
        )
        piece_k = acc_k[segment * segment_rows : (segment + 1) * segment_rows].reshape(
            data_ways, local_rows, kwidth
        )
        piece_v = acc_v[segment * segment_rows : (segment + 1) * segment_rows].reshape(
            data_ways, local_rows, kwidth
        )
        mine_k, mine_v = (
            lax.psum_scatter(piece_k, "dp", scatter_dimension=0, tiled=True),
            lax.psum_scatter(piece_v, "dp", scatter_dimension=0, tiled=True),
        )
        mine_k = mine_k.reshape(local_rows, heads_kv, HEAD_SIZE) * score_scale
        cosine_table, sine_table = tables(query_pos, HEAD_SIZE)

        def prepare(raw_in, gain_in, cosine_table=cosine_table, sine_table=sine_table):
            return rotate(norm_rows(raw_in, gain_in), cosine_table, sine_table)

        _, pull_query = jax.vjp(prepare, q_raw, query_gain)
        d_q_raw, d_query_gain = pull_query(
            (d_query * score_scale).reshape(local_rows, heads_q, HEAD_SIZE)
        )
        _, pull_key = jax.vjp(prepare, key_unrotated, key_gain)
        d_k_raw, d_key_gain = pull_key(mine_k)
        sum_query_gain = sum_query_gain + d_query_gain
        sum_key_gain = sum_key_gain + d_key_gain
        d_q_low = d_q_raw.reshape(local_rows, qwidth).astype(jnp.bfloat16)
        d_k_low = d_k_raw.reshape(local_rows, kwidth).astype(jnp.bfloat16)
        d_v_low = mine_v.reshape(local_rows, kwidth).astype(jnp.bfloat16)
        d_attn_in = jnp.einsum("rf,df->rd", d_q_low, q_full, preferred_element_type=jnp.float32)
        d_attn_in = d_attn_in + jnp.einsum(
            "rf,df->rd", d_k_low, k_full, preferred_element_type=jnp.float32
        )
        d_attn_in = d_attn_in + jnp.einsum(
            "rf,df->rd", d_v_low, v_full, preferred_element_type=jnp.float32
        )
        d_normed = lax.psum_scatter(
            d_attn_in.astype(jnp.bfloat16), "tp", scatter_dimension=0, tiled=True
        ).astype(jnp.float32)
        combined = jnp.concatenate([d_q_low, d_k_low, d_v_low], axis=1)

        def attn_term(
            offset,
            extent,
            normed_all=normed_all,
            d_branch_all=d_branch_all,
            combined=combined,
            head_out=head_out,
        ):
            return jnp.concatenate(
                [
                    jnp.einsum(
                        "rc,rf->cf", normed_all, combined, preferred_element_type=jnp.float32
                    ),
                    jnp.einsum(
                        "rc,rf->cf", d_branch_all, head_out, preferred_element_type=jnp.float32
                    ),
                ],
                axis=1,
            )

        local_attn = local_attn + attn_term(0, full_width)
        _, pull_attn = jax.vjp(norm_rows, resident, attn_gain)
        d_resident, d_attn_gain = pull_attn(d_normed)
        sum_attn_gain = sum_attn_gain + d_attn_gain
        input_rows[segment] = (d_middle + d_resident).astype(jnp.bfloat16)
    grads_mlp = lax.psum_scatter(local_mlp, "dp", scatter_dimension=0, tiled=True)
    grads_attn = lax.psum_scatter(local_attn, "dp", scatter_dimension=0, tiled=True)
    gain_attn, gain_mlp, gain_query, gain_key = lax.psum(
        (sum_attn_gain, sum_mlp_gain, sum_query_gain, sum_key_gain), ("tp", "dp")
    )
    layer_output = jnp.stack(outputs)[:, None]
    input_grad = jnp.stack(input_rows)[:, None]
    query_grad = grads_attn[:, :qwidth]
    key_grad = grads_attn[:, qwidth : qwidth + kwidth]
    value_grad = grads_attn[:, qwidth + kwidth : qwidth + 2 * kwidth]
    output_grad = grads_attn[:, qwidth + 2 * kwidth :].T
    gate_grad = grads_mlp[:, :ff_local]
    up_grad = grads_mlp[:, ff_local : 2 * ff_local]
    down_grad = grads_mlp[:, 2 * ff_local :].T
    return (
        layer_output,
        input_grad,
        query_grad,
        key_grad,
        value_grad,
        output_grad,
        gate_grad,
        up_grad,
        down_grad,
        gain_attn,
        gain_mlp,
        gain_query,
        gain_key,
    )


def solution(mesh):
    in_specs = (
        P(None, "dp", "tp", None),
        P("dp", "tp"),
        P("dp", "tp"),
        P("dp", "tp"),
        P("tp", "dp"),
        P("dp", "tp"),
        P("dp", "tp"),
        P("tp", "dp"),
        P(),
        P(),
        P(),
        P(),
        P(None, "dp", "tp", None),
    )
    out_specs = (
        P(None, "dp", "tp", None),
        P(None, "dp", "tp", None),
        P("dp", "tp"),
        P("dp", "tp"),
        P("dp", "tp"),
        P("tp", "dp"),
        P("dp", "tp"),
        P("dp", "tp"),
        P("tp", "dp"),
        P(),
        P(),
        P(),
        P(),
    )
    return jax.shard_map(local, mesh=mesh, in_specs=in_specs, out_specs=out_specs, check_vma=False)
```

profile of v0, /device:TPU:0, one launch (start us, length us, event | category | flops | bytes accessed | tf_op | source)
XLA Modules:
  0.0 2141.9 jit_solution(9579014943429360079)
XLA Ops:
  11.0 7.1 all_gather.89
  18.1 5.7 all_gather.38
  24.8 29.5 %all-gather.18.cloned.1.call-done = bf16[2048,512]{1,0:T(8,128)(2,1)} async-done(((bf16[128,512]{1,0:T(8,128)(2,1)}), bf16[2048,512]{1,0:T(8,128)(2,1)}) %all-gather.18.cloned.1.call-update) | async-done | bytes 2097168 | tf_op jit(solution)/shard_map/all_gather | solution.py:70
  63.8 32.9 %all-gather.14.cloned.1.call-done = bf16[2048,512]{1,0:T(8,128)(2,1)} async-done(((bf16[128,512]{1,0:T(8,128)(2,1)}), bf16[2048,512]{1,0:T(8,128)(2,1)}) %all-gather.14.cloned.1.call-update) | async-done | bytes 2097168 | tf_op jit(solution)/shard_map/all_gather | solution.py:71
  103.8 32.4 %all-gather.20.cloned.1.call-done = bf16[1024,4,128]{2,1,0:T(4,128)(2,1)} async-done(((bf16[64,4,128]{2,1,0:T(4,128)(2,1)}), bf16[1024,4,128]{2,1,0:T(4,128)(2,1)}) %all-gather.20.cloned.1.call-update) | async-done | bytes 1048592 | tf_op jit(solution)/shard_map/all_gather | solution.py:121
  136.2 39.5 %all-gather.34.cloned.1.call-done = bf16[1024,4,128]{2,1,0:T(4,128)(2,1)} async-done(((bf16[64,4,128]{2,1,0:T(4,128)(2,1)}), bf16[1024,4,128]{2,1,0:T(4,128)(2,1)}) %all-gather.34.cloned.1.call-update) | async-done | bytes 1048592 | tf_op jit(solution)/shard_map/all_gather | solution.py:121
  182.6 32.6 %all-gather.16.cloned.1.call-done = bf16[1024,4,128]{2,0,1:T(8,128)(2,1)} async-done(((bf16[64,4,128]{2,0,1:T(8,128)(2,1)}), bf16[1024,4,128]{2,0,1:T(8,128)(2,1)}) %all-gather.16.cloned.1.call-update) | async-done | bytes 1048592 | tf_op jit(solution)/shard_map/all_gather | solution.py:122
  220.3 34.4 %all-gather.32.cloned.1.call-done = bf16[1024,4,128]{2,0,1:T(8,128)(2,1)} async-done(((bf16[64,4,128]{2,0,1:T(8,128)(2,1)}), bf16[1024,4,128]{2,0,1:T(8,128)(2,1)}) %all-gather.32.cloned.1.call-update) | async-done | bytes 1048592 | tf_op jit(solution)/shard_map/all_gather | solution.py:122
  257.0 49.3 %all-gather.22.cloned.1.call-done = bf16[2048,1024]{1,0:T(8,128)(2,1)} async-done(((bf16[128,1024]{1,0:T(8,128)(2,1)}), bf16[2048,1024]{1,0:T(8,128)(2,1)}) %all-gather.22.cloned.1.call-update) | async-done | bytes 4194320 | tf_op jit(solution)/shard_map/all_gather | solution.py:69
  321.6 5.1 while.85
  330.3 30.0 %all-gather.24.cloned.1.call-done = bf16[1024,2048]{1,0:T(8,128)(2,1)} async-done(((bf16[1024,128]{1,0:T(8,128)(2,1)}), bf16[1024,2048]{1,0:T(8,128)(2,1)}) %all-gather.24.cloned.1.call-update) | async-done | bytes 4194320 | tf_op jit(solution)/shard_map/all_gather | solution.py:72
  373.0 6.4 all-gather
  379.4 7.4 all-gather.1
  391.1 6.1 all_gather.85
  397.2 5.6 all_gather.92
  402.8 89.0 %all-gather.28.cloned.1.call-done = bf16[2048,3072]{1,0:T(8,128)(2,1)} async-done(((bf16[128,3072]{1,0:T(8,128)(2,1)}), bf16[2048,3072]{1,0:T(8,128)(2,1)}) %all-gather.28.cloned.1.call-update) | async-done | bytes 12582928 | tf_op jit(solution)/shard_map/all_gather | solution.py:74
  491.9 7.7 fusion.223
  499.6 93.4 %all-gather.26.cloned.1.call-done = bf16[2048,3072]{1,0:T(8,128)(2,1)} async-done(((bf16[128,3072]{1,0:T(8,128)(2,1)}), bf16[2048,3072]{1,0:T(8,128)(2,1)}) %all-gather.26.cloned.1.call-update) | async-done | bytes 12582928 | tf_op jit(solution)/shard_map/all_gather | solution.py:73
  593.0 7.8 fusion.222
  600.7 96.6 %all-gather.30.cloned.1.call-done = bf16[3072,2048]{1,0:T(8,128)(2,1)} async-done(((bf16[3072,128]{1,0:T(8,128)(2,1)}), bf16[3072,2048]{1,0:T(8,128)(2,1)}) %all-gather.30.cloned.1.call-update) | async-done | bytes 12582928 | tf_op jit(solution)/shard_map/all_gather | solution.py:75
  697.3 10.1 multiply_convert_fusion
  712.4 18.0 fusion.111
  730.5 7.8 fusion.219
  738.3 8.0 fusion.218
  746.3 10.2 multiply_convert_fusion.2
  761.4 9.2 fusion.110
  771.0 7.7 convolution_convert_fusion
  782.4 12.5 reduce-scatter.21.cloned.1.call-done
  796.9 5.9 all_gather.96
  806.7 5.6 all_gather.95
  821.0 21.9 %while.86 = (s32[]{:T(128)}, f32[64,4,2,128]{3,0,2,1:T(8,128)S(1)}, f32[2048,4,128]{2,0,1:T(8,128)}, f32[2048,4,128]{2,0,1:T(8,128)}, s32[]{:T(128)}, /*index=5*...) while((s32[]{:T(128)}, f32[64,4,2,128]{3,0,2,1:T(8,128)S(1)}, ...), condition=%wide.region_30.31_spmd.clone, body=%wide.region_29.30_spmd.clone.sunk | while | flops 338002496 | bytes 11610847 | solution.py:342
  853.5 7.7 while.87
  884.7 37.8 %reduce-scatter.33.cloned.1.call-done = f32[1,64,512]{2,1,0:T(8,128)} async-done(((f32[16,64,512]{2,1,0:T(8,128)}), f32[1,64,512]{2,1,0:T(8,128)}) %reduce-scatter.33.cloned.1.call-update) | async-done | bytes 131088 | tf_op jit(solution)/shard_map/reduce_scatter | solution.py:355
  923.4 63.3 %reduce-scatter.27.cloned.1.call-done = f32[1,64,512]{2,1,0:T(8,128)} async-done(((f32[16,64,512]{2,1,0:T(8,128)}), f32[1,64,512]{2,1,0:T(8,128)}) %reduce-scatter.27.cloned.1.call-update) | async-done | bytes 131088 | tf_op jit(solution)/shard_map/reduce_scatter | solution.py:355
  994.8 56.7 %reduce-scatter.35.cloned.1.call-done = f32[1,64,512]{2,1,0:T(8,128)} async-done(((f32[16,64,512]{2,1,0:T(8,128)}), f32[1,64,512]{2,1,0:T(8,128)}) %reduce-scatter.35.cloned.1.call-update) | async-done | bytes 131088 | tf_op jit(solution)/shard_map/reduce_scatter | solution.py:356
  1061.3 54.4 %reduce-scatter.29.cloned.1.call-done = f32[1,64,512]{2,1,0:T(8,128)} async-done(((f32[16,64,512]{2,1,0:T(8,128)}), f32[1,64,512]{2,1,0:T(8,128)}) %reduce-scatter.29.cloned.1.call-update) | async-done | bytes 131088 | tf_op jit(solution)/shard_map/reduce_scatter | solution.py:356
  1118.2 7.6 convolution_convert_fusion.2
  1135.5 8.2 fusion.156
  1143.7 8.1 fusion.162
  1151.8 26.0 %maximum_add_fusion.1 = f32[2048,3072]{0,1:T(8,128)} fusion(f32[2048,1024]{0,1:T(8,128)} %fusion.226, f32[2048,2048]{0,1:T(8,128)} %fusion.156, f32[2048,1024]{0,1:T(8,128)} %fusion.227, f32[2048,2048]{0,1:T(8,128)} %fusion.162), kind=kLoop, calls=%fused_computation.135 | loop fusion | flops 18874368 | bytes 75497472 | tf_op jit(solution)/shard_map/add | solution.py:407
  1178.9 15.3 convolution_bitcast_fusion.9
  1194.2 15.7 convolution_bitcast_fusion.8
  1210.0 20.5 fusion.120
  1230.5 19.7 fusion.116
  1250.2 73.7 %maximum_add_fusion = f32[2048,9216]{1,0:T(8,128)} fusion(f32[2048,3072]{1,0:T(8,128)} %convolution_bitcast_fusion.9, f32[2048,6144]{1,0:T(8,128)} %fusion.116, f32[2048,3072]{1,0:T(8,128)} %convolution_bitcast_fusion.8, f32[2048,6144]{1,0:T(8,128)} %fusion.120), kind=kLoop, calls=%fused_computation.134 | loop fusion | flops 56623104 | bytes 226492416 | tf_op jit(solution)/shard_map/add | solution.py:284
  1326.3 39.6 %all-reduce.10 = (f32[2048]{0:T(1024)}, f32[2048]{0:T(1024)}, f32[128]{0:T(128)}, f32[128]{0:T(128)}) all-reduce(f32[2048]{0:T(1024)S(1)} %add.469, f32[2048]{0:T(1024)S(1)} %add.470, f32[128]{0:T(128)S(1)} %add.471, f32[128]{0:T(128)S(1)} %add.472), channel_id=1, replica_groups=mesh['tp'=2,'dp'=16] {'tp','dp'}, use_global_device_ids=true, to_apply=%region_50.51 | all-reduce | flops 4352 | bytes 34816 | tf_op jit(solution)/shard_map/psum | solution.py:414
  1369.9 51.4 %reduce-scatter.39.cloned.1.call-done = f32[128,3072]{0,1:T(8,128)} async-done(((f32[2048,3072]{0,1:T(8,128)}), f32[128,3072]{0,1:T(8,128)}) %reduce-scatter.39.cloned.1.call-update) | async-done | bytes 1572880 | tf_op jit(solution)/shard_map/reduce_scatter | solution.py:413
  1427.1 701.7 %reduce-scatter.41.cloned.1.call-done = f32[128,9216]{1,0:T(8,128)} async-done(((f32[2048,9216]{1,0:T(8,128)}), f32[128,9216]{1,0:T(8,128)}) %reduce-scatter.41.cloned.1.call-update) | async-done | bytes 4718608 | tf_op jit(solution)/shard_map/reduce_scatter | solution.py:412
  (548 shorter events, 222.9 us)
Async XLA Ops:
  7.2 53.2 %copy-start.93 = (f32[128]{0:T(128)S(1)}, f32[128]{0:T(128)}, u32[]{:S(2)}) copy-start(f32[128]{0:T(128)} %param.44) | copy-start | bytes 1540
  7.2 47.1 %all-gather.18.cloned.1.call-start = ((), (), s32[]{:S(2)}) async-start(), calls=%async_computation.16 | async-start | bytes 2228224 | tf_op jit(solution)/shard_map/all_gather | solution.py:70
  7.9 88.8 %all-gather.14.cloned.1.call-start = ((), (), s32[]{:S(2)}) async-start(), calls=%async_computation.14 | async-start | bytes 2228224 | tf_op jit(solution)/shard_map/all_gather | solution.py:71
  8.7 127.5 %all-gather.20.cloned.1.call-start = ((), (), s32[]{:S(2)}) async-start(), calls=%async_computation.17 | async-start | bytes 1114112 | tf_op jit(solution)/shard_map/all_gather | solution.py:121
  18.1 293.1 %copy-start.14 = (bf16[64,2048]{1,0:T(8,128)(2,1)}, bf16[64,2048]{1,0:T(8,128)(2,1)S(1)}, u32[]{:S(2)}) copy-start(bf16[64,2048]{1,0:T(8,128)(2,1)S(1)} %all_gather.89) | copy-start | bytes 786436
  23.8 282.6 %copy-start.12 = (bf16[64,2048]{1,0:T(8,128)(2,1)}, bf16[64,2048]{1,0:T(8,128)(2,1)S(1)}, u32[]{:S(2)}) copy-start(bf16[64,2048]{1,0:T(8,128)(2,1)S(1)} %all_gather.38) | copy-start | bytes 786436
  24.8 293.0 %copy-start.65 = (f32[64,128]{1,0:T(8,128)}, f32[64,128]{1,0:T(8,128)S(1)}, u32[]{:S(2)}) copy-start(f32[64,128]{1,0:T(8,128)S(1)} %get-tuple-element.1007) | copy-start | bytes 98308
  24.8 293.0 %copy-start.69 = (f32[64,128]{1,0:T(8,128)}, f32[64,128]{1,0:T(8,128)S(1)}, u32[]{:S(2)}) copy-start(f32[64,128]{1,0:T(8,128)S(1)} %get-tuple-element.1006) | copy-start | bytes 98308
  61.9 113.7 %all-gather.34.cloned.1.call-start = ((), (), s32[]{:S(2)}) async-start(), calls=%async_computation.26 | async-start | bytes 1114112 | tf_op jit(solution)/shard_map/all_gather | solution.py:121
  62.8 255.0 %copy-start.67 = (f32[64,128]{1,0:T(8,128)}, f32[64,128]{1,0:T(8,128)S(1)}, u32[]{:S(2)}) copy-start(f32[64,128]{1,0:T(8,128)S(1)} %get-tuple-element.1011) | copy-start | bytes 98308
  62.8 255.0 %copy-start.71 = (f32[64,128]{1,0:T(8,128)}, f32[64,128]{1,0:T(8,128)S(1)}, u32[]{:S(2)}) copy-start(f32[64,128]{1,0:T(8,128)S(1)} %get-tuple-element.1010) | copy-start | bytes 98308
  63.7 151.4 %all-gather.16.cloned.1.call-start = ((), (), s32[]{:S(2)}) async-start(), calls=%async_computation.15 | async-start | bytes 1114112 | tf_op jit(solution)/shard_map/all_gather | solution.py:122
  99.4 155.3 %all-gather.32.cloned.1.call-start = ((), (), s32[]{:S(2)}) async-start(), calls=%async_computation.25 | async-start | bytes 1114112 | tf_op jit(solution)/shard_map/all_gather | solution.py:122
  102.2 204.1 %all-gather.22.cloned.1.call-start = ((), (), s32[]{:S(2)}) async-start(), calls=%async_computation.18 | async-start | bytes 4456448 | tf_op jit(solution)/shard_map/all_gather | solution.py:69
  103.0 257.3 %all-gather.24.cloned.1.call-start = ((), (), s32[]{:S(2)}) async-start(), calls=%async_computation.19 | async-start | bytes 4456448 | tf_op jit(solution)/shard_map/all_gather | solution.py:72
  103.7 283.1 %reduce-scatter.19.cloned.1.call-start = ((), (), s32[]{:S(2)}) async-start(), calls=%async_computation.27 | async-start | bytes 393216 | tf_op jit(solution)/shard_map/reduce_scatter | solution.py:181
  364.1 24.7 %reduce-scatter.15.cloned.1.call-start = ((), (), s32[]{:S(2)}) async-start(), calls=%async_computation.20 | async-start | bytes 393216 | tf_op jit(solution)/shard_map/reduce_scatter | solution.py:181
  370.8 121.1 %all-gather.28.cloned.1.call-start = ((), (), s32[]{:S(2)}) async-start(), calls=%async_computation.22 | async-start | bytes 13369344 | tf_op jit(solution)/shard_map/all_gather | solution.py:74
  371.5 221.4 %all-gather.26.cloned.1.call-start = ((), (), s32[]{:S(2)}) async-start(), calls=%async_computation.21 | async-start | bytes 13369344 | tf_op jit(solution)/shard_map/all_gather | solution.py:73
  372.1 325.2 %all-gather.30.cloned.1.call-start = ((), (), s32[]{:S(2)}) async-start(), calls=%async_computation.23 | async-start | bytes 13369344 | tf_op jit(solution)/shard_map/all_gather | solution.py:75
  372.9 405.9 %reduce-scatter.25.cloned.1.call-start = ((), (), s32[]{:S(2)}) async-start(), calls=%async_computation.30 | async-start | bytes 393216 | tf_op jit(solution)/shard_map/reduce_scatter | solution.py:259
  389.9 405.0 %copy-start.87 = (f32[32]{0:T(128)}, f32[32]{0:T(128)S(1)}, u32[]{:S(2)}) copy-start(f32[32]{0:T(128)S(1)} %fusion.197) | copy-start | bytes 388
  390.0 405.0 %copy-start.89 = (f32[32]{0:T(128)}, f32[32]{0:T(128)S(1)}, u32[]{:S(2)}) copy-start(f32[32]{0:T(128)S(1)} %fusion.199) | copy-start | bytes 388
  397.2 341.1 %copy-start.10 = (bf16[64,2048]{1,0:T(8,128)(2,1)}, bf16[64,2048]{1,0:T(8,128)(2,1)S(1)}, u32[]{:S(2)}) copy-start(bf16[64,2048]{1,0:T(8,128)(2,1)S(1)} %all_gather.85) | copy-start | bytes 786436
  402.8 190.2 %copy-start.8 = (bf16[64,2048]{1,0:T(8,128)(2,1)}, bf16[64,2048]{1,0:T(8,128)(2,1)S(1)}, u32[]{:S(2)}) copy-start(bf16[64,2048]{1,0:T(8,128)(2,1)S(1)} %all_gather.92) | copy-start | bytes 786436
  707.4 63.6 %copy-start.16 = (bf16[64,3072]{1,0:T(8,128)(2,1)}, bf16[64,3072]{1,0:T(8,128)(2,1)S(1)}, u32[]{:S(2)}) copy-start(bf16[64,3072]{1,0:T(8,128)(2,1)S(1)} %get-tuple-element.976) | copy-start | bytes 1179652
  730.4 50.2 %reduce-scatter.23.cloned.1.call-start = ((), (), s32[]{:S(2)}) async-start(), calls=%async_computation.29 | async-start | bytes 393216 | tf_op jit(solution)/shard_map/reduce_scatter | solution.py:259
  770.7 24.3 %reduce-scatter.21.cloned.1.call-start = ((), (), s32[]{:S(2)}) async-start(), calls=%async_computation.28 | async-start | bytes 393216 | tf_op jit(solution)/shard_map/reduce_scatter | solution.py:193
  778.7 143.7 %reduce-scatter.33.cloned.1.call-start = ((), (), s32[]{:S(2)}) async-start(), calls=%async_computation.34 | async-start | bytes 2228224 | tf_op jit(solution)/shard_map/reduce_scatter | solution.py:355
  853.4 133.3 %reduce-scatter.27.cloned.1.call-start = ((), (), s32[]{:S(2)}) async-start(), calls=%async_computation.31 | async-start | bytes 2228224 | tf_op jit(solution)/shard_map/reduce_scatter | solution.py:355
  866.2 185.3 %reduce-scatter.35.cloned.1.call-start = ((), (), s32[]{:S(2)}) async-start(), calls=%async_computation.35 | async-start | bytes 2228224 | tf_op jit(solution)/shard_map/reduce_scatter | solution.py:356
  871.2 244.4 %reduce-scatter.29.cloned.1.call-start = ((), (), s32[]{:S(2)}) async-start(), calls=%async_computation.32 | async-start | bytes 2228224 | tf_op jit(solution)/shard_map/reduce_scatter | solution.py:356
  878.7 446.0 %reduce-scatter.37.cloned.1.call-start = ((), (), s32[]{:S(2)}) async-start(), calls=%async_computation.36 | async-start | bytes 393216 | tf_op jit(solution)/shard_map/reduce_scatter | solution.py:382
  883.2 107.1 %copy-start.29 = (f32[64,4,128]{2,1,0:T(4,128)S(1)}, f32[64,4,128]{2,1,0:T(4,128)}, u32[]{:S(2)}) copy-start(f32[64,4,128]{2,1,0:T(4,128)} %copy-done.28) | copy-start | bytes 393220
  883.2 107.1 %copy-start.31 = (f32[64,4,128]{2,1,0:T(4,128)S(1)}, f32[64,4,128]{2,1,0:T(4,128)}, u32[]{:S(2)}) copy-start(f32[64,4,128]{2,1,0:T(4,128)} %copy-done.30) | copy-start | bytes 393220
  883.2 107.1 %copy-start.94 = (f32[128]{0:T(128)S(1)}, f32[128]{0:T(128)}, u32[]{:S(2)}) copy-start(f32[128]{0:T(128)} %param.44) | copy-start | bytes 1540
  883.3 111.3 %copy-start.84 = (f32[64,4]{0,1:T(4,128)S(1)}, f32[64,4]{0,1:T(4,128)}, u32[]{:S(2)}) copy-start(f32[64,4]{0,1:T(4,128)} %copy-done.83) | copy-start | bytes 3076
  883.3 111.4 %copy-start.86 = (f32[64,4]{0,1:T(4,128)S(1)}, f32[64,4]{0,1:T(4,128)}, u32[]{:S(2)}) copy-start(f32[64,4]{0,1:T(4,128)} %copy-done.85) | copy-start | bytes 3076
  884.7 172.7 %copy-start.5 = (bf16[2048,512]{1,0:T(8,128)(2,1)S(1)}, bf16[2048,512]{1,0:T(8,128)(2,1)}, u32[]{:S(2)}) copy-start(bf16[2048,512]{1,0:T(8,128)(2,1)} %all-gather.14.cloned.1.call-done) | copy-start | bytes 6291460
  1057.4 60.8 %copy-start.18 = (bf16[64,3072]{1,0:T(8,128)(2,1)S(1)}, bf16[64,3072]{1,0:T(8,128)(2,1)}, u32[]{:S(2)}) copy-start(bf16[64,3072]{1,0:T(8,128)(2,1)} %get-tuple-element.973) | copy-start | bytes 1179652
  1058.9 265.9 %reduce-scatter.31.cloned.1.call-start = ((), (), s32[]{:S(2)}) async-start(), calls=%async_computation.33 | async-start | bytes 393216 | tf_op jit(solution)/shard_map/reduce_scatter | solution.py:382
  1118.1 249.1 %reduce-scatter.17.cloned.1.call-start = ((), (), s32[]{:S(2)}) async-start(), calls=%async_computation.24 | async-start | bytes 393216 | tf_op jit(solution)/shard_map/reduce_scatter | solution.py:193
  1125.9 295.4 %reduce-scatter.39.cloned.1.call-start = ((), (), s32[]{:S(2)}) async-start(), calls=%async_computation.37 | async-start | bytes 26738688 | tf_op jit(solution)/shard_map/reduce_scatter | solution.py:413
  1177.9 950.9 %reduce-scatter.41.cloned.1.call-start = ((), (), s32[]{:S(2)}) async-start(), calls=%async_computation.38 | async-start | bytes 80216064 | tf_op jit(solution)/shard_map/reduce_scatter | solution.py:412
  1324.1 43.1 %copy-start.33 = (bf16[32,2048]{1,0:T(8,128)(2,1)S(1)}, bf16[32,2048]{1,0:T(8,128)(2,1)}, u32[]{:S(2)}) copy-start(bf16[32,2048]{1,0:T(8,128)(2,1)} %reduce-scatter.15.cloned.1.call-done) | copy-start | bytes 393220
  1324.1 43.1 %copy-start.53 = (bf16[32,2048]{1,0:T(8,128)(2,1)S(1)}, bf16[32,2048]{1,0:T(8,128)(2,1)}, u32[]{:S(2)}) copy-start(bf16[32,2048]{1,0:T(8,128)(2,1)} %reduce-scatter.23.cloned.1.call-done) | copy-start | bytes 393220
  1324.1 43.1 %copy-start.88 = (f32[32]{0:T(128)S(1)}, f32[32]{0:T(128)}, u32[]{:S(2)}) copy-start(f32[32]{0:T(128)} %copy-done.87) | copy-start | bytes 388
  1324.1 45.0 %copy-start.75 = (bf16[1,32,2048]{2,1,0:T(8,128)(2,1)S(1)}, bf16[1,32,2048]{2,1,0:T(8,128)(2,1)}, u32[]{:S(2)}) copy-start(bf16[1,32,2048]{2,1,0:T(8,128)(2,1)} %get-tuple-element.979) | copy-start | bytes 393220
  (95 other events, 1142.8 us)
Sparse Core Ops, SparseCore 0:
  10.2 44.0 all-gather.17
  56.5 40.1 all-gather.13
  99.4 36.6 all-gather.19
  138.8 36.8 all-gather.33
  178.2 36.8 all-gather.15
  217.8 36.8 all-gather.31
  256.8 49.4 all-gather.21
  308.5 51.7 all-gather.23
  364.2 9.8 reduce-scatter.18
  376.8 11.9 reduce-scatter.14
  391.1 100.7 all-gather.27
  494.0 98.9 all-gather.25
  595.1 102.1 all-gather.29
  730.6 9.8 reduce-scatter.24
  770.8 9.7 reduce-scatter.22
  783.3 11.6 reduce-scatter.20
  853.5 68.8 reduce-scatter.32
  926.0 60.5 reduce-scatter.26
  990.9 60.5 reduce-scatter.34
  1055.1 60.5 reduce-scatter.28
  1118.6 10.6 reduce-scatter.36
  1132.0 11.6 reduce-scatter.30
  1146.7 11.6 reduce-scatter.16
  1178.0 243.2 reduce-scatter.38
  1425.5 703.2 reduce-scatter.40
where the time goes:
time: 2150 us; the launch traced here: 2140 us
  waiting for transfers between devices  1550 us (72%)
  matrix products  281 us (13%)
  other arithmetic  138 us (6%)
  blocking collectives  89.5 us (4%)
  local copies, waits for them, and re-layouts  67.8 us (3%)
    reduce_scatter x1, waiting for transfers between devices, local(): lax.psum_scatter(local_mlp, 'dp', scatter_dimension=0, tiled=True)  702 us
    reduce_scatter x2, waiting for transfers between devices, local(): lax.psum_scatter(piece_v, 'dp', scatter_dimension=0, tiled=True)  111 us
    reduce_scatter x2, waiting for transfers between devices, local(): lax.psum_scatter(piece_k, 'dp', scatter_dimension=0, tiled=True)  101 us
    all_gather x1, waiting for transfers between devices, fetch_weights(): lax.all_gather(down_weight, 'dp', axis=1, tiled=True)  96.6 us
    all_gather x1, waiting for transfers between devices, fetch_weights(): lax.all_gather(gate_weight, 'dp', axis=0, tiled=True)  93.4 us
    all_gather x1, waiting for transfers between devices, fetch_weights(): lax.all_gather(up_weight, 'dp', axis=0, tiled=True)  89 us
    add x1, other arithmetic, local(): local_mlp = local_mlp + mlp_term(0, full_width)  73.7 us
    all_gather x2, waiting for transfers between devices, local(): lax.all_gather(key_rows, 'dp', axis=0, tiled=True)  71.9 us
  transfers between devices with their start and end apart: 25, of which 20 were waited for; matrix products, arithmetic and copies ran while one was open for 18% of the time, Pallas kernels for 0%

commit v1 on v0

v1 whole, which is shorter than its diff:
```python
import functools

import jax
import jax.numpy as jnp
from jax import lax
from jax.experimental import pallas as pl
from jax.experimental.pallas import tpu as pltpu
from jax.sharding import PartitionSpec as P

HEAD_SIZE = 128
ROWS_DEV = 64

EPSILON = 1e-06
ROPE_BASE = 1000000.0
MASKED = -1e30

CORE = 1
SPLIT = 8

BF = jnp.bfloat16
F32 = jnp.float32


def norm_rows(value_rows, gain_vec):
    return (
        value_rows
        * lax.rsqrt(jnp.mean(value_rows * value_rows, axis=-1, keepdims=True) + EPSILON)
        * gain_vec
    )


def rotate(value_rows, cosine_table, sine_table):
    half_width = value_rows.shape[-1] // 2
    turned = jnp.concatenate([-value_rows[..., half_width:], value_rows[..., :half_width]], axis=-1)
    return value_rows * cosine_table + turned * sine_table


def tables(positions, head_width):
    half_width = head_width // 2
    inverse = ROPE_BASE ** (-(jnp.arange(half_width, dtype=F32) * 2.0 / head_width))
    angles = positions.astype(F32)[:, None] * inverse[None, :]
    angles = jnp.concatenate([angles, angles], axis=-1)
    return (jnp.cos(angles), jnp.sin(angles))


def dot(left, right):
    return jnp.dot(left, right, preferred_element_type=F32)


def dot_nt(left, right):
    return lax.dot_general(left, right, (((1,), (1,)), ((), ())), preferred_element_type=F32)


def dot_tn(left, right):
    return lax.dot_general(left, right, (((0,), (0,)), ((), ())), preferred_element_type=F32)


def stack_heads(ref, segment):
    value = ref[:, segment]
    rows = value.shape[0] * value.shape[1]
    return jnp.concatenate(
        [
            value[:, :, h : h + HEAD_SIZE].reshape(rows, HEAD_SIZE)
            for h in range(0, value.shape[2], HEAD_SIZE)
        ],
        axis=0,
    )


def unstack_heads(ref, segment, value):
    rows = ref.shape[0] * ref.shape[2]
    for h in range(ref.shape[3] // HEAD_SIZE):
        block = value[h * rows : (h + 1) * rows]
        ref[:, segment, :, h * HEAD_SIZE : (h + 1) * HEAD_SIZE] = block.reshape(
            ref.shape[0], ref.shape[2], HEAD_SIZE
        )


def attend_kernel(scale, q_ref, kv_ref, qpos_ref, kpos_ref, out_ref, lse_ref):
    groups, _, segments, half, wide = kv_ref.shape
    rows = 2 * half
    for segment in range(segments):
        q = stack_heads(q_ref, segment)
        qpos = qpos_ref[segment]
        qpos = jnp.concatenate([qpos] * (q.shape[0] // rows), axis=0)

        def step(index, carry, q=q, qpos=qpos):
            high, total, acc = carry
            part = lax.div(index, groups)
            block = kv_ref[lax.rem(index, groups), :, part].reshape(rows, wide)
            scores = dot_nt(q, block[:, :HEAD_SIZE]) * scale
            scores = jnp.where(kpos_ref[index] <= qpos, scores, MASKED)
            top = jnp.maximum(high, jnp.max(scores, axis=-1, keepdims=True))
            shrink = jnp.exp(high - top)
            probs = jnp.exp(scores - top)
            total = total * shrink + jnp.sum(probs, axis=-1, keepdims=True)
            acc = acc * shrink + dot(probs.astype(BF), block[:, HEAD_SIZE:])
            return top, total, acc

        high, total, acc = lax.fori_loop(
            0,
            (segment + 1) * groups,
            step,
            (
                jnp.full((q.shape[0], 1), MASKED, F32),
                jnp.zeros((q.shape[0], 1), F32),
                jnp.zeros((q.shape[0], HEAD_SIZE), F32),
            ),
        )
        unstack_heads(out_ref, segment, acc / total)
        lse_ref[segment] = high + jnp.log(total)


def attend_back_kernel(
    scale, q_ref, kv_ref, qpos_ref, kpos_ref, out_ref, lse_ref, grad_ref, dq_ref, dkv_ref
):
    groups, _, segments, half, wide = kv_ref.shape
    rows = 2 * half
    dkv_ref[...] = jnp.zeros_like(dkv_ref)
    for segment in range(segments):
        q = stack_heads(q_ref, segment)
        grad = stack_heads(grad_ref, segment)
        out = stack_heads(out_ref, segment)
        delta = jnp.sum(out * grad.astype(F32), axis=-1, keepdims=True)
        lse = lse_ref[segment]
        qpos = qpos_ref[segment]
        qpos = jnp.concatenate([qpos] * (q.shape[0] // rows), axis=0)

        def step(index, dq, q=q, grad=grad, delta=delta, lse=lse, qpos=qpos):
            part = lax.div(index, groups)
            group = lax.rem(index, groups)
            block = kv_ref[group, :, part].reshape(rows, wide)
            keys = block[:, :HEAD_SIZE]
            scores = dot_nt(q, keys) * scale
            scores = jnp.where(kpos_ref[index] <= qpos, scores, MASKED)
            probs = jnp.exp(scores - lse)
            d_probs = dot_nt(grad, block[:, HEAD_SIZE:])
            d_scores = (probs * (d_probs - delta)).astype(BF)
            d_keys = dot_tn(d_scores, q) * scale
            d_values = dot_tn(probs.astype(BF), grad)
            both = jnp.concatenate([d_keys, d_values], axis=1).reshape(2, half, wide)
            dkv_ref[group, :, part] = dkv_ref[group, :, part] + both
            return dq + dot(d_scores, keys)

        dq = lax.fori_loop(
            0, (segment + 1) * groups, step, jnp.zeros((q.shape[0], HEAD_SIZE), F32)
        )
        unstack_heads(dq_ref, segment, dq * scale)


def attend(q, kv, qpos, kpos):
    half, wide = q.shape[2], q.shape[3]
    scores = 4 * half * 3 * kv.shape[0] * 2 * half
    return pl.pallas_call(
        functools.partial(attend_kernel, HEAD_SIZE**-0.5),
        out_shape=[
            jax.ShapeDtypeStruct(q.shape, F32),
            jax.ShapeDtypeStruct((q.shape[1], 2 * half * (wide // HEAD_SIZE), 1), F32),
        ],
        compiler_params=pltpu.CompilerParams(vmem_limit_bytes=40 << 20),
        cost_estimate=pl.CostEstimate(
            flops=4 * HEAD_SIZE * scores, bytes_accessed=4 << 20, transcendentals=scores
        ),
        name="attend",
    )(q, kv, qpos, kpos)


def attend_back(q, kv, qpos, kpos, out, lse, grad):
    half = q.shape[2]
    scores = 4 * half * 3 * kv.shape[0] * 2 * half
    return pl.pallas_call(
        functools.partial(attend_back_kernel, HEAD_SIZE**-0.5),
        out_shape=[
            jax.ShapeDtypeStruct(q.shape, F32),
            jax.ShapeDtypeStruct(kv.shape, F32),
        ],
        compiler_params=pltpu.CompilerParams(vmem_limit_bytes=48 << 20),
        cost_estimate=pl.CostEstimate(
            flops=10 * HEAD_SIZE * scores, bytes_accessed=6 << 20, transcendentals=scores
        ),
        name="attend_back",
    )(q, kv, qpos, kpos, out, lse, grad)


def local(
    layer_input,
    query_weight,
    key_matrix,
    value_matrix,
    output_weight,
    gate_weight,
    up_weight,
    down_weight,
    attn_gain,
    mlp_gain,
    query_gain,
    key_gain,
    cotangent,
):
    ways = lax.axis_size("dp")
    place = lax.axis_index("dp")
    side = lax.axis_index("tp")
    segments, _, rows, width = layer_input.shape
    piece = width // ways
    row_bits = [1 << k for k in range(ways.bit_length() - 1) if (1 << k) not in (CORE, SPLIT)]
    mixes = [0]
    for bit in row_bits:
        mixes = mixes + [mix | bit for mix in mixes]
    groups = len(mixes)
    chunk = 4 * piece
    quad = [
        [base, base | CORE, base | SPLIT, base | CORE | SPLIT] for base in mixes
    ]

    def swap(value, bit):
        return lax.ppermute(value, "dp", [(i, i ^ bit) for i in range(ways)])

    def swap_tp(value):
        return lax.ppermute(value, "tp", [(0, 1), (1, 0)])

    def bit_set(bit):
        return (place & bit) != 0

    def turn(blocks):
        for bit in row_bits:
            flag = bit_set(bit)
            blocks = [jnp.where(flag, blocks[k ^ bit], blocks[k]) for k in range(ways)]
        return blocks

    def to_local(value):
        blocks = [value[..., k * piece : (k + 1) * piece] for k in range(ways)]
        blocks = turn(blocks)
        return jnp.concatenate([blocks[k] for four in quad for k in four], axis=-1)

    def from_local(value):
        order = [k for four in quad for k in four]
        where = {k: n for n, k in enumerate(order)}
        blocks = [
            value[..., where[k] * piece : (where[k] + 1) * piece] for k in range(ways)
        ]
        return jnp.concatenate(turn(blocks), axis=-1)

    quads = [[base | CORE * (n & 1) | SPLIT * (n >> 1) for n in range(4)] for base in mixes]

    def trade(value):
        return lax.all_to_all(value, "dp", 0, 0, axis_index_groups=quads, tiled=True)

    def spread(value, order):
        held = {0: value}
        for bit in order:
            for mix in list(held):
                held[mix ^ bit] = swap(held[mix], bit)
        return [held[mix] for mix in mixes]

    def reduce_groups(parts, order):
        held = dict(zip(mixes, parts))
        for bit in order:
            sent = {mix: swap(held[mix].astype(BF), bit) for mix in held if mix & bit}
            held = {
                mix: held[mix] + sent[mix ^ bit].astype(F32) for mix in held if not mix & bit
            }
        return held[0]

    near, far = row_bits, row_bits[::-1]

    def split_columns(weight):
        wide = weight.shape[1] // 4
        return weight.reshape(piece, 4, wide).transpose(1, 0, 2)

    def rows_of(weight):
        return weight.reshape(4, weight.shape[0] // 4, piece)

    def fetch_in(value, order):
        value = trade(value)
        value = value.reshape(chunk, value.shape[2])
        return spread(value, order)

    def fetch_out(value, order):
        value = trade(value)
        value = jnp.concatenate([value[n] for n in range(4)], axis=1)
        return spread(value, order)

    q_parts = fetch_in(split_columns(query_weight), near)
    kv_parts = fetch_in(
        jnp.concatenate([split_columns(key_matrix), split_columns(value_matrix)], axis=2), far
    )
    o_parts = fetch_out(rows_of(output_weight), far)
    gate_parts = fetch_in(split_columns(gate_weight), near)
    up_parts = fetch_in(split_columns(up_weight), far)
    down_parts = fetch_out(rows_of(down_weight), near)

    def gather_rows(value):
        halves = [[], []]
        for s in range(segments):
            held = [value[s]]
            held = held + [swap(v, SPLIT) for v in held]
            held = held + [swap_tp(v) for v in held]
            halves[0] += held
            halves[1] += [swap(v, CORE) for v in held]
        return jnp.concatenate(halves[0] + halves[1], axis=0)

    def scatter_rows(produce):
        mine = 4 * rows
        sent = produce(1).astype(BF)
        kept = produce(0)
        done = []
        for s in range(segments):
            part = slice(s * mine, (s + 1) * mine)
            low = (kept[part] + swap(sent[part], CORE).astype(F32)).astype(BF)
            low = low[: 2 * rows].astype(F32) + swap_tp(low[2 * rows :]).astype(F32)
            low = low.astype(BF)
            low = low[:rows].astype(F32) + swap(low[rows:], SPLIT).astype(F32)
            done.append(low)
        return jnp.stack(done)

    half = 4 * rows
    all_rows = 2 * segments * half
    side_by = segments * half

    index = jnp.arange(all_rows, dtype=jnp.int32)
    row_in = index % rows
    split_by = (index // rows) % 2
    tp_by = (index // (2 * rows)) % 2
    segment_by = (index // half) % segments
    core_by = index // side_by

    def positions(base):
        block = base ^ (split_by * SPLIT) ^ (core_by * CORE)
        return (segment_by * ways + block) * ROWS_DEV + (side ^ tp_by) * rows + row_in

    query_pos = positions(place)
    cosine_table, sine_table = tables(query_pos, HEAD_SIZE)

    def by_segment(pos):
        return pos.reshape(2, segments, half).transpose(1, 0, 2).reshape(segments, 2 * half)

    qpos = by_segment(query_pos)[:, :, None]
    kpos = jnp.stack([by_segment(positions(place ^ mix)) for mix in mixes], axis=1)
    kpos = kpos.reshape(segments * groups, 1, 2 * half)

    attn_gain_local = to_local(attn_gain[None])
    mlp_gain_local = to_local(mlp_gain[None])
    incoming = to_local(cotangent[:, 0])
    incoming_all = gather_rows(incoming)

    resident = to_local(layer_input[:, 0].astype(F32))
    normed = norm_rows(resident, attn_gain_local).astype(BF)
    normed_all = gather_rows(normed)

    q_full = jnp.concatenate(q_parts, axis=0)
    kv_full = jnp.concatenate(kv_parts, axis=0)
    o_full = jnp.concatenate(o_parts, axis=1)
    gate_full = jnp.concatenate(gate_parts, axis=0)
    up_full = jnp.concatenate(up_parts, axis=0)
    down_full = jnp.concatenate(down_parts, axis=1)

    heads_q = q_full.shape[1] // HEAD_SIZE
    q_raw = dot(normed_all, q_full)
    kv_raw = dot(normed_all, kv_full)
    key_raw = kv_raw[:, :HEAD_SIZE]
    value_rows = kv_raw[:, HEAD_SIZE:].astype(BF)
    q_raws = [q_raw[:, h * HEAD_SIZE : (h + 1) * HEAD_SIZE] for h in range(heads_q)]

    def prepare(raw_in, gain_in):
        return rotate(norm_rows(raw_in, gain_in), cosine_table, sine_table)

    query_rows = jnp.concatenate([prepare(v, query_gain).astype(BF) for v in q_raws], axis=1)
    key_rows = prepare(key_raw, key_gain).astype(BF)
    keys_all = spread(key_rows, near)
    values_all = spread(value_rows, far)
    kv_all = jnp.stack(
        [jnp.concatenate([k, v], axis=1) for k, v in zip(keys_all, values_all)]
    ).reshape(groups, 2, segments, half, 2 * HEAD_SIZE)
    q4 = query_rows.reshape(2, segments, half, heads_q * HEAD_SIZE)
    attended, lse = attend(q4, kv_all, qpos, kpos)
    heads = attended.astype(BF).reshape(all_rows, heads_q * HEAD_SIZE)

    def of_side(value, c):
        return value[c * side_by : (c + 1) * side_by]

    branch = scatter_rows(lambda c: dot(of_side(heads, c), o_full))
    middle = resident + branch
    normed2 = norm_rows(middle, mlp_gain_local).astype(BF)
    normed2_all = gather_rows(normed2)
    gate_pre = dot(normed2_all, gate_full)
    up_pre = dot(normed2_all, up_full)
    active = (jax.nn.silu(gate_pre) * up_pre).astype(BF)
    mlp_out = scatter_rows(lambda c: dot(of_side(active, c), down_full))
    layer_output = from_local((middle + mlp_out).astype(BF))[:, None]

    d_active = dot_nt(incoming_all, down_full)
    sigma = jax.nn.sigmoid(gate_pre)
    d_gate = (d_active * up_pre * sigma * (1.0 + gate_pre * (1.0 - sigma))).astype(BF)
    d_upper = (d_active * gate_pre * sigma).astype(BF)
    d_normed2 = scatter_rows(
        lambda c: dot_nt(of_side(d_gate, c), gate_full) + dot_nt(of_side(d_upper, c), up_full)
    )

    def part_of(value, j):
        return value[:, j * chunk : (j + 1) * chunk]

    def grad_in(rows_in, grad_rows, order):
        parts = [dot_tn(part_of(rows_in, j), grad_rows) for j in range(groups)]
        total = reduce_groups(parts, order).astype(BF)
        return trade(total.reshape(4, piece, total.shape[1])).astype(F32)

    def grad_out(rows_in, grad_rows, order):
        parts = [dot_tn(rows_in, part_of(grad_rows, j)) for j in range(groups)]
        total = reduce_groups(parts, order).astype(BF)
        total = jnp.stack([total[:, n * piece : (n + 1) * piece] for n in range(4)])
        return trade(total).astype(F32)

    def join_columns(value):
        return jnp.concatenate([value[n] for n in range(4)], axis=1)

    def join_rows(value):
        return value.reshape(4 * value.shape[1], piece)

    down_grad = join_rows(grad_out(active, incoming_all, far))
    gate_grad = join_columns(grad_in(normed2_all, d_gate, far))
    up_grad = join_columns(grad_in(normed2_all, d_upper, near))

    _, pull_mlp = jax.vjp(norm_rows, middle, mlp_gain_local)
    d_mid_norm, d_mlp_gain = pull_mlp(d_normed2)
    d_middle = incoming.astype(F32) + d_mid_norm
    d_branch_all = gather_rows(d_middle.astype(BF))
    d_heads = dot_nt(d_branch_all, o_full).astype(BF)
    output_grad = join_rows(grad_out(heads, d_branch_all, near))

    dq, dkv = attend_back(
        q4, kv_all, qpos, kpos, attended, lse, d_heads.reshape(q4.shape)
    )
    dkv = dkv.reshape(groups, all_rows, 2 * HEAD_SIZE)
    d_keys = reduce_groups([dkv[j, :, :HEAD_SIZE] for j in range(groups)], far)
    d_values = reduce_groups([dkv[j, :, HEAD_SIZE:] for j in range(groups)], near)
    dq = dq.reshape(all_rows, heads_q * HEAD_SIZE)

    d_q_raws = []
    d_query_gain = jnp.zeros_like(query_gain)
    for h in range(heads_q):
        _, pull_query = jax.vjp(prepare, q_raws[h], query_gain)
        d_raw, d_gain = pull_query(dq[:, h * HEAD_SIZE : (h + 1) * HEAD_SIZE])
        d_q_raws.append(d_raw.astype(BF))
        d_query_gain = d_query_gain + d_gain
    d_q_low = jnp.concatenate(d_q_raws, axis=1)
    _, pull_key = jax.vjp(prepare, key_raw, key_gain)
    d_k_raw, d_key_gain = pull_key(d_keys)
    d_kv_low = jnp.concatenate([d_k_raw.astype(BF), d_values.astype(BF)], axis=1)

    d_normed = scatter_rows(
        lambda c: dot_nt(of_side(d_q_low, c), q_full) + dot_nt(of_side(d_kv_low, c), kv_full)
    )
    query_grad = join_columns(grad_in(normed_all, d_q_low, far))
    kv_grad = grad_in(normed_all, d_kv_low, near)
    key_grad = join_columns(kv_grad[:, :, :HEAD_SIZE])
    value_grad = join_columns(kv_grad[:, :, HEAD_SIZE:])

    _, pull_attn = jax.vjp(norm_rows, resident, attn_gain_local)
    d_resident, d_attn_gain = pull_attn(d_normed)
    input_grad = from_local((d_middle + d_resident).astype(BF))[:, None]

    gains = jnp.concatenate(
        [
            from_local(d_attn_gain)[0],
            from_local(d_mlp_gain)[0],
            d_query_gain,
            d_key_gain,
        ]
    ).reshape(-1, 128)
    for bit in [CORE, SPLIT] + row_bits:
        gains = gains + swap(gains, bit)
    gains = (gains + swap_tp(gains)).reshape(-1)
    gain_attn = gains[:width]
    gain_mlp = gains[width : 2 * width]
    gain_query = gains[2 * width : 2 * width + HEAD_SIZE]
    gain_key = gains[2 * width + HEAD_SIZE :]
    return (
        layer_output,
        input_grad,
        query_grad,
        key_grad,
        value_grad,
        output_grad,
        gate_grad,
        up_grad,
        down_grad,
        gain_attn,
        gain_mlp,
        gain_query,
        gain_key,
    )


def solution(mesh):
    in_specs = (
        P(None, "dp", "tp", None),
        P("dp", "tp"),
        P("dp", "tp"),
        P("dp", "tp"),
        P("tp", "dp"),
        P("dp", "tp"),
        P("dp", "tp"),
        P("tp", "dp"),
        P(),
        P(),
        P(),
        P(),
        P(None, "dp", "tp", None),
    )
    out_specs = (
        P(None, "dp", "tp", None),
        P(None, "dp", "tp", None),
        P("dp", "tp"),
        P("dp", "tp"),
        P("dp", "tp"),
        P("tp", "dp"),
        P("dp", "tp"),
        P("dp", "tp"),
        P("tp", "dp"),
        P(),
        P(),
        P(),
        P(),
    )
    return jax.shard_map(local, mesh=mesh, in_specs=in_specs, out_specs=out_specs, check_vma=False)
```

time: 2150 us -> 708 us (0.33)
  waiting for transfers between devices: 1550 us -> 337 us
  matrix products: 281 us -> 73 us
  starting transfers between devices: 1.86 us -> 171 us
  other arithmetic: 138 us -> 35.6 us
  blocking collectives: 89.5 us -> 0 us
    reduce_scatter x14 -> x0, waiting for transfers between devices: 982 us -> none  [the longest x1 702 us: local(): lax.psum_scatter(local_mlp, 'dp', scatter_dimension=0, tiled=True)]
    all_gather x11 -> x0, waiting for transfers between devices: 559 us -> none  [the longest x1 96.6 us: fetch_weights(): lax.all_gather(down_weight, 'dp', axis=1, tiled=True)]
    ppermute x0 -> x133, waiting for transfers between devices: none -> 267 us  [the longest x108 195 us: swap(): return lax.ppermute(value, 'dp', [(i, i ^ bit) for i in range(ways)])]
    dot_general x64 -> x42, matrix products: 281 us -> 73 us  [the longest x24 31.1 us: dot_tn(): lax.dot_general(left, right, (((0,), (0,)), ((), ())), preferred_element_...]
    ppermute x0 -> x133, starting transfers between devices: none -> 121 us  [the longest x108 94.8 us: swap(): return lax.ppermute(value, 'dp', [(i, i ^ bit) for i in range(ways)])]
    add x36 -> x9, other arithmetic: 99.8 us -> 1.73 us  [the longest x3 1.18 us: positions(): (segment_by * ways + block) * ROWS_DEV + (side ^ tp_by) * rows + row_in]
    all_to_all x0 -> x12, waiting for transfers between devices: none -> 70.6 us  [trade(): lax.all_to_all(value, 'dp', 0, 0, axis_index_groups=quads, tiled=True)]
    all_to_all x0 -> x12, starting transfers between devices: none -> 50.1 us  [trade(): lax.all_to_all(value, 'dp', 0, 0, axis_index_groups=quads, tiled=True)]
  transfers between devices with their start and end apart: 25 -> 145, of which waited for: 20 -> 73; matrix products, arithmetic and copies ran while one was open for 18% -> 20% of each run, Pallas kernels for 0% -> 3%
where the time goes in v1:
time: 708 us; the launch traced here: 701 us
  waiting for transfers between devices  337 us (48%)
  starting transfers between devices  171 us (24%)
  matrix products  73 us (10%)
  local copies, waits for them, and re-layouts  62.6 us (9%)
  other arithmetic  35.6 us (5%)
  Pallas kernels  17.8 us (3%)
    ppermute x108, waiting for transfers between devices, swap(): return lax.ppermute(value, 'dp', [(i, i ^ bit) for i in range(ways)])  195 us
    ppermute x108, starting transfers between devices, swap(): return lax.ppermute(value, 'dp', [(i, i ^ bit) for i in range(ways)])  94.8 us
    ppermute x25, waiting for transfers between devices, swap_tp(): return lax.ppermute(value, 'tp', [(0, 1), (1, 0)])  72 us
    all_to_all x12, waiting for transfers between devices, trade(): lax.all_to_all(value, 'dp', 0, 0, axis_index_groups=quads, tiled=True)  70.6 us
    all_to_all x12, starting transfers between devices, trade(): lax.all_to_all(value, 'dp', 0, 0, axis_index_groups=quads, tiled=True)  50.1 us
    unnamed x293, local copies, waits for them, and re-layouts  42.4 us
    dot_general x24, matrix products, dot_tn(): lax.dot_general(left, right, (((0,), (0,)), ((), ())), preferred_element_...  31.1 us
    ppermute x25, starting transfers between devices, swap_tp(): return lax.ppermute(value, 'tp', [(0, 1), (1, 0)])  25.8 us
  transfers between devices with their start and end apart: 145, of which 73 were waited for; matrix products, arithmetic and copies ran while one was open for 20% of the time, Pallas kernels for 3%

profile of v1, /device:TPU:0, one launch (start us, length us, event | category | flops | bytes accessed | tf_op | source)
XLA Modules:
  0.0 700.9 jit_solution(9498344580038722511)
XLA Ops:
  3.5 4.0 collective-permute-start
  10.6 4.3 all-to-all-start.1
  28.4 6.2 collective-permute-done.64
  54.6 3.8 collective-permute-done.5
  65.9 3.9 collective-permute-done.69
  80.7 4.2 all-to-all-start.2
  86.2 5.6 all-to-all-done.2
  102.3 4.4 all-to-all-start.3
  111.5 8.7 %collective-permute-done.14 = bf16[512,256]{1,0:T(8,128)(2,1)S(1)} collective-permute-done((bf16[512,256]{1,0:T(8,128)(2,1)S(1)}, bf16[512,256]{1,0:T(8,128)(2,1)S(1)}, u32[]{:S(2)}, u32[]{:S(2)}) %collective-permute-start.14) | collective-permute-done | bytes 262176 | tf_op jit(solution)/shard_map/ppermute | solution.py:216
  154.0 8.0 %attend.1 = (f32[2,2,128,256]{3,2,1,0:T(8,128)S(1)}, f32[2,512,1]{2,1,0:T(8,128)S(1)}) custom-call(bf16[2,2,128,256]{3,2,1,0:T(8,128)(2,1)S(1)} %bitcast.287, bf16[4,2,2,128,256]{4,3,2,1,0:T(8,128)(2,1)S(1)} %pad_maximum_fusion.6.kv_ref, s32[2,256,1]{2,1,0:T(8,128)S(1)} %fusion.62.qpos_ref, s32[8,1,256]{2,1,0:T(1,128)S(1)} %reshape.983.kpos_ref), custom_call_target="tpu_custom_call" | custom-call | flops 805306368 | bytes 4194304 | tf_op jit(solution)/shard_map/attend/pallas_call | solution.py:154
  163.7 8.1 %all-to-all-start.5 = ((bf16[4,768,128]{2,1,0:T(8,128)(2,1)}), bf16[4,768,128]{2,1,0:T(8,128)(2,1)S(1)}, u32[]{:S(2)}, u32[]{:S(2)}) async-start(bf16[4,768,128]{2,1,0:T(8,128)(2,1)} %bitcast.320), calls=%async_computation.5 | async-start | bytes 1572864 | tf_op jit(solution)/shard_map/all_to_all | solution.py:246
  183.6 9.2 %all-to-all-done.5 = bf16[4,768,128]{2,1,0:T(8,128)(2,1)S(1)} async-done(((bf16[4,768,128]{2,1,0:T(8,128)(2,1)}), bf16[4,768,128]{2,1,0:T(8,128)(2,1)S(1)}, u32[]{:S(2)}, u32[]{:S(2)}) %all-to-all-start.5) | async-done | bytes 786464 | tf_op jit(solution)/shard_map/all_to_all | solution.py:246
  192.8 4.2 all-to-all-start.4
  206.3 11.9 %all-to-all-done.4 = bf16[4,128,768]{1,2,0:T(8,128)(2,1)} async-done(((bf16[4,128,768]{1,2,0:T(8,128)(2,1)}), bf16[4,128,768]{1,2,0:T(8,128)(2,1)}, u32[]{:S(2)}, u32[]{:S(2)}) %all-to-all-start.4) | async-done | bytes 786464 | tf_op jit(solution)/shard_map/all_to_all | solution.py:246
  224.3 5.8 collective-permute-done.30
  240.0 11.1 %collective-permute-done.34 = bf16[32,2048]{1,0:T(8,128)(2,1)S(1)} collective-permute-done((bf16[32,2048]{1,0:T(8,128)(2,1)S(1)}, bf16[32,2048]{1,0:T(8,128)(2,1)S(1)}, u32[]{:S(2)}, u32[]{:S(2)}) %collective-permute-start.34) | collective-permute-done | bytes 131104 | tf_op jit(solution)/shard_map/ppermute | solution.py:216
  257.7 13.9 %collective-permute-done.35 = bf16[32,2048]{1,0:T(8,128)(2,1)S(1)} collective-permute-done((bf16[32,2048]{1,0:T(8,128)(2,1)S(1)}, bf16[32,2048]{1,0:T(8,128)(2,1)S(1)}, u32[]{:S(2)}, u32[]{:S(2)}) %collective-permute-start.35) | collective-permute-done | bytes 131104 | tf_op jit(solution)/shard_map/ppermute | solution.py:216
  272.5 4.1 collective-permute-done.36
  277.6 4.0 collective-permute-done.37
  281.6 4.1 collective-permute-start.38
  285.7 4.3 collective-permute-done.38
  291.0 4.0 collective-permute-done.39
  295.9 4.0 collective-permute-done.40
  312.2 4.5 fusion.173
  316.8 13.6 %collective-permute-done.54 = bf16[512,768]{1,0:T(8,128)(2,1)S(1)} collective-permute-done((bf16[512,768]{1,0:T(8,128)(2,1)S(1)}, bf16[512,768]{1,0:T(8,128)(2,1)S(1)}, u32[]{:S(2)}, u32[]{:S(2)}) %collective-permute-start.54) | collective-permute-done | bytes 786464 | tf_op jit(solution)/shard_map/ppermute | solution.py:216
  333.1 4.4 multiply_convert_fusion.1
  357.2 5.3 convolution_add_fusion.1
  367.8 5.8 collective-permute-done.82
  374.7 5.4 collective-permute-done.79
  381.1 5.3 collective-permute-done.62
  395.8 19.3 %collective-permute-done.126 = bf16[768,512]{1,0:T(8,128)(2,1)S(1)} collective-permute-done((bf16[768,512]{1,0:T(8,128)(2,1)S(1)}, bf16[768,512]{1,0:T(8,128)(2,1)S(1)}, u32[]{:S(2)}, u32[]{:S(2)}) %collective-permute-start.126) | collective-permute-done | bytes 786464 | tf_op jit(solution)/shard_map/ppermute | solution.py:216
  416.6 10.8 %collective-permute-done.83 = bf16[32,2048]{1,0:T(8,128)(2,1)S(1)} collective-permute-done((bf16[32,2048]{1,0:T(8,128)(2,1)S(1)}, bf16[32,2048]{1,0:T(8,128)(2,1)S(1)}, u32[]{:S(2)}, u32[]{:S(2)}) %collective-permute-start.83) | collective-permute-done | bytes 131104 | tf_op jit(solution)/shard_map/ppermute | solution.py:216
  437.3 6.0 collective-permute-done.60
  449.6 4.0 collective-permute-done.86
  454.7 4.1 collective-permute-done.88
  459.7 4.0 collective-permute-done.89
  473.5 9.8 %attend_back.1 = (f32[2,2,128,256]{3,2,1,0:T(8,128)S(1)}, f32[4,2,2,128,256]{4,3,2,1,0:T(8,128)S(1)}) custom-call(bf16[2,2,128,256]{3,2,1,0:T(8,128)(2,1)S(1)} %bitcast.288, bf16[4,2,2,128,256]{4,3,2,1,0:T(8,128)(2,1)S(1)} %pad_maximum_fusion.6.kv_ref, s32[2,256,1]{2,1,0:T(8,128)S(1)} %fusion.62.qpos_ref, s32[8,1,256]{2,1,0:T(1,128)S(1)} %reshape.983.kpos_ref, ...), custom_call_target="tpu_custom_call" | custom-call | flops 2013265920 | bytes 6291456 | tf_op jit(solution)/shard_map/attend_back/pallas_call | solution.py:171
  503.7 28.3 %collective-permute-done.121 = bf16[512,768]{1,0:T(8,128)(2,1)S(1)} collective-permute-done((bf16[512,768]{1,0:T(8,128)(2,1)}, bf16[512,768]{1,0:T(8,128)(2,1)S(1)}, u32[]{:S(2)}, u32[]{:S(2)}) %collective-permute-start.121) | collective-permute-done | bytes 786464 | tf_op jit(solution)/shard_map/ppermute | solution.py:216
  561.9 7.0 %collective-permute-done.118 = bf16[256,512]{1,0:T(8,128)(2,1)S(1)} collective-permute-done((bf16[256,512]{1,0:T(8,128)(2,1)S(1)}, bf16[256,512]{1,0:T(8,128)(2,1)S(1)}, u32[]{:S(2)}, u32[]{:S(2)}) %collective-permute-start.118) | collective-permute-done | bytes 262176 | tf_op jit(solution)/shard_map/ppermute | solution.py:216
  571.6 3.7 all-to-all-start.8
  585.2 4.7 collective-permute-done.112
  593.1 4.0 all-to-all-start.6
  601.2 13.6 %collective-permute-done.109 = bf16[32,2048]{1,0:T(8,128)(2,1)S(1)} collective-permute-done((bf16[32,2048]{1,0:T(8,128)(2,1)S(1)}, bf16[32,2048]{1,0:T(8,128)(2,1)S(1)}, u32[]{:S(2)}, u32[]{:S(2)}) %collective-permute-start.109) | collective-permute-done | bytes 131104 | tf_op jit(solution)/shard_map/ppermute | solution.py:216
  623.0 7.9 %all-to-all-done.7 = bf16[4,128,256]{2,1,0:T(8,128)(2,1)S(1)} async-done(((bf16[4,128,256]{2,1,0:T(8,128)(2,1)}), bf16[4,128,256]{2,1,0:T(8,128)(2,1)S(1)}, u32[]{:S(2)}, u32[]{:S(2)}) %all-to-all-start.7) | async-done | bytes 262176 | tf_op jit(solution)/shard_map/all_to_all | solution.py:246
  638.6 15.4 %all-to-all-done.9 = bf16[4,128,768]{2,1,0:T(8,128)(2,1)S(1)} async-done(((bf16[4,128,768]{2,1,0:T(8,128)(2,1)}), bf16[4,128,768]{2,1,0:T(8,128)(2,1)S(1)}, u32[]{:S(2)}, u32[]{:S(2)}) %all-to-all-start.9) | async-done | bytes 786464 | tf_op jit(solution)/shard_map/all_to_all | solution.py:246
  662.1 5.3 collective-permute-done.131
  672.5 4.2 all-to-all-done.10
  683.3 16.1 %all-to-all-done.11 = bf16[4,768,128]{2,1,0:T(8,128)(2,1)S(1)} async-done(((bf16[4,768,128]{2,1,0:T(8,128)(2,1)}), bf16[4,768,128]{2,1,0:T(8,128)(2,1)S(1)}, u32[]{:S(2)}, u32[]{:S(2)}) %all-to-all-start.11) | async-done | bytes 786464 | tf_op jit(solution)/shard_map/all_to_all | solution.py:246
  (857 shorter events, 342.7 us)
Async XLA Ops:
  3.5 19.5 %collective-permute-start = (bf16[32,2048]{1,0:T(8,128)(2,1)}, bf16[32,2048]{1,0:T(8,128)(2,1)}, u32[]{:S(2)}, u32[]{:S(2)}) collective-permute-start(bf16[32,2048]{1,0:T(8,128)(2,1)} %get-tuple-element.189), channel_id=1, source_target_pairs={{0,8},{1,9},{2,10},{3,11},{4,12},{5,13},{6,14},{7,15},{8,0},{9,1},... | collective-permute-start | bytes 393224 | tf_op jit(solution)/shard_map/ppermute | solution.py:216
  9.0 42.2 %collective-permute-start.3 = (bf16[32,2048]{1,0:T(8,128)(2,1)}, bf16[32,2048]{1,0:T(8,128)(2,1)S(1)}, u32[]{:S(2)}, u32[]{:S(2)}) collective-permute-start(bf16[32,2048]{1,0:T(8,128)(2,1)} %get-tuple-element.188), channel_id=1, source_target_pairs={{0,8},{1,9},{2,10},{3,11},{4,12},{5,13},{6,14},{7,15},{8,0},{9,1},... | collective-permute-start | bytes 393224 | tf_op jit(solution)/shard_map/ppermute | solution.py:216
  9.4 44.0 %collective-permute-start.4 = (bf16[32,2048]{1,0:T(8,128)(2,1)}, bf16[32,2048]{1,0:T(8,128)(2,1)S(1)}, u32[]{:S(2)}, u32[]{:S(2)}) collective-permute-start(bf16[32,2048]{1,0:T(8,128)(2,1)} %get-tuple-element.188), channel_id=1, source_target_pairs={{0,16},{16,0},{1,17},{17,1},{2,18},{18,2},{3,19},{19,3},{4,20},{20... | collective-permute-start | bytes 393224 | tf_op jit(solution)/shard_map/ppermute | solution.py:219
  9.6 49.4 %collective-permute-start.6 = (bf16[32,2048]{1,0:T(8,128)(2,1)}, bf16[32,2048]{1,0:T(8,128)(2,1)}, u32[]{:S(2)}, u32[]{:S(2)}) collective-permute-start(bf16[32,2048]{1,0:T(8,128)(2,1)} %get-tuple-element.189), channel_id=1, source_target_pairs={{0,1},{1,0},{2,3},{3,2},{4,5},{5,4},{6,7},{7,6},{8,9},{9,8},{10,11... | collective-permute-start | bytes 393224 | tf_op jit(solution)/shard_map/ppermute | solution.py:216
  10.6 70.1 %all-to-all-start.1 = ((bf16[4,128,256]{1,2,0:T(8,128)(2,1)}), bf16[4,128,256]{1,2,0:T(8,128)(2,1)S(1)}, u32[]{:S(2)}, u32[]{:S(2)}) async-start(bf16[4,128,256]{1,2,0:T(8,128)(2,1)} %pad_maximum_fusion.16), calls=%async_computation.1 | async-start | bytes 524288 | tf_op jit(solution)/shard_map/all_to_all | solution.py:246
  23.0 52.7 %collective-permute-start.10 = (bf16[32,2048]{1,0:T(8,128)(2,1)}, bf16[32,2048]{1,0:T(8,128)(2,1)S(1)}, u32[]{:S(2)}, u32[]{:S(2)}) collective-permute-start(bf16[32,2048]{1,0:T(8,128)(2,1)} %get-tuple-element.188), channel_id=1, source_target_pairs={{0,1},{1,0},{2,3},{3,2},{4,5},{5,4},{6,7},{7,6},{8,9},{9,8},{10,11... | collective-permute-start | bytes 393224 | tf_op jit(solution)/shard_map/ppermute | solution.py:216
  99.7 26.3 %collective-permute-start.17 = (bf16[512,256]{1,0:T(8,128)(2,1)S(1)}, bf16[512,256]{1,0:T(8,128)(2,1)}, u32[]{:S(2)}, u32[]{:S(2)}) collective-permute-start(bf16[512,256]{1,0:T(8,128)(2,1)S(1)} %bitcast.337), channel_id=1, source_target_pairs={{0,2},{1,3},{2,0},{3,1},{4,6},{5,7},{6,4},{7,5},{8,10},{9,11},{10,... | collective-permute-start | bytes 786440 | tf_op jit(solution)/shard_map/ppermute | solution.py:216
  101.9 20.3 %collective-permute-start.27 = (bf16[256,512]{1,0:T(8,128)(2,1)S(1)}, bf16[256,512]{1,0:T(8,128)(2,1)}, u32[]{:S(2)}, u32[]{:S(2)}) collective-permute-start(bf16[256,512]{1,0:T(8,128)(2,1)S(1)} %pad_maximum_fusion.21), channel_id=1, source_target_pairs={{0,4},{1,5},{2,6},{3,7},{4,0},{5,1},{6,2},{7,3},{8,12},{9,13},{10,... | collective-permute-start | bytes 786440 | tf_op jit(solution)/shard_map/ppermute | solution.py:216
  102.3 61.4 %all-to-all-start.3 = ((bf16[4,128,768]{1,2,0:T(8,128)(2,1)}), bf16[4,128,768]{1,2,0:T(8,128)(2,1)}, u32[]{:S(2)}, u32[]{:S(2)}) async-start(bf16[4,128,768]{1,2,0:T(8,128)(2,1)} %bitcast.37), calls=%async_computation.3 | async-start | bytes 1572864 | tf_op jit(solution)/shard_map/all_to_all | solution.py:246
  122.2 20.5 %collective-permute-start.28 = (bf16[256,512]{1,0:T(8,128)(2,1)}, bf16[256,512]{1,0:T(8,128)(2,1)S(1)}, u32[]{:S(2)}, u32[]{:S(2)}) collective-permute-start(bf16[256,512]{1,0:T(8,128)(2,1)} %collective-permute-done.27), channel_id=1, source_target_pairs={{0,2},{1,3},{2,0},{3,1},{4,6},{5,7},{6,4},{7,5},{8,10},{9,11},{10,... | collective-permute-start | bytes 786440 | tf_op jit(solution)/shard_map/ppermute | solution.py:216
  163.7 29.2 %all-to-all-start.5 = ((bf16[4,768,128]{2,1,0:T(8,128)(2,1)}), bf16[4,768,128]{2,1,0:T(8,128)(2,1)S(1)}, u32[]{:S(2)}, u32[]{:S(2)}) async-start(bf16[4,768,128]{2,1,0:T(8,128)(2,1)} %bitcast.320), calls=%async_computation.5 | async-start | bytes 1572864 | tf_op jit(solution)/shard_map/all_to_all | solution.py:246
  174.5 26.5 %collective-permute-start.29 = (bf16[128,2048]{1,0:T(8,128)(2,1)}, bf16[128,2048]{1,0:T(8,128)(2,1)}, u32[]{:S(2)}, u32[]{:S(2)}) collective-permute-start(bf16[128,2048]{1,0:T(8,128)(2,1)} %get-tuple-element.130), channel_id=1, source_target_pairs={{0,1},{1,0},{2,3},{3,2},{4,5},{5,4},{6,7},{7,6},{8,9},{9,8},{10,11... | collective-permute-start | bytes 1572872 | tf_op jit(solution)/shard_map/ppermute | solution.py:216
  175.0 26.0 %collective-permute-start.32 = (bf16[128,2048]{1,0:T(8,128)(2,1)}, bf16[128,2048]{1,0:T(8,128)(2,1)}, u32[]{:S(2)}, u32[]{:S(2)}) collective-permute-start(bf16[128,2048]{1,0:T(8,128)(2,1)} %get-tuple-element.131), channel_id=1, source_target_pairs={{0,1},{1,0},{2,3},{3,2},{4,5},{5,4},{6,7},{7,6},{8,9},{9,8},{10,11... | collective-permute-start | bytes 1572872 | tf_op jit(solution)/shard_map/ppermute | solution.py:216
  180.4 56.7 %collective-permute-start.49 = (bf16[512,768]{1,0:T(8,128)(2,1)}, bf16[512,768]{1,0:T(8,128)(2,1)}, u32[]{:S(2)}, u32[]{:S(2)}) collective-permute-start(bf16[512,768]{1,0:T(8,128)(2,1)} %bitcast.322), channel_id=1, source_target_pairs={{0,2},{1,3},{2,0},{3,1},{4,6},{5,7},{6,4},{7,5},{8,10},{9,11},{10,... | collective-permute-start | bytes 2359304 | tf_op jit(solution)/shard_map/ppermute | solution.py:216
  181.9 130.3 %collective-permute-start.50 = (bf16[512,768]{1,0:T(8,128)(2,1)}, bf16[512,768]{1,0:T(8,128)(2,1)}, u32[]{:S(2)}, u32[]{:S(2)}) collective-permute-start(bf16[512,768]{1,0:T(8,128)(2,1)} %bitcast.323), channel_id=1, source_target_pairs={{0,4},{1,5},{2,6},{3,7},{4,0},{5,1},{6,2},{7,3},{8,12},{9,13},{10,... | collective-permute-start | bytes 2359304 | tf_op jit(solution)/shard_map/ppermute | solution.py:216
  192.8 25.4 %all-to-all-start.4 = ((bf16[4,128,768]{1,2,0:T(8,128)(2,1)}), bf16[4,128,768]{1,2,0:T(8,128)(2,1)}, u32[]{:S(2)}, u32[]{:S(2)}) async-start(bf16[4,128,768]{1,2,0:T(8,128)(2,1)} %bitcast.306), calls=%async_computation.4 | async-start | bytes 1572864 | tf_op jit(solution)/shard_map/all_to_all | solution.py:246
  198.1 33.0 %collective-permute-start.55 = (bf16[768,512]{1,0:T(8,128)(2,1)}, bf16[768,512]{1,0:T(8,128)(2,1)}, u32[]{:S(2)}, u32[]{:S(2)}) collective-permute-start(bf16[768,512]{1,0:T(8,128)(2,1)} %pad_maximum_fusion.7), channel_id=1, source_target_pairs={{0,2},{1,3},{2,0},{3,1},{4,6},{5,7},{6,4},{7,5},{8,10},{9,11},{10,... | collective-permute-start | bytes 2359304 | tf_op jit(solution)/shard_map/ppermute | solution.py:216
  201.0 34.0 %collective-permute-start.56 = (bf16[768,512]{1,0:T(8,128)(2,1)}, bf16[768,512]{1,0:T(8,128)(2,1)}, u32[]{:S(2)}, u32[]{:S(2)}) collective-permute-start(bf16[768,512]{1,0:T(8,128)(2,1)} %pad_maximum_fusion.7), channel_id=1, source_target_pairs={{0,4},{1,5},{2,6},{3,7},{4,0},{5,1},{6,2},{7,3},{8,12},{9,13},{10,... | collective-permute-start | bytes 2359304 | tf_op jit(solution)/shard_map/ppermute | solution.py:216
  230.0 79.5 %collective-permute-start.53 = (bf16[512,768]{1,0:T(8,128)(2,1)}, bf16[512,768]{1,0:T(8,128)(2,1)S(1)}, u32[]{:S(2)}, u32[]{:S(2)}) collective-permute-start(bf16[512,768]{1,0:T(8,128)(2,1)} %bitcast.327), channel_id=1, source_target_pairs={{0,4},{1,5},{2,6},{3,7},{4,0},{5,1},{6,2},{7,3},{8,12},{9,13},{10,... | collective-permute-start | bytes 2359304 | tf_op jit(solution)/shard_map/ppermute | solution.py:216
  231.1 85.6 %collective-permute-start.52 = (bf16[512,768]{1,0:T(8,128)(2,1)S(1)}, bf16[512,768]{1,0:T(8,128)(2,1)S(1)}, u32[]{:S(2)}, u32[]{:S(2)}) collective-permute-start(bf16[512,768]{1,0:T(8,128)(2,1)S(1)} %bitcast.328), channel_id=1, source_target_pairs={{0,2},{1,3},{2,0},{3,1},{4,6},{5,7},{6,4},{7,5},{8,10},{9,11},{10,... | collective-permute-start | bytes 2359304 | tf_op jit(solution)/shard_map/ppermute | solution.py:216
  251.1 61.2 %collective-permute-start.51 = (bf16[512,768]{1,0:T(8,128)(2,1)}, bf16[512,768]{1,0:T(8,128)(2,1)S(1)}, u32[]{:S(2)}, u32[]{:S(2)}) collective-permute-start(bf16[512,768]{1,0:T(8,128)(2,1)} %collective-permute-done.49), channel_id=1, source_target_pairs={{0,4},{1,5},{2,6},{3,7},{4,0},{5,1},{6,2},{7,3},{8,12},{9,13},{10,... | collective-permute-start | bytes 2359304 | tf_op jit(solution)/shard_map/ppermute | solution.py:216
  309.5 22.6 %collective-permute-start.57 = (bf16[768,512]{1,0:T(8,128)(2,1)}, bf16[768,512]{1,0:T(8,128)(2,1)S(1)}, u32[]{:S(2)}, u32[]{:S(2)}) collective-permute-start(bf16[768,512]{1,0:T(8,128)(2,1)} %collective-permute-done.55), channel_id=1, source_target_pairs={{0,4},{1,5},{2,6},{3,7},{4,0},{5,1},{6,2},{7,3},{8,12},{9,13},{10,... | collective-permute-start | bytes 2359304 | tf_op jit(solution)/shard_map/ppermute | solution.py:216
  310.7 19.6 %collective-permute-start.54 = (bf16[512,768]{1,0:T(8,128)(2,1)S(1)}, bf16[512,768]{1,0:T(8,128)(2,1)S(1)}, u32[]{:S(2)}, u32[]{:S(2)}) collective-permute-start(bf16[512,768]{1,0:T(8,128)(2,1)S(1)} %collective-permute-done.53), channel_id=1, source_target_pairs={{0,2},{1,3},{2,0},{3,1},{4,6},{5,7},{6,4},{7,5},{8,10},{9,11},{10,... | collective-permute-start | bytes 2359304 | tf_op jit(solution)/shard_map/ppermute | solution.py:216
  355.3 32.4 %collective-permute-start.120 = (bf16[512,768]{1,0:T(8,128)(2,1)S(1)}, bf16[512,768]{1,0:T(8,128)(2,1)S(1)}, u32[]{:S(2)}, u32[]{:S(2)}) collective-permute-start(bf16[512,768]{1,0:T(8,128)(2,1)S(1)} %convolution_convert_fusion.6), channel_id=1, source_target_pairs={{0,4},{1,5},{2,6},{3,7},{4,0},{5,1},{6,2},{7,3},{8,12},{9,13},{10,... | collective-permute-start | bytes 2359304 | tf_op jit(solution)/shard_map/ppermute | solution.py:216
  362.5 139.4 %collective-permute-start.119 = (bf16[512,768]{1,0:T(8,128)(2,1)}, bf16[512,768]{1,0:T(8,128)(2,1)}, u32[]{:S(2)}, u32[]{:S(2)}) collective-permute-start(bf16[512,768]{1,0:T(8,128)(2,1)} %convolution_convert_fusion.7), channel_id=1, source_target_pairs={{0,4},{1,5},{2,6},{3,7},{4,0},{5,1},{6,2},{7,3},{8,12},{9,13},{10,... | collective-permute-start | bytes 2359304 | tf_op jit(solution)/shard_map/ppermute | solution.py:216
  363.7 26.6 %collective-permute-start.123 = (bf16[512,768]{1,0:T(8,128)(2,1)S(1)}, bf16[512,768]{1,0:T(8,128)(2,1)S(1)}, u32[]{:S(2)}, u32[]{:S(2)}) collective-permute-start(bf16[512,768]{1,0:T(8,128)(2,1)S(1)} %convolution_convert_fusion.4), channel_id=1, source_target_pairs={{0,2},{1,3},{2,0},{3,1},{4,6},{5,7},{6,4},{7,5},{8,10},{9,11},{10,... | collective-permute-start | bytes 2359304 | tf_op jit(solution)/shard_map/ppermute | solution.py:216
  365.6 49.5 %collective-permute-start.126 = (bf16[768,512]{1,0:T(8,128)(2,1)S(1)}, bf16[768,512]{1,0:T(8,128)(2,1)S(1)}, u32[]{:S(2)}, u32[]{:S(2)}) collective-permute-start(bf16[768,512]{1,0:T(8,128)(2,1)S(1)} %convolution_convert_fusion.2), channel_id=1, source_target_pairs={{0,4},{1,5},{2,6},{3,7},{4,0},{5,1},{6,2},{7,3},{8,12},{9,13},{10,... | collective-permute-start | bytes 2359304 | tf_op jit(solution)/shard_map/ppermute | solution.py:216
  386.5 111.2 %collective-permute-start.125 = (bf16[768,512]{1,0:T(8,128)(2,1)}, bf16[768,512]{1,0:T(8,128)(2,1)}, u32[]{:S(2)}, u32[]{:S(2)}) collective-permute-start(bf16[768,512]{1,0:T(8,128)(2,1)} %convolution_convert_fusion.3), channel_id=1, source_target_pairs={{0,4},{1,5},{2,6},{3,7},{4,0},{5,1},{6,2},{7,3},{8,12},{9,13},{10,... | collective-permute-start | bytes 2359304 | tf_op jit(solution)/shard_map/ppermute | solution.py:216
  390.3 37.1 %collective-permute-start.83 = (bf16[32,2048]{1,0:T(8,128)(2,1)S(1)}, bf16[32,2048]{1,0:T(8,128)(2,1)S(1)}, u32[]{:S(2)}, u32[]{:S(2)}) collective-permute-start(bf16[32,2048]{1,0:T(8,128)(2,1)S(1)} %slice.1282), channel_id=1, source_target_pairs={{0,8},{1,9},{2,10},{3,11},{4,12},{5,13},{6,14},{7,15},{8,0},{9,1},... | collective-permute-start | bytes 393224 | tf_op jit(solution)/shard_map/ppermute | solution.py:216
  394.2 36.7 %collective-permute-start.80 = (bf16[32,2048]{1,0:T(8,128)(2,1)S(1)}, bf16[32,2048]{1,0:T(8,128)(2,1)S(1)}, u32[]{:S(2)}, u32[]{:S(2)}) collective-permute-start(bf16[32,2048]{1,0:T(8,128)(2,1)S(1)} %slice.1276), channel_id=1, source_target_pairs={{0,8},{1,9},{2,10},{3,11},{4,12},{5,13},{6,14},{7,15},{8,0},{9,1},... | collective-permute-start | bytes 393224 | tf_op jit(solution)/shard_map/ppermute | solution.py:216
  430.9 67.8 %collective-permute-start.127 = (bf16[768,512]{1,0:T(8,128)(2,1)}, bf16[768,512]{1,0:T(8,128)(2,1)}, u32[]{:S(2)}, u32[]{:S(2)}) collective-permute-start(bf16[768,512]{1,0:T(8,128)(2,1)} %add_convert_fusion.1), channel_id=1, source_target_pairs={{0,2},{1,3},{2,0},{3,1},{4,6},{5,7},{6,4},{7,5},{8,10},{9,11},{10,... | collective-permute-start | bytes 2359304 | tf_op jit(solution)/shard_map/ppermute | solution.py:216
  494.6 41.5 %collective-permute-start.122 = (bf16[512,768]{1,0:T(8,128)(2,1)S(1)}, bf16[512,768]{1,0:T(8,128)(2,1)S(1)}, u32[]{:S(2)}, u32[]{:S(2)}) collective-permute-start(bf16[512,768]{1,0:T(8,128)(2,1)S(1)} %copy-done.99), channel_id=1, source_target_pairs={{0,2},{1,3},{2,0},{3,1},{4,6},{5,7},{6,4},{7,5},{8,10},{9,11},{10,... | collective-permute-start | bytes 2359304 | tf_op jit(solution)/shard_map/ppermute | solution.py:216
  496.1 35.8 %collective-permute-start.121 = (bf16[512,768]{1,0:T(8,128)(2,1)}, bf16[512,768]{1,0:T(8,128)(2,1)S(1)}, u32[]{:S(2)}, u32[]{:S(2)}) collective-permute-start(bf16[512,768]{1,0:T(8,128)(2,1)} %add_convert_fusion.5), channel_id=1, source_target_pairs={{0,2},{1,3},{2,0},{3,1},{4,6},{5,7},{6,4},{7,5},{8,10},{9,11},{10,... | collective-permute-start | bytes 2359304 | tf_op jit(solution)/shard_map/ppermute | solution.py:216
  497.7 38.4 %collective-permute-start.124 = (bf16[512,768]{1,0:T(8,128)(2,1)S(1)}, bf16[512,768]{1,0:T(8,128)(2,1)S(1)}, u32[]{:S(2)}, u32[]{:S(2)}) collective-permute-start(bf16[512,768]{1,0:T(8,128)(2,1)S(1)} %copy-done.100), channel_id=1, source_target_pairs={{0,4},{1,5},{2,6},{3,7},{4,0},{5,1},{6,2},{7,3},{8,12},{9,13},{10,... | collective-permute-start | bytes 2359304 | tf_op jit(solution)/shard_map/ppermute | solution.py:216
  498.6 41.4 %collective-permute-start.101 = (bf16[512,128]{0,1:T(8,128)(2,1)}, bf16[512,128]{0,1:T(8,128)(2,1)S(1)}, u32[]{:S(2)}, u32[]{:S(2)}) collective-permute-start(bf16[512,128]{0,1:T(8,128)(2,1)} %get-tuple-element.122), channel_id=1, source_target_pairs={{0,2},{1,3},{2,0},{3,1},{4,6},{5,7},{6,4},{7,5},{8,10},{9,11},{10,... | collective-permute-start | bytes 393224 | tf_op jit(solution)/shard_map/ppermute | solution.py:216
  501.9 38.9 %collective-permute-start.98 = (bf16[512,128]{0,1:T(8,128)(2,1)S(1)}, bf16[512,128]{0,1:T(8,128)(2,1)S(1)}, u32[]{:S(2)}, u32[]{:S(2)}) collective-permute-start(bf16[512,128]{0,1:T(8,128)(2,1)S(1)} %get-tuple-element.125), channel_id=1, source_target_pairs={{0,4},{1,5},{2,6},{3,7},{4,0},{5,1},{6,2},{7,3},{8,12},{9,13},{10,... | collective-permute-start | bytes 393224 | tf_op jit(solution)/shard_map/ppermute | solution.py:216
  531.9 24.0 %collective-permute-start.117 = (bf16[256,512]{1,0:T(8,128)(2,1)S(1)}, bf16[256,512]{1,0:T(8,128)(2,1)S(1)}, u32[]{:S(2)}, u32[]{:S(2)}) collective-permute-start(bf16[256,512]{1,0:T(8,128)(2,1)S(1)} %convolution_convert_fusion.8), channel_id=1, source_target_pairs={{0,2},{1,3},{2,0},{3,1},{4,6},{5,7},{6,4},{7,5},{8,10},{9,11},{10,... | collective-permute-start | bytes 786440 | tf_op jit(solution)/shard_map/ppermute | solution.py:216
  540.1 21.0 %collective-permute-start.116 = (bf16[256,512]{1,0:T(8,128)(2,1)S(1)}, bf16[256,512]{1,0:T(8,128)(2,1)S(1)}, u32[]{:S(2)}, u32[]{:S(2)}) collective-permute-start(bf16[256,512]{1,0:T(8,128)(2,1)S(1)} %convolution_convert_fusion.9), channel_id=1, source_target_pairs={{0,2},{1,3},{2,0},{3,1},{4,6},{5,7},{6,4},{7,5},{8,10},{9,11},{10,... | collective-permute-start | bytes 786440 | tf_op jit(solution)/shard_map/ppermute | solution.py:216
  553.5 27.0 %collective-permute-start.104 = (bf16[128,2048]{1,0:T(8,128)(2,1)}, bf16[128,2048]{1,0:T(8,128)(2,1)}, u32[]{:S(2)}, u32[]{:S(2)}) collective-permute-start(bf16[128,2048]{1,0:T(8,128)(2,1)} %get-tuple-element.120), channel_id=1, source_target_pairs={{0,1},{1,0},{2,3},{3,2},{4,5},{5,4},{6,7},{7,6},{8,9},{9,8},{10,11... | collective-permute-start | bytes 1572872 | tf_op jit(solution)/shard_map/ppermute | solution.py:216
  553.5 27.2 %collective-permute-start.107 = (bf16[128,2048]{1,0:T(8,128)(2,1)S(1)}, bf16[128,2048]{1,0:T(8,128)(2,1)}, u32[]{:S(2)}, u32[]{:S(2)}) collective-permute-start(bf16[128,2048]{1,0:T(8,128)(2,1)S(1)} %get-tuple-element.121), channel_id=1, source_target_pairs={{0,1},{1,0},{2,3},{3,2},{4,5},{5,4},{6,7},{7,6},{8,9},{9,8},{10,11... | collective-permute-start | bytes 1572872 | tf_op jit(solution)/shard_map/ppermute | solution.py:216
  554.0 21.4 %collective-permute-start.111 = (bf16[512,256]{1,0:T(8,128)(2,1)}, bf16[512,256]{1,0:T(8,128)(2,1)}, u32[]{:S(2)}, u32[]{:S(2)}) collective-permute-start(bf16[512,256]{1,0:T(8,128)(2,1)} %convolution_convert_fusion.12), channel_id=1, source_target_pairs={{0,4},{1,5},{2,6},{3,7},{4,0},{5,1},{6,2},{7,3},{8,12},{9,13},{10,... | collective-permute-start | bytes 786440 | tf_op jit(solution)/shard_map/ppermute | solution.py:216
  561.1 23.0 %collective-permute-start.110 = (bf16[512,256]{1,0:T(8,128)(2,1)}, bf16[512,256]{1,0:T(8,128)(2,1)}, u32[]{:S(2)}, u32[]{:S(2)}) collective-permute-start(bf16[512,256]{1,0:T(8,128)(2,1)} %convolution_convert_fusion.13), channel_id=1, source_target_pairs={{0,4},{1,5},{2,6},{3,7},{4,0},{5,1},{6,2},{7,3},{8,12},{9,13},{10,... | collective-permute-start | bytes 786440 | tf_op jit(solution)/shard_map/ppermute | solution.py:216
  571.6 21.5 %all-to-all-start.8 = ((bf16[4,256,128]{2,1,0:T(8,128)(2,1)}), bf16[4,256,128]{2,1,0:T(8,128)(2,1)S(1)}, u32[]{:S(2)}, u32[]{:S(2)}) async-start(bf16[4,256,128]{2,1,0:T(8,128)(2,1)} %pad_maximum_fusion.24), calls=%async_computation.8 | async-start | bytes 524288 | tf_op jit(solution)/shard_map/all_to_all | solution.py:246
  593.1 26.3 %all-to-all-start.6 = ((bf16[4,128,256]{2,1,0:T(8,128)(2,1)}), bf16[4,128,256]{2,1,0:T(8,128)(2,1)S(1)}, u32[]{:S(2)}, u32[]{:S(2)}) async-start(bf16[4,128,256]{2,1,0:T(8,128)(2,1)} %bitcast.73), calls=%async_computation.6 | async-start | bytes 524288 | tf_op jit(solution)/shard_map/all_to_all | solution.py:246
  630.9 23.1 %all-to-all-start.9 = ((bf16[4,128,768]{2,1,0:T(8,128)(2,1)}), bf16[4,128,768]{2,1,0:T(8,128)(2,1)S(1)}, u32[]{:S(2)}, u32[]{:S(2)}) async-start(bf16[4,128,768]{2,1,0:T(8,128)(2,1)} %bitcast.93), calls=%async_computation.9 | async-start | bytes 1572864 | tf_op jit(solution)/shard_map/all_to_all | solution.py:246
  635.8 21.7 %collective-permute-start.129 = (f32[34,128]{1,0:T(8,128)S(1)}, f32[34,128]{1,0:T(8,128)S(1)}, u32[]{:S(2)}, u32[]{:S(2)}) collective-permute-start(f32[34,128]{1,0:T(8,128)S(1)} %fusion.168), channel_id=1, source_target_pairs={{0,8},{1,9},{2,10},{3,11},{4,12},{5,13},{6,14},{7,15},{8,0},{9,1},... | collective-permute-start | bytes 52232 | tf_op jit(solution)/shard_map/ppermute | solution.py:216
  654.0 22.7 %all-to-all-start.10 = ((bf16[4,128,768]{2,1,0:T(8,128)(2,1)}), bf16[4,128,768]{2,1,0:T(8,128)(2,1)S(1)}, u32[]{:S(2)}, u32[]{:S(2)}) async-start(bf16[4,128,768]{2,1,0:T(8,128)(2,1)} %bitcast.321), calls=%async_computation.10 | async-start | bytes 1572864 | tf_op jit(solution)/shard_map/all_to_all | solution.py:246
  676.7 22.6 %all-to-all-start.11 = ((bf16[4,768,128]{2,1,0:T(8,128)(2,1)}), bf16[4,768,128]{2,1,0:T(8,128)(2,1)S(1)}, u32[]{:S(2)}, u32[]{:S(2)}) async-start(bf16[4,768,128]{2,1,0:T(8,128)(2,1)} %pad_maximum_fusion.8), calls=%async_computation.11 | async-start | bytes 1572864 | tf_op jit(solution)/shard_map/all_to_all | solution.py:246
  (204 other events, 3154.6 us)

commit v2 on v1

v2 whole, which is shorter than its diff:
```python
import functools

import jax
import jax.numpy as jnp
from jax import lax
from jax.experimental import pallas as pl
from jax.experimental.pallas import tpu as pltpu
from jax.sharding import PartitionSpec as P

HEAD_SIZE = 128
ROWS_DEV = 64

EPSILON = 1e-06
ROPE_BASE = 1000000.0
MASKED = -1e30

CORE = 1
SPLIT = 8

BF = jnp.bfloat16
F32 = jnp.float32
MIB = 1 << 20


def dot(left, right):
    return jnp.dot(left, right, preferred_element_type=F32)


def dot_nt(left, right):
    return lax.dot_general(left, right, (((1,), (1,)), ((), ())), preferred_element_type=F32)


def dot_tn(left, right):
    return lax.dot_general(left, right, (((0,), (0,)), ((), ())), preferred_element_type=F32)


def tables(positions, head_width):
    half_width = head_width // 2
    inverse = ROPE_BASE ** (-(jnp.arange(half_width, dtype=F32) * 2.0 / head_width))
    angles = positions.astype(F32)[:, None] * inverse[None, :]
    angles = jnp.concatenate([angles, angles], axis=-1)
    return (jnp.cos(angles), jnp.sin(angles))


def call(body, name, outs, ins, ties=(), scratch=(), limit=32, specs=None):
    ins, ties = list(ins), list(ties)
    count = len(ins)

    def kernel(*refs):
        body(*refs[:count], *refs[count + len(ties) :])

    in_specs = [pl.BlockSpec(memory_space=pltpu.VMEM)] * count
    for at, spec in (specs or {}).items():
        in_specs[at] = spec
    return pl.pallas_call(
        kernel,
        grid=(1,) if specs else (),
        out_shape=[jax.ShapeDtypeStruct(s, d) for s, d in outs],
        in_specs=in_specs + [pl.BlockSpec(memory_space=pl.ANY)] * len(ties),
        out_specs=[pl.BlockSpec(memory_space=pltpu.VMEM)] * len(outs),
        scratch_shapes=list(scratch),
        compiler_params=pltpu.CompilerParams(vmem_limit_bytes=limit * MIB),
        cost_estimate=pl.CostEstimate(flops=0, bytes_accessed=0, transcendentals=0),
        name=name,
    )(*ins, *ties)


def rms(value):
    return lax.rsqrt(jnp.mean(value * value, axis=-1, keepdims=True) + EPSILON)


def flip_sign(shape):
    lane = lax.broadcasted_iota(jnp.int32, shape, 1)
    return jnp.where(lane < HEAD_SIZE // 2, -1.0, 1.0).astype(F32)


def rope(raw, gain, cosine, sine):
    scaled = raw * rms(raw) * gain
    turned = pltpu.roll(scaled, HEAD_SIZE // 2, 1) * flip_sign(scaled.shape)
    return scaled * cosine + turned * sine


def rope_back(grad, raw, gain, cosine, sine):
    swung = grad * sine
    turned = pltpu.roll(swung, HEAD_SIZE // 2, 1) * flip_sign(swung.shape)
    d_scaled = grad * cosine - turned
    scale = rms(raw)
    unit = raw * scale
    d_gain = jnp.sum(d_scaled * unit, axis=0, keepdims=True)
    d_unit = d_scaled * gain
    d_raw = scale * (d_unit - unit * jnp.mean(d_unit * unit, axis=-1, keepdims=True))
    return d_raw, d_gain


def norm_back(grad, value, gain):
    scale = rms(value)
    unit = value * scale
    d_gain = jnp.sum(grad * unit, axis=0, keepdims=True)
    d_unit = grad * gain
    return scale * (d_unit - unit * jnp.mean(d_unit * unit, axis=-1, keepdims=True)), d_gain


def assemble(pieces, out_ref, segments, rows):
    block = len(pieces) * rows
    for m, piece in enumerate(pieces):
        for s in range(segments):
            out_ref[s * block + m * rows : s * block + (m + 1) * rows, :] = piece[
                s * rows : (s + 1) * rows, :
            ]


def local(
    layer_input,
    query_weight,
    key_matrix,
    value_matrix,
    output_weight,
    gate_weight,
    up_weight,
    down_weight,
    attn_gain,
    mlp_gain,
    query_gain,
    key_gain,
    cotangent,
):
    ways = lax.axis_size("dp")
    place = lax.axis_index("dp")
    side = lax.axis_index("tp")
    segments, _, rows, width = layer_input.shape
    piece = width // ways
    row_bits = [1 << k for k in range(ways.bit_length() - 1) if (1 << k) not in (CORE, SPLIT)]
    near, far = row_bits, row_bits[::-1]
    groups = 1 << len(row_bits)
    chunk = 4 * piece
    block = 8 * rows
    half = 4 * rows
    all_rows = segments * block
    own = segments * rows
    scale = HEAD_SIZE**-0.5
    wide_q = query_weight.shape[1] // 4
    heads_q = wide_q // HEAD_SIZE
    wide_f = gate_weight.shape[1] // 4

    def mix_list(order):
        mixes = [0]
        for bit in reversed(order):
            mixes = mixes + [mix | bit for mix in mixes]
        return mixes

    mixes = mix_list(near)
    slot = {mix: j for j, mix in enumerate(mixes)}
    quads = [[mix | CORE * (n & 1) | SPLIT * (n >> 1) for n in range(4)] for mix in mixes]
    local_order = [k for four in quads for k in four]

    def swap(value, bit):
        with jax.named_scope("swap%d" % bit):
            return lax.ppermute(value, "dp", [(i, i ^ bit) for i in range(ways)])

    def swap_tp(value):
        with jax.named_scope("swaptp"):
            return lax.ppermute(value, "tp", [(0, 1), (1, 0)])

    def trade(value, name):
        with jax.named_scope(name):
            return lax.all_to_all(value, "dp", 0, 0, axis_index_groups=quads, tiled=True)

    def turn(blocks):
        for bit in row_bits:
            flag = (place & bit) != 0
            blocks = [jnp.where(flag, blocks[k ^ bit], blocks[k]) for k in range(ways)]
        return blocks

    def to_local(value):
        blocks = turn([value[..., k * piece : (k + 1) * piece] for k in range(ways)])
        return jnp.concatenate([blocks[k] for k in local_order], axis=-1)

    def from_local(value):
        where = {k: n for n, k in enumerate(local_order)}
        blocks = [value[..., where[k] * piece : (where[k] + 1) * piece] for k in range(ways)]
        return jnp.concatenate(turn(blocks), axis=-1)

    def spread(value, order, name):
        held = {0: value}
        with jax.named_scope(name):
            for bit in order:
                for mix in list(held):
                    held[mix ^ bit] = swap(held[mix], bit)
        return [held[mix] for mix in mixes]

    wide_k = 2 * HEAD_SIZE
    wide_1 = 2 * wide_q + wide_k

    def pack_first(q_ref, k_ref, v_ref, o_ref, out_ref):
        for n in range(4):
            out_ref[n, :, :wide_q] = q_ref[:, n * wide_q : (n + 1) * wide_q]
            for at, ref in ((wide_q, k_ref), (wide_q + HEAD_SIZE, v_ref)):
                out_ref[n, :, at : at + HEAD_SIZE] = ref[:, n * HEAD_SIZE : (n + 1) * HEAD_SIZE]
            for b in range(0, wide_q, piece):
                at = wide_q + wide_k + b
                out_ref[n, :, at : at + piece] = o_ref[n * wide_q + b : n * wide_q + b + piece, :]

    def pack_columns(ref, out_ref):
        for n in range(4):
            out_ref[n] = ref[:, n * wide_f : (n + 1) * wide_f]

    (packed,) = call(
        pack_first,
        "pack1",
        [((4, piece, wide_1), BF)],
        [query_weight, key_matrix, value_matrix, output_weight],
    )
    wide_shape = ((4, piece, wide_f), BF)
    first = trade(packed, "t_first").reshape(chunk, wide_1)
    (packed,) = call(pack_columns, "pack2", [wide_shape], [gate_weight])
    gate = trade(packed, "t_gate").reshape(chunk, wide_f)
    (packed,) = call(pack_columns, "pack3", [wide_shape], [up_weight], ties=[gate])
    up = trade(packed, "t_up").reshape(chunk, wide_f)
    down = trade(down_weight.reshape(4, wide_f, piece), "t_down")
    q_parts = spread(first[:, :wide_q], near, "s_q")
    kv_parts = spread(first[:, wide_q : wide_q + wide_k], far, "s_kv")
    o_parts = spread(first[:, wide_q + wide_k :], near, "s_o")
    gate_parts = spread(gate, near, "s_gate")
    up_parts = spread(up, far, "s_up")
    down_parts = spread(down, near, "s_down")

    def gather_rows(value, name):
        held = [value]
        with jax.named_scope(name):
            held = held + [swap(v, SPLIT) for v in held]
            held = held + [swap_tp(v) for v in held]
            return held + [swap(v, CORE) for v in held]

    def add_split(kept, got, name, ties=()):
        count = kept.shape[1] // 2

        def body(kept_ref, got_ref, sent_out, kept_out):
            total = kept_ref[...].astype(F32) + got_ref[...].astype(F32)
            kept_out[...] = total[:, :count].astype(BF)
            sent_out[...] = total[:, count:].astype(BF)

        shape = (segments, count, width)
        return call(body, name, [(shape, BF), (shape, BF)], [kept, got], ties=ties)

    def scatter_rows(sent, kept, name, ties_c=(), ties_t=()):
        with jax.named_scope(name):
            sent, kept = add_split(kept, swap(sent, CORE), name + "_c", ties_c)
            sent, kept = add_split(kept, swap_tp(sent), name + "_t", ties_t)
            return kept.reshape(own, width), swap(sent, SPLIT).reshape(own, width)

    pair = [((segments, half, width), BF)] * 2

    def store_pair(sent_ref, kept_ref, s, value, at):
        stop = at + value.shape[1]
        kept_ref[s, :, at:stop] = value[:half].astype(BF)
        sent_ref[s, :, at:stop] = value[half:].astype(BF)

    index = jnp.arange(all_rows, dtype=jnp.int32)
    segment_by = index // block
    m_by = (index // rows) % 8

    def positions(base):
        at = base ^ ((m_by & 1) * SPLIT) ^ ((m_by >> 2) * CORE)
        return (
            (segment_by * ways + at) * ROWS_DEV
            + (side ^ ((m_by >> 1) & 1)) * rows
            + index % rows
        )

    query_pos = positions(place)
    cosine, sine = tables(query_pos, HEAD_SIZE)
    qpos = query_pos[:, None]
    kpos = jnp.stack([positions(place ^ mix).reshape(segments, block) for mix in mixes], axis=1)
    kpos = kpos.reshape(1, segments * groups * block)
    span = min(groups, 2)

    gain_q, gain_k = query_gain[None], key_gain[None]
    row_mask = ways - 1 - CORE - SPLIT
    where_spec = pl.BlockSpec(memory_space=pltpu.SMEM)
    where = (place & row_mask)[None]

    def lanes_of(where_ref, n):
        return pl.ds(pl.multiple_of((local_order[n] ^ where_ref[0]) * piece, piece), piece)

    def enter(where_ref, x_ref, c_ref, ga_ref, gm_ref, x_out, c_out, ga_out, gm_out, out_ref):
        for n in range(ways):
            lanes, here = lanes_of(where_ref, n), slice(n * piece, (n + 1) * piece)
            x_out[:, here] = x_ref[:, lanes]
            c_out[:, here] = c_ref[:, lanes]
            ga_out[:, here] = ga_ref[:, lanes]
            gm_out[:, here] = gm_ref[:, lanes]
        value = x_out[...].astype(F32)
        out_ref[...] = (value * rms(value) * ga_out[...]).astype(BF)

    own_shape, line_shape = (own, width), (1, width)
    if piece % 128 == 0:
        x_own, c_own, gain_a, gain_m, normed = call(
            enter,
            "enter",
            [
                (own_shape, BF),
                (own_shape, BF),
                (line_shape, F32),
                (line_shape, F32),
                (own_shape, BF),
            ],
            [
                where,
                layer_input.reshape(own_shape),
                cotangent.reshape(own_shape),
                attn_gain[None],
                mlp_gain[None],
            ],
            specs={0: where_spec},
        )
    else:
        x_own = to_local(layer_input.reshape(own_shape))
        c_own = to_local(cotangent.reshape(own_shape))
        gain_a = to_local(attn_gain[None])
        gain_m = to_local(mlp_gain[None])

        def first_norm(x_ref, gain_ref, out_ref):
            value = x_ref[...].astype(F32)
            out_ref[...] = (value * rms(value) * gain_ref[...]).astype(BF)

        (normed,) = call(first_norm, "norm1", [(own_shape, BF)], [x_own, gain_a])

    def put_back(values, name):
        if piece % 128:
            return [from_local(v) for v in values]

        def body(*refs):
            where_ref, ins, outs = refs[0], refs[1 : 1 + len(values)], refs[1 + len(values) :]
            for in_ref, out_ref in zip(ins, outs):
                for n in range(ways):
                    out_ref[:, lanes_of(where_ref, n)] = in_ref[:, n * piece : (n + 1) * piece]

        outs = [(v.shape, v.dtype) for v in values]
        return call(body, name, outs, [where, *values], specs={0: where_spec})

    normed_parts = gather_rows(normed, "g_norm1")
    c_parts = gather_rows(c_own, "g_cot")

    def project(*refs):
        parts, refs = refs[:8], refs[8:]
        wq, wkv, refs = refs[:groups], refs[groups : 2 * groups], refs[2 * groups :]
        cos_ref, sin_ref, gq_ref, gk_ref, x_ref, q_ref, kv_ref, q_raw_ref, k_raw_ref = refs
        assemble(parts, x_ref, segments, rows)
        for s in range(segments):
            at = slice(s * block, (s + 1) * block)
            q = sum(dot(x_ref[at, j * chunk : (j + 1) * chunk], wq[j][...]) for j in range(groups))
            kv = sum(
                dot(x_ref[at, j * chunk : (j + 1) * chunk], wkv[j][...]) for j in range(groups)
            )
            q_raw_ref[at, :] = q
            k_raw_ref[at, :] = kv[:, :HEAD_SIZE]
            cos, sin = cos_ref[at, :], sin_ref[at, :]
            for h in range(heads_q):
                lanes = slice(h * HEAD_SIZE, (h + 1) * HEAD_SIZE)
                q_ref[at, lanes] = rope(q[:, lanes], gq_ref[...], cos, sin).astype(BF)
            kv_ref[at, :HEAD_SIZE] = rope(kv[:, :HEAD_SIZE], gk_ref[...], cos, sin).astype(BF)
            kv_ref[at, HEAD_SIZE:] = kv[:, HEAD_SIZE:].astype(BF)

    normed_all, q, kv, q_raw, k_raw = call(
        project,
        "project",
        [
            ((all_rows, width), BF),
            ((all_rows, wide_q), BF),
            ((all_rows, 2 * HEAD_SIZE), BF),
            ((all_rows, wide_q), F32),
            ((all_rows, HEAD_SIZE), F32),
        ],
        [*normed_parts, *q_parts, *kv_parts, cosine, sine, gain_q, gain_k],
        ties=[gate],
    )
    kv_all = spread(kv, near, "s_keys")

    def load_keys(parts, scratch):
        for j, part in enumerate(parts):
            for s in range(segments):
                scratch[s * groups + j] = part[s * block : (s + 1) * block, :]

    def stack_heads(ref, s):
        at = slice(s * block, (s + 1) * block)
        return jnp.concatenate(
            [ref[at, h * HEAD_SIZE : (h + 1) * HEAD_SIZE] for h in range(heads_q)], axis=0
        )

    def load_out_weight(parts, scratch):
        for j, part in enumerate(parts):
            for n in range(4):
                at = (4 * j + n) * piece
                for b in range(0, wide_q, piece):
                    scratch[b : b + piece, at : at + piece] = part[
                        n * piece : (n + 1) * piece, b : b + piece
                    ]

    def load_down_weight(parts, scratch):
        for j, part in enumerate(parts):
            for n in range(4):
                at = (4 * j + n) * piece
                scratch[:, at : at + piece] = part[n]

    strip = min(chunk * groups, 512)

    def attend(*refs):
        kv_refs, wo, refs = refs[:groups], refs[groups : 2 * groups], refs[2 * groups :]
        q_ref, qpos_ref, kpos_ref, out_ref, lse_ref, sent_ref, kept_ref, keys, w_out = refs
        load_keys(kv_refs, keys)
        load_out_weight(wo, w_out)
        for s in range(segments):
            at = slice(s * block, (s + 1) * block)
            q = stack_heads(q_ref, s)
            pos = jnp.concatenate([qpos_ref[at, :]] * heads_q, axis=0)

            high = jnp.full((q.shape[0], 1), MASKED, F32)
            summed = jnp.zeros((q.shape[0], 1), F32)
            acc = jnp.zeros((q.shape[0], HEAD_SIZE), F32)
            for n in range(0, (s + 1) * groups, span):
                both = keys[n : n + span].reshape(span * block, 2 * HEAD_SIZE)
                scores = dot_nt(q, both[:, :HEAD_SIZE]) * scale
                key_at = kpos_ref[:, n * block : (n + span) * block]
                scores = jnp.where(key_at <= pos, scores, MASKED)
                top = jnp.maximum(high, jnp.max(scores, axis=-1, keepdims=True))
                shrink = jnp.exp(high - top)
                probs = jnp.exp(scores - top)
                summed = summed * shrink + jnp.sum(probs, axis=-1, keepdims=True)
                acc = acc * shrink + dot(probs.astype(BF), both[:, HEAD_SIZE:])
                high = top
            acc = acc / summed
            lse_ref[s] = high + jnp.log(summed)
            acc = jnp.concatenate(
                [acc[h * block : (h + 1) * block] for h in range(heads_q)], axis=1
            )
            out_ref[at, :] = acc
            heads = acc.astype(BF)
            for n in range(0, width, strip):
                store_pair(sent_ref, kept_ref, s, dot(heads, w_out[:, n : n + strip]), n)

    attended, lse, sent, kept = call(
        attend,
        "attend",
        [
            ((all_rows, wide_q), F32),
            ((segments, heads_q * block, 1), F32),
            *pair,
        ],
        [*kv_all, *o_parts, q, qpos, kpos],
        ties=[up],
        scratch=[
            pltpu.VMEM((segments * groups, block, 2 * HEAD_SIZE), BF),
            pltpu.VMEM((wide_q, width), BF),
        ],
        limit=40,
    )
    kept, got = scatter_rows(
        sent, kept, "rs1", [gate_parts[slot[near[0]]]], [down, c_parts[1], gate_parts[slot[far[0]]]]
    )

    def second_norm(x_ref, kept_ref, got_ref, gain_ref, mid_ref, out_ref):
        value = x_ref[...].astype(F32) + (
            kept_ref[...].astype(F32) + got_ref[...].astype(F32)
        )
        mid_ref[...] = value
        out_ref[...] = (value * rms(value) * gain_ref[...]).astype(BF)

    middle, normed2 = call(
        second_norm,
        "norm2",
        [((own, width), F32), ((own, width), BF)],
        [x_own, kept, got, gain_m],
        ties=[*c_parts, *gate_parts, up_parts[slot[far[0]]]],
    )
    normed2_parts = gather_rows(normed2, "g_norm2")

    def feed(*refs):
        parts, c_refs, refs = refs[:8], refs[8:16], refs[16:]
        wg, wu, wd = refs[:groups], refs[groups : 2 * groups], refs[2 * groups : 3 * groups]
        (
            x_ref,
            c_ref,
            active_ref,
            dg_ref,
            du_ref,
            sent_ref,
            kept_ref,
            w_down,
        ) = refs[3 * groups :]
        assemble(parts, x_ref, segments, rows)
        assemble(c_refs, c_ref, segments, rows)
        load_down_weight(wd, w_down)

        for s in range(segments):
            at = slice(s * block, (s + 1) * block)
            gate_pre = sum(
                dot(x_ref[at, j * chunk : (j + 1) * chunk], wg[j][...]) for j in range(groups)
            )
            up_pre = sum(
                dot(x_ref[at, j * chunk : (j + 1) * chunk], wu[j][...]) for j in range(groups)
            )
            sigma = jax.nn.sigmoid(gate_pre)
            swish = gate_pre * sigma
            active_ref[at, :] = (swish * up_pre).astype(BF)
            d_active = dot_nt(c_ref[at, :], w_down[...])
            d_gate = (d_active * up_pre * sigma * (1.0 + gate_pre * (1.0 - sigma))).astype(BF)
            d_upper = (d_active * swish).astype(BF)
            dg_ref[at, :] = d_gate
            du_ref[at, :] = d_upper
            for j in range(groups):
                value = dot_nt(d_gate, wg[j][...]) + dot_nt(d_upper, wu[j][...])
                lanes = slice(j * chunk, (j + 1) * chunk)
                kept_ref[s, :, lanes] = value[:half].astype(BF)
                sent_ref[s, :, lanes] = value[half:].astype(BF)

    normed2_all, c_all, active, d_gate, d_upper, sent, kept = call(
        feed,
        "feed",
        [
            ((all_rows, width), BF),
            ((all_rows, width), BF),
            ((all_rows, wide_f), BF),
            ((all_rows, wide_f), BF),
            ((all_rows, wide_f), BF),
            *pair,
        ],
        [*normed2_parts, *c_parts, *gate_parts, *up_parts, *down_parts],
        scratch=[pltpu.VMEM((wide_f, width), BF)],
        limit=52,
    )
    kept, got = scatter_rows(sent, kept, "rs2")

    def grad_in(x_all, grads, orders, name):
        lists = [mix_list(order) for order in orders]

        def body(*refs):
            x_ref, g_refs, outs = refs[0], refs[1 : 1 + len(grads)], refs[1 + len(grads) :]
            for g_ref, mix, n in zip(g_refs, lists, range(len(grads))):
                for at, which in enumerate(mix):
                    j = slot[which]
                    value = dot_tn(x_ref[:, j * chunk : (j + 1) * chunk], g_ref[...]).astype(BF)
                    if at < groups // 2:
                        outs[2 * n + 1][at] = value
                    else:
                        outs[2 * n][at - groups // 2] = value

        outs = []
        for g in grads:
            outs += [((groups // 2, chunk, g.shape[1]), BF)] * 2
        return call(body, name, outs, [x_all, *grads], limit=48)

    def grad_out(left, c_value, order, name):
        mix = mix_list(order)
        tall = left.shape[1]

        def body(left_ref, c_ref, sent_ref, kept_ref):
            for at, which in enumerate(mix):
                j = slot[which]
                value = dot_tn(
                    left_ref[...].astype(BF), c_ref[:, j * chunk : (j + 1) * chunk]
                ).astype(BF)
                for n in range(4):
                    part = value[:, n * piece : (n + 1) * piece]
                    if at < groups // 2:
                        kept_ref[at, n] = part
                    else:
                        sent_ref[at - groups // 2, n] = part

        return call(
            body, name, [((groups // 2, 4, tall, piece), BF)] * 2, [left, c_value], limit=48
        )

    def reduce_groups(sent, kept, order, name):
        with jax.named_scope(name):
            for bit in order[:-1]:
                total = kept.astype(F32) + swap(sent, bit).astype(F32)
                count = total.shape[0] // 2
                kept, sent = total[:count].astype(BF), total[count:].astype(BF)
            return (kept.astype(F32) + swap(sent, order[-1]).astype(F32))[0]

    down_sums = reduce_groups(*grad_out(active, c_all, near, "w_down"), near, "r_down")
    gate_sent, gate_kept, up_sent, up_kept = grad_in(
        normed2_all, [d_gate, d_upper], [near, far], "w_gate_up"
    )
    gate_sums = reduce_groups(gate_sent, gate_kept, near, "r_gate")
    up_sums = reduce_groups(up_sent, up_kept, far, "r_up")
    down_grad = trade(down_sums.astype(BF), "t_ddown").astype(F32).reshape(4 * wide_f, piece)
    gate_up = jnp.concatenate([gate_sums, up_sums], axis=1).astype(BF)
    gate_up = trade(gate_up.reshape(4, piece, 2 * wide_f), "t_dgu").astype(F32)

    def join(value, start, stop):
        return jnp.concatenate([value[n, :, start:stop] for n in range(4)], axis=1)

    gate_grad = join(gate_up, 0, wide_f)
    up_grad = join(gate_up, wide_f, 2 * wide_f)

    def norm_step_back(kept_ref, got_ref, mid_ref, gain_ref, c_ref, d_ref, low_ref, gain_out):
        grad = kept_ref[...].astype(F32) + got_ref[...].astype(F32)
        back, gain_grad = norm_back(grad, mid_ref[...], gain_ref[...])
        total = c_ref[...].astype(F32) + back
        d_ref[...] = total
        low_ref[...] = total.astype(BF)
        gain_out[...] = gain_grad

    d_middle, d_branch, d_gain_m = call(
        norm_step_back,
        "norm2_back",
        [((own, width), F32), ((own, width), BF), ((1, width), F32)],
        [kept, got, middle, gain_m, c_own],
    )
    d_parts = gather_rows(d_branch, "g_branch")

    def feed_out(*refs):
        wd, refs = refs[:groups], refs[groups:]
        active_ref, sent_ref, kept_ref, w_down = refs
        load_down_weight(wd, w_down)
        for s in range(segments):
            at = slice(s * block, (s + 1) * block)
            for n in range(0, width, strip):
                store_pair(
                    sent_ref, kept_ref, s, dot(active_ref[at, :], w_down[:, n : n + strip]), n
                )

    out_sent, out_kept = call(
        feed_out,
        "feed_out",
        pair,
        [*down_parts, active],
        ties=[],
        scratch=[pltpu.VMEM((wide_f, width), BF)],
    )
    out_kept, out_got = scatter_rows(out_sent, out_kept, "rs3")
    layer_output = (middle + (out_kept.astype(F32) + out_got.astype(F32))).astype(BF)
    layer_output = put_back([layer_output], "leave1")[0].reshape(layer_input.shape)

    key_mix, value_mix = mix_list(near), mix_list(far)

    def attend_back(*refs):
        parts, kv_refs, wo = refs[:8], refs[8 : 8 + groups], refs[8 + groups : 8 + 2 * groups]
        (
            q_ref,
            qpos_ref,
            kpos_ref,
            out_ref,
            lse_ref,
            q_raw_ref,
            cos_ref,
            sin_ref,
            gq_ref,
            d_all_ref,
            dq_ref,
            gain_out,
            k_sent,
            k_kept,
            v_sent,
            v_kept,
            keys,
            w_out,
            sums,
        ) = refs[8 + 2 * groups :]
        assemble(parts, d_all_ref, segments, rows)
        load_keys(kv_refs, keys)
        load_out_weight(wo, w_out)
        sums[...] = jnp.zeros_like(sums)
        gain_total = jnp.zeros((1, HEAD_SIZE), F32)
        for s in range(segments):
            at = slice(s * block, (s + 1) * block)
            q = stack_heads(q_ref, s)
            out = stack_heads(out_ref, s)
            d_heads = dot_nt(d_all_ref[at, :], w_out[...]).astype(BF)
            grad = jnp.concatenate(
                [d_heads[:, h * HEAD_SIZE : (h + 1) * HEAD_SIZE] for h in range(heads_q)], axis=0
            )
            delta = jnp.sum(out * grad.astype(F32), axis=-1, keepdims=True)
            lse = lse_ref[s]
            pos = jnp.concatenate([qpos_ref[at, :]] * heads_q, axis=0)

            dq = jnp.zeros((q.shape[0], HEAD_SIZE), F32)
            for n in range(0, (s + 1) * groups, span):
                both = keys[n : n + span].reshape(span * block, 2 * HEAD_SIZE)
                key = both[:, :HEAD_SIZE]
                scores = dot_nt(q, key) * scale
                key_at = kpos_ref[:, n * block : (n + span) * block]
                scores = jnp.where(key_at <= pos, scores, MASKED)
                probs = jnp.exp(scores - lse)
                d_probs = dot_nt(grad, both[:, HEAD_SIZE:])
                d_scores = (probs * (d_probs - delta)).astype(BF)
                d_keys = dot_tn(d_scores, q) * scale
                d_values = dot_tn(probs.astype(BF), grad)
                both = jnp.concatenate([d_keys, d_values], axis=1)
                both = both.reshape(span, block, 2 * HEAD_SIZE)
                sums[n : n + span] = sums[n : n + span] + both
                dq = dq + dot(d_scores, key)
            dq = dq * scale
            for h in range(heads_q):
                lanes = slice(h * HEAD_SIZE, (h + 1) * HEAD_SIZE)
                d_raw, d_gain = rope_back(
                    dq[h * block : (h + 1) * block],
                    q_raw_ref[at, lanes],
                    gq_ref[...],
                    cos_ref[at, :],
                    sin_ref[at, :],
                )
                dq_ref[at, lanes] = d_raw.astype(BF)
                gain_total = gain_total + d_gain
        gain_out[...] = gain_total
        for mix, lane, sent_ref, kept_ref in (
            (key_mix, 0, k_sent, k_kept),
            (value_mix, HEAD_SIZE, v_sent, v_kept),
        ):
            for n, which in enumerate(mix):
                for s in range(segments):
                    value = sums[s * groups + slot[which], :, lane : lane + HEAD_SIZE].astype(BF)
                    rows_at = slice(s * block, (s + 1) * block)
                    if n < groups // 2:
                        kept_ref[n, rows_at, :] = value
                    else:
                        sent_ref[n - groups // 2, rows_at, :] = value

    part_shape = ((groups // 2, all_rows, HEAD_SIZE), BF)
    d_all, d_q, d_gain_q, k_sent, k_kept, v_sent, v_kept = call(
        attend_back,
        "attend_back",
        [
            ((all_rows, width), BF),
            ((all_rows, wide_q), BF),
            ((1, HEAD_SIZE), F32),
            part_shape,
            part_shape,
            part_shape,
            part_shape,
        ],
        [
            *d_parts,
            *kv_all,
            *o_parts,
            q,
            qpos,
            kpos,
            attended,
            lse,
            q_raw,
            cosine,
            sine,
            gain_q,
        ],
        scratch=[
            pltpu.VMEM((segments * groups, block, 2 * HEAD_SIZE), BF),
            pltpu.VMEM((wide_q, width), BF),
            pltpu.VMEM((segments * groups, block, 2 * HEAD_SIZE), F32),
        ],
        limit=52,
    )

    out_sums = reduce_groups(*grad_out(attended, d_all, near, "w_out"), near, "r_out")
    output_grad = trade(out_sums.astype(BF), "t_dout").astype(F32).reshape(4 * wide_q, piece)

    d_keys = reduce_groups(k_sent, k_kept, near, "r_k")
    d_values = reduce_groups(v_sent, v_kept, far, "r_v")

    def key_back(dk_ref, dv_ref, raw_ref, cos_ref, sin_ref, gain_ref, out_ref, gain_out):
        d_raw, d_gain = rope_back(
            dk_ref[...], raw_ref[...], gain_ref[...], cos_ref[...], sin_ref[...]
        )
        out_ref[:, :HEAD_SIZE] = d_raw.astype(BF)
        out_ref[:, HEAD_SIZE:] = dv_ref[...].astype(BF)
        gain_out[...] = d_gain

    d_kv, d_gain_k = call(
        key_back,
        "key_back",
        [((all_rows, 2 * HEAD_SIZE), BF), ((1, HEAD_SIZE), F32)],
        [d_keys, d_values, k_raw, cosine, sine, gain_k],
    )

    def project_back(*refs):
        wq, wkv, refs = refs[:groups], refs[groups : 2 * groups], refs[2 * groups :]
        dq_ref, dkv_ref, sent_ref, kept_ref = refs
        for s in range(segments):
            at = slice(s * block, (s + 1) * block)
            for j in range(groups):
                value = dot_nt(dq_ref[at, :], wq[j][...]) + dot_nt(dkv_ref[at, :], wkv[j][...])
                store_pair(sent_ref, kept_ref, s, value, j * chunk)

    sent, kept = call(
        project_back, "project_back", pair, [*q_parts, *kv_parts, d_q, d_kv]
    )
    kept, got = scatter_rows(sent, kept, "rs4")

    q_sent, q_kept, kv_sent, kv_kept = grad_in(
        normed_all, [d_q, d_kv], [near, far], "w_qkv"
    )
    q_sums = reduce_groups(q_sent, q_kept, near, "r_q")
    kv_sums = reduce_groups(kv_sent, kv_kept, far, "r_kv")
    qkv_sums = jnp.concatenate([q_sums, kv_sums], axis=1).astype(BF)
    qkv_sums = trade(qkv_sums.reshape(4, piece, qkv_sums.shape[1]), "t_dqkv").astype(F32)
    query_grad = join(qkv_sums, 0, wide_q)
    key_grad = join(qkv_sums, wide_q, wide_q + HEAD_SIZE)
    value_grad = join(qkv_sums, wide_q + HEAD_SIZE, wide_q + 2 * HEAD_SIZE)

    def last_back(kept_ref, got_ref, x_ref, gain_ref, d_ref, out_ref, gain_out):
        grad = kept_ref[...].astype(F32) + got_ref[...].astype(F32)
        back, gain_grad = norm_back(grad, x_ref[...].astype(F32), gain_ref[...])
        out_ref[...] = (d_ref[...] + back).astype(BF)
        gain_out[...] = gain_grad

    d_x, d_gain_a = call(
        last_back,
        "norm1_back",
        [((own, width), BF), ((1, width), F32)],
        [kept, got, x_own, gain_a, d_middle],
    )
    d_x, d_gain_a, d_gain_m = put_back([d_x, d_gain_a, d_gain_m], "leave2")
    input_grad = d_x.reshape(layer_input.shape)

    gains = jnp.concatenate([d_gain_a, d_gain_m, d_gain_q, d_gain_k], axis=1).reshape(-1, 128)
    for bit in [CORE, SPLIT] + row_bits:
        gains = gains + swap(gains, bit)
    gains = (gains + swap_tp(gains)).reshape(-1)
    return (
        layer_output,
        input_grad,
        query_grad,
        key_grad,
        value_grad,
        output_grad,
        gate_grad,
        up_grad,
        down_grad,
        gains[:width],
        gains[width : 2 * width],
        gains[2 * width : 2 * width + HEAD_SIZE],
        gains[2 * width + HEAD_SIZE :],
    )


def solution(mesh):
    rows_in = P(None, "dp", "tp", None)
    in_specs = (
        rows_in,
        P("dp", "tp"),
        P("dp", "tp"),
        P("dp", "tp"),
        P("tp", "dp"),
        P("dp", "tp"),
        P("dp", "tp"),
        P("tp", "dp"),
        P(),
        P(),
        P(),
        P(),
        rows_in,
    )
    out_specs = (
        rows_in,
        rows_in,
        P("dp", "tp"),
        P("dp", "tp"),
        P("dp", "tp"),
        P("tp", "dp"),
        P("dp", "tp"),
        P("dp", "tp"),
        P("tp", "dp"),
        P(),
        P(),
        P(),
        P(),
    )
    return jax.shard_map(local, mesh=mesh, in_specs=in_specs, out_specs=out_specs, check_vma=False)
```

time: 708 us -> 557 us (0.79)
  matrix products: 73 us -> 0 us
  starting transfers between devices: 171 us -> 111 us
  Pallas kernels: 17.8 us -> 57.1 us
  local copies, waits for them, and re-layouts: 62.6 us -> 30.7 us
  waiting for transfers between devices: 337 us -> 320 us
    dot_general x42 -> x0, matrix products: 73 us -> none  [the longest x24 31.1 us: dot_tn(): lax.dot_general(left, right, (((0,), (0,)), ((), ())), preferred_element_...]
    pallas_call x2 -> x28, Pallas kernels: 17.8 us -> 57.1 us  [call(): pl.pallas_call(kernel, grid=(1,) if specs else (), out_shape=[jax.ShapeDt...]
    all_to_all x12 -> x8, waiting for transfers between devices: 70.6 us -> 34.6 us  [trade(): lax.all_to_all(value, 'dp', 0, 0, axis_index_groups=quads, tiled=True)]
    ppermute x108 -> x69, starting transfers between devices: 94.8 us -> 61.5 us  [swap(): return lax.ppermute(value, 'dp', [(i, i ^ bit) for i in range(ways)])]
    ppermute x108 -> x69, waiting for transfers between devices: 195 us -> 226 us  [swap(): return lax.ppermute(value, 'dp', [(i, i ^ bit) for i in range(ways)])]
    unnamed x293 -> x220, local copies, waits for them, and re-layouts: 42.4 us -> 24.4 us
    all_to_all x12 -> x8, starting transfers between devices: 50.1 us -> 33 us  [trade(): lax.all_to_all(value, 'dp', 0, 0, axis_index_groups=quads, tiled=True)]
    ppermute x25 -> x13, waiting for transfers between devices: 72 us -> 60.1 us  [swap_tp(): return lax.ppermute(value, 'tp', [(0, 1), (1, 0)])]
  transfers between devices with their start and end apart: 145 -> 90, of which waited for: 73 -> 44; matrix products, arithmetic and copies ran while one was open for 20% -> 6% of each run, Pallas kernels for 3% -> 7%
where the time goes in v2:
time: 557 us; the launch traced here: 552 us
  waiting for transfers between devices  320 us (57%)
  starting transfers between devices  111 us (20%)
  Pallas kernels  57.1 us (10%)
  local copies, waits for them, and re-layouts  30.7 us (6%)
  other arithmetic  30 us (5%)
    ppermute x69, waiting for transfers between devices, swap(): return lax.ppermute(value, 'dp', [(i, i ^ bit) for i in range(ways)])  226 us
    ppermute x69, starting transfers between devices, swap(): return lax.ppermute(value, 'dp', [(i, i ^ bit) for i in range(ways)])  61.5 us
    ppermute x13, waiting for transfers between devices, swap_tp(): return lax.ppermute(value, 'tp', [(0, 1), (1, 0)])  60.1 us
    pallas_call x28, Pallas kernels, call(): pl.pallas_call(kernel, grid=(1,) if specs else (), out_shape=[jax.ShapeDt...  57.1 us
    all_to_all x8, waiting for transfers between devices, trade(): lax.all_to_all(value, 'dp', 0, 0, axis_index_groups=quads, tiled=True)  34.6 us
    all_to_all x8, starting transfers between devices, trade(): lax.all_to_all(value, 'dp', 0, 0, axis_index_groups=quads, tiled=True)  33 us
    unnamed x220, local copies, waits for them, and re-layouts  24.4 us
    ppermute x13, starting transfers between devices, swap_tp(): return lax.ppermute(value, 'tp', [(0, 1), (1, 0)])  16.9 us
  transfers between devices with their start and end apart: 90, of which 44 were waited for; matrix products, arithmetic and copies ran while one was open for 6% of the time, Pallas kernels for 7%

profile of v2, /device:TPU:0, one launch (start us, length us, event | category | flops | bytes accessed | tf_op | source)
XLA Modules:
  0.0 551.5 jit_solution(8152117372305800709)
XLA Ops:
  2.7 5.3 all-to-all-start.1
  9.1 19.9 %all-to-all-done.1 = bf16[4,128,768]{2,1,0:T(8,128)(2,1)S(1)} async-done(((bf16[4,128,768]{2,1,0:T(8,128)(2,1)}), bf16[4,128,768]{2,1,0:T(8,128)(2,1)S(1)}, u32[]{:S(2)}, u32[]{:S(2)}) %all-to-all-start.1) | async-done | bytes 786464 | tf_op jit(solution)/shard_map/t_gate/all_to_all | solution.py:166
  29.0 4.2 all-to-all-start
  39.3 24.5 %collective-permute-done.refs_1_ = bf16[64,2048]{1,0:T(8,128)(2,1)S(1)} collective-permute-done((bf16[64,2048]{1,0:T(8,128)(2,1)S(1)}, bf16[64,2048]{1,0:T(8,128)(2,1)S(1)}, u32[]{:S(2)}, u32[]{:S(2)}) %collective-permute-start) | collective-permute-done | bytes 262176 | tf_op jit(solution)/shard_map/g_norm1/swap8/ppermute | solution.py:158
  66.4 3.5 all-to-all-start.2
  75.5 9.8 %collective-permute-done.10.refs_13_.refs_5_ = bf16[512,256]{1,0:T(8,128)(2,1)S(1)} collective-permute-done((bf16[512,256]{1,0:T(8,128)(2,1)S(1)}, bf16[512,256]{1,0:T(8,128)(2,1)S(1)}, u32[]{:S(2)}, u32[]{:S(2)}) %collective-permute-start.10) | collective-permute-done | bytes 262176 | tf_op jit(solution)/shard_map/s_kv/swap4/ppermute | solution.py:158
  91.2 3.1 collective-permute-done.7.refs_9_.refs_1_
  94.3 5.2 collective-permute-done.9.refs_11_.refs_3_
  102.5 3.4 project.1
  113.4 4.4 collective-permute-done.14.refs_2_.refs_10_
  117.8 3.7 all-to-all-start.3
  121.8 11.5 %collective-permute-done.18.refs_7_.refs_15_ = bf16[512,256]{1,0:T(8,128)(2,1)} collective-permute-done((bf16[512,256]{1,0:T(8,128)(2,1)S(1)}, bf16[512,256]{1,0:T(8,128)(2,1)}, u32[]{:S(2)}, u32[]{:S(2)}) %collective-permute-start.18) | collective-permute-done | bytes 262176 | tf_op jit(solution)/shard_map/s_o/swap4/ppermute | solution.py:158
  133.3 6.8 %collective-permute-done.13.refs_1_.refs_9_ = bf16[512,256]{1,0:T(8,128)(2,1)} collective-permute-done((bf16[512,256]{1,0:T(8,128)(2,1)}, bf16[512,256]{1,0:T(8,128)(2,1)}, u32[]{:S(2)}, u32[]{:S(2)}) %collective-permute-start.13) | collective-permute-done | bytes 262176 | tf_op jit(solution)/shard_map/s_keys/swap4/ppermute | solution.py:158
  140.1 4.2 collective-permute-done.15.refs_3_.refs_11_
  147.1 5.2 attend.1
  154.2 8.0 %collective-permute-done.25.refs_6_.refs_10_ = bf16[64,2048]{1,0:T(8,128)(2,1)} collective-permute-done((bf16[64,2048]{1,0:T(8,128)(2,1)S(1)}, bf16[64,2048]{1,0:T(8,128)(2,1)}, u32[]{:S(2)}, u32[]{:S(2)}) %collective-permute-start.25) | collective-permute-done | bytes 262176 | tf_op jit(solution)/shard_map/g_cot/swaptp/ppermute | solution.py:162
  162.2 5.7 %collective-permute-done.22.refs_3_.refs_5_.refs_9_ = bf16[64,2048]{1,0:T(8,128)(2,1)} collective-permute-done((bf16[64,2048]{1,0:T(8,128)(2,1)S(1)}, bf16[64,2048]{1,0:T(8,128)(2,1)}, u32[]{:S(2)}, u32[]{:S(2)}) %collective-permute-start.22) | collective-permute-done | bytes 262176 | tf_op jit(solution)/shard_map/g_cot/swap8/ppermute | solution.py:158
  168.0 5.2 collective-permute-done.20.refs_2_.refs_14_.refs_18_
  178.5 4.2 collective-permute-done.26.refs_7_.refs_11_
  182.6 10.7 %collective-permute-done.21.refs_1_ = bf16[2,64,2048]{2,1,0:T(8,128)(2,1)S(1)} collective-permute-done((bf16[2,64,2048]{2,1,0:T(8,128)(2,1)}, bf16[2,64,2048]{2,1,0:T(8,128)(2,1)S(1)}, u32[]{:S(2)}, u32[]{:S(2)}) %collective-permute-start.21) | collective-permute-done | bytes 524320 | tf_op jit(solution)/shard_map/rs1/swaptp/ppermute | solution.py:162
  197.3 7.1 %collective-permute-start.43 = (bf16[512,768]{1,0:T(8,128)(2,1)S(1)}, bf16[512,768]{1,0:T(8,128)(2,1)S(1)}, u32[]{:S(2)}, u32[]{:S(2)}) collective-permute-start(bf16[512,768]{1,0:T(8,128)(2,1)S(1)} %bitcast.105), channel_id=1, source_target_pairs={{0,2},{1,3},{2,0},{3,1},{4,6},{5,7},{6,4},{7,5},{8,10},{9,11},{10,... | collective-permute-start | bytes 2359304 | tf_op jit(solution)/shard_map/s_up/swap2/ppermute | solution.py:158
  204.5 15.3 %collective-permute-done.32.refs_16_.refs_21_ = bf16[512,768]{1,0:T(8,128)(2,1)S(1)} collective-permute-done((bf16[512,768]{1,0:T(8,128)(2,1)S(1)}, bf16[512,768]{1,0:T(8,128)(2,1)S(1)}, u32[]{:S(2)}, u32[]{:S(2)}) %collective-permute-start.32) | collective-permute-done | bytes 786464 | tf_op jit(solution)/shard_map/s_up/swap4/ppermute | solution.py:158
  221.3 12.8 %collective-permute-done.24 = bf16[2,32,2048]{2,1,0:T(8,128)(2,1)S(1)} collective-permute-done((bf16[2,32,2048]{2,1,0:T(8,128)(2,1)S(1)}, bf16[2,32,2048]{2,1,0:T(8,128)(2,1)S(1)}, u32[]{:S(2)}, u32[]{:S(2)}) %collective-permute-start.24) | collective-permute-done | bytes 262176 | tf_op jit(solution)/shard_map/rs1/swap8/ppermute | solution.py:158
  234.4 3.5 collective-permute-start.36
  239.4 16.4 %collective-permute-done.36.refs_1_ = bf16[64,2048]{1,0:T(8,128)(2,1)S(1)} collective-permute-done((bf16[64,2048]{1,0:T(8,128)(2,1)S(1)}, bf16[64,2048]{1,0:T(8,128)(2,1)S(1)}, u32[]{:S(2)}, u32[]{:S(2)}) %collective-permute-start.36) | collective-permute-done | bytes 262176 | tf_op jit(solution)/shard_map/g_norm2/swap8/ppermute | solution.py:158
  258.6 4.7 collective-permute-done.38.refs_3_
  265.6 15.0 %feed.1 = (bf16[512,2048]{1,0:T(8,128)(2,1)}, bf16[512,2048]{1,0:T(8,128)(2,1)}, bf16[512,768]{1,0:T(8,128)(2,1)}, bf16[512,768]{1,0:T(8,128)(2,1)}, bf16[512,76...) custom-call(bf16[64,2048]{1,0:T(8,128)(2,1)S(1)} %get-tuple-element.98.refs_0_, ...), custom_call_target="tpu_custom_call" | custom-call | tf_op jit(solution)/shard_map/feed/pallas_call | solution.py:55
  288.0 6.5 %w_gate_up.1 = (bf16[2,512,768]{2,1,0:T(8,128)(2,1)S(1)}, bf16[2,512,768]{2,1,0:T(8,128)(2,1)S(1)}, bf16[2,512,768]{2,1,0:T(8,128)(2,1)}, bf16[2,512,768]{2,1,0:T(8,128)(2,1)}) custom-call(bf16[512,2048]{1,0:T(8,128)(2,1)} %get-tuple-element.143.refs_0_, bf16[512,768]{1,0:T(8,128)(2,1)S(1)} %copy-done.62, bf16[512,768]{1,0:T(8,128)(2,1)S(1)} %copy-done.63), custom_call_target="tpu_custom_call" | custom-call | tf_op jit(solution)/shard_map/w_gate_up/pallas_call | solution.py:55
  301.1 12.5 %collective-permute-done.49.refs_1_ = bf16[2,64,2048]{2,1,0:T(8,128)(2,1)S(1)} collective-permute-done((bf16[2,64,2048]{2,1,0:T(8,128)(2,1)S(1)}, bf16[2,64,2048]{2,1,0:T(8,128)(2,1)S(1)}, u32[]{:S(2)}, u32[]{:S(2)}) %collective-permute-start.49) | collective-permute-done | bytes 524320 | tf_op jit(solution)/shard_map/rs2/swaptp/ppermute | solution.py:162
  317.1 22.1 %collective-permute-done.50 = bf16[2,32,2048]{2,1,0:T(8,128)(2,1)S(1)} collective-permute-done((bf16[2,32,2048]{2,1,0:T(8,128)(2,1)S(1)}, bf16[2,32,2048]{2,1,0:T(8,128)(2,1)S(1)}, u32[]{:S(2)}, u32[]{:S(2)}) %collective-permute-start.50) | collective-permute-done | bytes 262176 | tf_op jit(solution)/shard_map/rs2/swap8/ppermute | solution.py:158
  340.4 3.4 collective-permute-start.51
  344.6 12.4 %collective-permute-done.71 = bf16[2,512,768]{2,1,0:T(8,128)(2,1)S(1)} collective-permute-done((bf16[2,512,768]{2,1,0:T(8,128)(2,1)S(1)}, bf16[2,512,768]{2,1,0:T(8,128)(2,1)S(1)}, u32[]{:S(2)}, u32[]{:S(2)}) %collective-permute-start.71) | collective-permute-done | bytes 1572896 | tf_op jit(solution)/shard_map/r_gate/swap2/ppermute | solution.py:158
  361.0 5.3 collective-permute-done.52.refs_2_
  366.2 4.3 collective-permute-done.53.refs_3_
  373.8 3.4 collective-permute-start.47
  379.5 9.6 %attend_back.1 = (bf16[512,2048]{1,0:T(8,128)(2,1)}, bf16[512,256]{1,0:T(8,128)(2,1)S(1)}, f32[1,128]{1,0:T(1,128)S(1)}, bf16[2,512,128]{2,1,0:T(8,128)(2,1)}, b...) custom-call(bf16[64,2048]{1,0:T(8,128)(2,1)S(1)} %get-tuple-element.112.refs_0_, ...), custom_call_target="tpu_custom_call" | custom-call | tf_op jit(solution)/shard_map/attend_back/pallas_call | solution.py:55
  395.2 4.4 all-to-all-start.7
  405.5 6.1 %collective-permute-done.60 = bf16[2,512,128]{2,1,0:T(8,128)(2,1)} collective-permute-done((bf16[2,512,128]{2,1,0:T(8,128)(2,1)}, bf16[2,512,128]{2,1,0:T(8,128)(2,1)}, u32[]{:S(2)}, u32[]{:S(2)}) %collective-permute-start.60) | collective-permute-done | bytes 262176 | tf_op jit(solution)/shard_map/r_v/swap4/ppermute | solution.py:158
  412.8 8.0 %collective-permute-done.59 = bf16[1,512,128]{2,1,0:T(8,128)(2,1)S(1)} collective-permute-done((bf16[1,512,128]{2,1,0:T(8,128)(2,1)S(1)}, bf16[1,512,128]{2,1,0:T(8,128)(2,1)S(1)}, u32[]{:S(2)}, u32[]{:S(2)}) %collective-permute-start.59) | collective-permute-done | bytes 131104 | tf_op jit(solution)/shard_map/r_k/swap4/ppermute | solution.py:158
  422.4 3.7 collective-permute-done.61
  433.9 3.3 collective-permute-done.65
  449.8 3.4 all-to-all-start.5
  457.6 5.3 all-to-all-done.5
  462.9 4.1 all-to-all-start.4
  471.5 9.4 %all-to-all-done.4 = bf16[4,128,512]{2,1,0:T(8,128)(2,1)} async-done(((bf16[4,128,512]{2,1,0:T(8,128)(2,1)}), bf16[4,128,512]{2,1,0:T(8,128)(2,1)}, u32[]{:S(2)}, u32[]{:S(2)}) %all-to-all-start.4) | async-done | bytes 524320 | tf_op jit(solution)/shard_map/t_dqkv/all_to_all | solution.py:166
  480.9 4.4 all-to-all-start.6
  492.2 9.5 %collective-permute-done.63.refs_1_ = bf16[2,64,2048]{2,1,0:T(8,128)(2,1)S(1)} collective-permute-done((bf16[2,64,2048]{2,1,0:T(8,128)(2,1)S(1)}, bf16[2,64,2048]{2,1,0:T(8,128)(2,1)S(1)}, u32[]{:S(2)}, u32[]{:S(2)}) %collective-permute-start.63) | collective-permute-done | bytes 524320 | tf_op jit(solution)/shard_map/rs4/swaptp/ppermute | solution.py:162
  506.6 25.0 %collective-permute-done.64 = bf16[2,32,2048]{2,1,0:T(8,128)(2,1)S(1)} collective-permute-done((bf16[2,32,2048]{2,1,0:T(8,128)(2,1)S(1)}, bf16[2,32,2048]{2,1,0:T(8,128)(2,1)S(1)}, u32[]{:S(2)}, u32[]{:S(2)}) %collective-permute-start.64) | collective-permute-done | bytes 262176 | tf_op jit(solution)/shard_map/rs4/swap8/ppermute | solution.py:158
  (438 shorter events, 160.0 us)
Async XLA Ops:
  2.7 26.3 %all-to-all-start.1 = ((bf16[4,128,768]{2,1,0:T(8,128)(2,1)}), bf16[4,128,768]{2,1,0:T(8,128)(2,1)S(1)}, u32[]{:S(2)}, u32[]{:S(2)}) async-start(bf16[4,128,768]{2,1,0:T(8,128)(2,1)} %pack2.1), calls=%async_computation.1 | async-start | bytes 1572864 | tf_op jit(solution)/shard_map/t_gate/all_to_all | solution.py:166
  29.0 37.4 %all-to-all-start = ((bf16[4,128,768]{2,1,0:T(8,128)(2,1)}), bf16[4,128,768]{2,1,0:T(8,128)(2,1)}, u32[]{:S(2)}, u32[]{:S(2)}) async-start(bf16[4,128,768]{2,1,0:T(8,128)(2,1)} %pack1.1), calls=%async_computation | async-start | bytes 1572864 | tf_op jit(solution)/shard_map/t_first/all_to_all | solution.py:166
  34.9 28.8 %collective-permute-start = (bf16[64,2048]{1,0:T(8,128)(2,1)S(1)}, bf16[64,2048]{1,0:T(8,128)(2,1)S(1)}, u32[]{:S(2)}, u32[]{:S(2)}) collective-permute-start(bf16[64,2048]{1,0:T(8,128)(2,1)S(1)} %get-tuple-element.86.refs_0_), channel_id=1, source_target_pairs={{0,8},{1,9},{2,10},{3,11},{4,12},{5,13},{6,14},{7,15},{8,0},{9,1},... | collective-permute-start | bytes 786440 | tf_op jit(solution)/shard_map/g_norm1/swap8/ppermute | solution.py:158
  37.8 27.5 %collective-permute-start.1 = (bf16[64,2048]{1,0:T(8,128)(2,1)S(1)}, bf16[64,2048]{1,0:T(8,128)(2,1)S(1)}, u32[]{:S(2)}, u32[]{:S(2)}) collective-permute-start(bf16[64,2048]{1,0:T(8,128)(2,1)S(1)} %get-tuple-element.86.refs_0_), channel_id=1, source_target_pairs={{0,16},{16,0},{1,17},{17,1},{2,18},{18,2},{3,19},{19,3},{4,20},{20... | collective-permute-start | bytes 786440 | tf_op jit(solution)/shard_map/g_norm1/swaptp/ppermute | solution.py:162
  39.3 32.0 %collective-permute-start.3 = (bf16[64,2048]{1,0:T(8,128)(2,1)S(1)}, bf16[64,2048]{1,0:T(8,128)(2,1)}, u32[]{:S(2)}, u32[]{:S(2)}) collective-permute-start(bf16[64,2048]{1,0:T(8,128)(2,1)S(1)} %get-tuple-element.86.refs_0_), channel_id=1, source_target_pairs={{0,1},{1,0},{2,3},{3,2},{4,5},{5,4},{6,7},{7,6},{8,9},{9,8},{10,11... | collective-permute-start | bytes 786440 | tf_op jit(solution)/shard_map/g_norm1/swap1/ppermute | solution.py:158
  66.4 51.4 %all-to-all-start.2 = ((bf16[4,128,768]{2,1,0:T(8,128)(2,1)}), bf16[4,128,768]{2,1,0:T(8,128)(2,1)S(1)}, u32[]{:S(2)}, u32[]{:S(2)}) async-start(bf16[4,128,768]{2,1,0:T(8,128)(2,1)} %pack3.1), calls=%async_computation.2 | async-start | bytes 1572864 | tf_op jit(solution)/shard_map/t_up/all_to_all | solution.py:166
  72.9 17.7 %collective-permute-start.6 = (bf16[64,2048]{1,0:T(8,128)(2,1)}, bf16[64,2048]{1,0:T(8,128)(2,1)S(1)}, u32[]{:S(2)}, u32[]{:S(2)}) collective-permute-start(bf16[64,2048]{1,0:T(8,128)(2,1)} %collective-permute-done.2.refs_3_), channel_id=1, source_target_pairs={{0,1},{1,0},{2,3},{3,2},{4,5},{5,4},{6,7},{7,6},{8,9},{9,8},{10,11... | collective-permute-start | bytes 786440 | tf_op jit(solution)/shard_map/g_norm1/swap1/ppermute | solution.py:158
  73.2 18.0 %collective-permute-start.11 = (bf16[512,256]{1,0:T(8,128)(2,1)S(1)}, bf16[512,256]{1,0:T(8,128)(2,1)S(1)}, u32[]{:S(2)}, u32[]{:S(2)}) collective-permute-start(bf16[512,256]{1,0:T(8,128)(2,1)S(1)} %get-tuple-element.191.refs_12_.refs_4_), channel_id=1, source_target_pairs={{0,2},{1,3},{2,0},{3,1},{4,6},{5,7},{6,4},{7,5},{8,10},{9,11},{10,... | collective-permute-start | bytes 786440 | tf_op jit(solution)/shard_map/s_kv/swap2/ppermute | solution.py:158
  74.1 20.2 %collective-permute-start.7 = (bf16[512,256]{1,0:T(8,128)(2,1)S(1)}, bf16[512,256]{1,0:T(8,128)(2,1)S(1)}, u32[]{:S(2)}, u32[]{:S(2)}) collective-permute-start(bf16[512,256]{1,0:T(8,128)(2,1)S(1)} %get-tuple-element.192.refs_8_.refs_0_), channel_id=1, source_target_pairs={{0,4},{1,5},{2,6},{3,7},{4,0},{5,1},{6,2},{7,3},{8,12},{9,13},{10,... | collective-permute-start | bytes 786440 | tf_op jit(solution)/shard_map/s_q/swap4/ppermute | solution.py:158
  90.6 20.6 %collective-permute-start.17 = (bf16[512,256]{1,0:T(8,128)(2,1)S(1)}, bf16[512,256]{1,0:T(8,128)(2,1)S(1)}, u32[]{:S(2)}, u32[]{:S(2)}) collective-permute-start(bf16[512,256]{1,0:T(8,128)(2,1)S(1)} %get-tuple-element.190.refs_4_.refs_12_), channel_id=1, source_target_pairs={{0,2},{1,3},{2,0},{3,1},{4,6},{5,7},{6,4},{7,5},{8,10},{9,11},{10,... | collective-permute-start | bytes 786440 | tf_op jit(solution)/shard_map/s_o/swap2/ppermute | solution.py:158
  111.3 22.0 %collective-permute-start.18 = (bf16[512,256]{1,0:T(8,128)(2,1)S(1)}, bf16[512,256]{1,0:T(8,128)(2,1)}, u32[]{:S(2)}, u32[]{:S(2)}) collective-permute-start(bf16[512,256]{1,0:T(8,128)(2,1)S(1)} %collective-permute-done.17.refs_6_.refs_14_), channel_id=1, source_target_pairs={{0,4},{1,5},{2,6},{3,7},{4,0},{5,1},{6,2},{7,3},{8,12},{9,13},{10,... | collective-permute-start | bytes 786440 | tf_op jit(solution)/shard_map/s_o/swap4/ppermute | solution.py:158
  113.3 26.8 %collective-permute-start.13 = (bf16[512,256]{1,0:T(8,128)(2,1)}, bf16[512,256]{1,0:T(8,128)(2,1)}, u32[]{:S(2)}, u32[]{:S(2)}) collective-permute-start(bf16[512,256]{1,0:T(8,128)(2,1)} %get-tuple-element.87.refs_0_.refs_8_), channel_id=1, source_target_pairs={{0,4},{1,5},{2,6},{3,7},{4,0},{5,1},{6,2},{7,3},{8,12},{9,13},{10,... | collective-permute-start | bytes 786440 | tf_op jit(solution)/shard_map/s_keys/swap4/ppermute | solution.py:158
  117.8 26.5 %collective-permute-start.15 = (bf16[512,256]{1,0:T(8,128)(2,1)S(1)}, bf16[512,256]{1,0:T(8,128)(2,1)}, u32[]{:S(2)}, u32[]{:S(2)}) collective-permute-start(bf16[512,256]{1,0:T(8,128)(2,1)S(1)} %collective-permute-done.14.refs_2_.refs_10_), channel_id=1, source_target_pairs={{0,4},{1,5},{2,6},{3,7},{4,0},{5,1},{6,2},{7,3},{8,12},{9,13},{10,... | collective-permute-start | bytes 786440 | tf_op jit(solution)/shard_map/s_keys/swap4/ppermute | solution.py:158
  117.8 58.5 %all-to-all-start.3 = ((bf16[4,768,128]{2,1,0:T(8,128)(2,1)}), bf16[4,768,128]{2,1,0:T(8,128)(2,1)S(1)}, u32[]{:S(2)}, u32[]{:S(2)}) async-start(bf16[4,768,128]{2,1,0:T(8,128)(2,1)} %bitcast.125), calls=%async_computation.3 | async-start | bytes 1572864 | tf_op jit(solution)/shard_map/t_down/all_to_all | solution.py:166
  153.2 20.0 %collective-permute-start.19 = (bf16[2,128,2048]{2,1,0:T(8,128)(2,1)S(1)}, bf16[2,128,2048]{2,1,0:T(8,128)(2,1)S(1)}, u32[]{:S(2)}, u32[]{:S(2)}) collective-permute-start(bf16[2,128,2048]{2,1,0:T(8,128)(2,1)S(1)} %get-tuple-element.90), channel_id=1, source_target_pairs={{0,1},{1,0},{2,3},{3,2},{4,5},{5,4},{6,7},{7,6},{8,9},{9,8},{10,11... | collective-permute-start | bytes 3145736 | tf_op jit(solution)/shard_map/rs1/swap1/ppermute | solution.py:158
  153.2 20.0 %collective-permute-start.20 = (bf16[512,768]{1,0:T(8,128)(2,1)S(1)}, bf16[512,768]{1,0:T(8,128)(2,1)S(1)}, u32[]{:S(2)}, u32[]{:S(2)}) collective-permute-start(bf16[512,768]{1,0:T(8,128)(2,1)S(1)} %bitcast.99), channel_id=1, source_target_pairs={{0,2},{1,3},{2,0},{3,1},{4,6},{5,7},{6,4},{7,5},{8,10},{9,11},{10,... | collective-permute-start | bytes 2359304 | tf_op jit(solution)/shard_map/s_gate/swap2/ppermute | solution.py:158
  154.2 28.4 %collective-permute-start.23 = (bf16[512,768]{1,0:T(8,128)(2,1)S(1)}, bf16[512,768]{1,0:T(8,128)(2,1)}, u32[]{:S(2)}, u32[]{:S(2)}) collective-permute-start(bf16[512,768]{1,0:T(8,128)(2,1)S(1)} %bitcast.100), channel_id=1, source_target_pairs={{0,4},{1,5},{2,6},{3,7},{4,0},{5,1},{6,2},{7,3},{8,12},{9,13},{10,... | collective-permute-start | bytes 2359304 | tf_op jit(solution)/shard_map/s_gate/swap4/ppermute | solution.py:158
  176.3 19.7 %collective-permute-start.34 = (bf16[4,768,128]{2,1,0:T(8,128)(2,1)S(1)}, bf16[4,768,128]{2,1,0:T(8,128)(2,1)S(1)}, u32[]{:S(2)}, u32[]{:S(2)}) collective-permute-start(bf16[4,768,128]{2,1,0:T(8,128)(2,1)S(1)} %all-to-all-done.3.refs_2_.refs_24_.refs_0_), channel_id=1, source_target_pairs={{0,2},{1,3},{2,0},{3,1},{4,6},{5,7},{6,4},{7,5},{8,10},{9,11},{10,... | collective-permute-start | bytes 2359304 | tf_op jit(solution)/shard_map/s_down/swap2/ppermute | solution.py:158
  176.9 20.4 %collective-permute-start.31 = (bf16[512,768]{1,0:T(8,128)(2,1)S(1)}, bf16[512,768]{1,0:T(8,128)(2,1)S(1)}, u32[]{:S(2)}, u32[]{:S(2)}) collective-permute-start(bf16[512,768]{1,0:T(8,128)(2,1)S(1)} %collective-permute-done.20.refs_2_.refs_14_.refs_18_), channel_id=1, source_target_pairs={{0,4},{1,5},{2,6},{3,7},{4,0},{5,1},{6,2},{7,3},{8,12},{9,13},{10,... | collective-permute-start | bytes 2359304 | tf_op jit(solution)/shard_map/s_gate/swap4/ppermute | solution.py:158
  176.9 16.4 %collective-permute-start.21 = (bf16[2,64,2048]{2,1,0:T(8,128)(2,1)}, bf16[2,64,2048]{2,1,0:T(8,128)(2,1)S(1)}, u32[]{:S(2)}, u32[]{:S(2)}) collective-permute-start(bf16[2,64,2048]{2,1,0:T(8,128)(2,1)} %copy-done.94), channel_id=1, source_target_pairs={{0,16},{16,0},{1,17},{17,1},{2,18},{18,2},{3,19},{19,3},{4,20},{20... | collective-permute-start | bytes 1572872 | tf_op jit(solution)/shard_map/rs1/swaptp/ppermute | solution.py:162
  182.6 37.2 %collective-permute-start.32 = (bf16[512,768]{1,0:T(8,128)(2,1)S(1)}, bf16[512,768]{1,0:T(8,128)(2,1)S(1)}, u32[]{:S(2)}, u32[]{:S(2)}) collective-permute-start(bf16[512,768]{1,0:T(8,128)(2,1)S(1)} %bitcast.104), channel_id=1, source_target_pairs={{0,4},{1,5},{2,6},{3,7},{4,0},{5,1},{6,2},{7,3},{8,12},{9,13},{10,... | collective-permute-start | bytes 2359304 | tf_op jit(solution)/shard_map/s_up/swap4/ppermute | solution.py:158
  193.3 44.6 %collective-permute-start.33 = (bf16[4,768,128]{2,1,0:T(8,128)(2,1)S(1)}, bf16[4,768,128]{2,1,0:T(8,128)(2,1)S(1)}, u32[]{:S(2)}, u32[]{:S(2)}) collective-permute-start(bf16[4,768,128]{2,1,0:T(8,128)(2,1)S(1)} %all-to-all-done.3.refs_2_.refs_24_.refs_0_), channel_id=1, source_target_pairs={{0,4},{1,5},{2,6},{3,7},{4,0},{5,1},{6,2},{7,3},{8,12},{9,13},{10,... | collective-permute-start | bytes 2359304 | tf_op jit(solution)/shard_map/s_down/swap4/ppermute | solution.py:158
  194.5 39.6 %collective-permute-start.24 = (bf16[2,32,2048]{2,1,0:T(8,128)(2,1)S(1)}, bf16[2,32,2048]{2,1,0:T(8,128)(2,1)S(1)}, u32[]{:S(2)}, u32[]{:S(2)}) collective-permute-start(bf16[2,32,2048]{2,1,0:T(8,128)(2,1)S(1)} %get-tuple-element.95), channel_id=1, source_target_pairs={{0,8},{1,9},{2,10},{3,11},{4,12},{5,13},{6,14},{7,15},{8,0},{9,1},... | collective-permute-start | bytes 786440 | tf_op jit(solution)/shard_map/rs1/swap8/ppermute | solution.py:158
  196.0 62.0 %collective-permute-start.35 = (bf16[4,768,128]{2,1,0:T(8,128)(2,1)S(1)}, bf16[4,768,128]{2,1,0:T(8,128)(2,1)S(1)}, u32[]{:S(2)}, u32[]{:S(2)}) collective-permute-start(bf16[4,768,128]{2,1,0:T(8,128)(2,1)S(1)} %collective-permute-done.34.refs_26_.refs_2_), channel_id=1, source_target_pairs={{0,4},{1,5},{2,6},{3,7},{4,0},{5,1},{6,2},{7,3},{8,12},{9,13},{10,... | collective-permute-start | bytes 2359304 | tf_op jit(solution)/shard_map/s_down/swap4/ppermute | solution.py:158
  197.3 60.7 %collective-permute-start.43 = (bf16[512,768]{1,0:T(8,128)(2,1)S(1)}, bf16[512,768]{1,0:T(8,128)(2,1)S(1)}, u32[]{:S(2)}, u32[]{:S(2)}) collective-permute-start(bf16[512,768]{1,0:T(8,128)(2,1)S(1)} %bitcast.105), channel_id=1, source_target_pairs={{0,2},{1,3},{2,0},{3,1},{4,6},{5,7},{6,4},{7,5},{8,10},{9,11},{10,... | collective-permute-start | bytes 2359304 | tf_op jit(solution)/shard_map/s_up/swap2/ppermute | solution.py:158
  219.8 43.6 %collective-permute-start.44 = (bf16[512,768]{1,0:T(8,128)(2,1)S(1)}, bf16[512,768]{1,0:T(8,128)(2,1)S(1)}, u32[]{:S(2)}, u32[]{:S(2)}) collective-permute-start(bf16[512,768]{1,0:T(8,128)(2,1)S(1)} %collective-permute-done.32.refs_16_.refs_21_), channel_id=1, source_target_pairs={{0,2},{1,3},{2,0},{3,1},{4,6},{5,7},{6,4},{7,5},{8,10},{9,11},{10,... | collective-permute-start | bytes 2359304 | tf_op jit(solution)/shard_map/s_up/swap2/ppermute | solution.py:158
  234.4 21.4 %collective-permute-start.36 = (bf16[64,2048]{1,0:T(8,128)(2,1)S(1)}, bf16[64,2048]{1,0:T(8,128)(2,1)S(1)}, u32[]{:S(2)}, u32[]{:S(2)}) collective-permute-start(bf16[64,2048]{1,0:T(8,128)(2,1)S(1)} %get-tuple-element.98.refs_0_), channel_id=1, source_target_pairs={{0,8},{1,9},{2,10},{3,11},{4,12},{5,13},{6,14},{7,15},{8,0},{9,1},... | collective-permute-start | bytes 786440 | tf_op jit(solution)/shard_map/g_norm2/swap8/ppermute | solution.py:158
  237.9 20.6 %collective-permute-start.37 = (bf16[64,2048]{1,0:T(8,128)(2,1)S(1)}, bf16[64,2048]{1,0:T(8,128)(2,1)S(1)}, u32[]{:S(2)}, u32[]{:S(2)}) collective-permute-start(bf16[64,2048]{1,0:T(8,128)(2,1)S(1)} %get-tuple-element.98.refs_0_), channel_id=1, source_target_pairs={{0,16},{16,0},{1,17},{17,1},{2,18},{18,2},{3,19},{19,3},{4,20},{20... | collective-permute-start | bytes 786440 | tf_op jit(solution)/shard_map/g_norm2/swaptp/ppermute | solution.py:162
  280.6 18.7 %collective-permute-start.48 = (bf16[2,128,2048]{2,1,0:T(8,128)(2,1)}, bf16[2,128,2048]{2,1,0:T(8,128)(2,1)S(1)}, u32[]{:S(2)}, u32[]{:S(2)}) collective-permute-start(bf16[2,128,2048]{2,1,0:T(8,128)(2,1)} %get-tuple-element.107), channel_id=1, source_target_pairs={{0,1},{1,0},{2,3},{3,2},{4,5},{5,4},{6,7},{7,6},{8,9},{9,8},{10,11... | collective-permute-start | bytes 3145736 | tf_op jit(solution)/shard_map/rs2/swap1/ppermute | solution.py:158
  286.4 57.4 %collective-permute-start.75 = (bf16[2,4,768,128]{3,2,1,0:T(8,128)(2,1)}, bf16[2,4,768,128]{3,2,1,0:T(8,128)(2,1)S(1)}, u32[]{:S(2)}, u32[]{:S(2)}) collective-permute-start(bf16[2,4,768,128]{3,2,1,0:T(8,128)(2,1)} %get-tuple-element.152), channel_id=1, source_target_pairs={{0,2},{1,3},{2,0},{3,1},{4,6},{5,7},{6,4},{7,5},{8,10},{9,11},{10,... | collective-permute-start | bytes 4718600 | tf_op jit(solution)/shard_map/r_down/swap2/ppermute | solution.py:158
  294.5 62.5 %collective-permute-start.71 = (bf16[2,512,768]{2,1,0:T(8,128)(2,1)S(1)}, bf16[2,512,768]{2,1,0:T(8,128)(2,1)S(1)}, u32[]{:S(2)}, u32[]{:S(2)}) collective-permute-start(bf16[2,512,768]{2,1,0:T(8,128)(2,1)S(1)} %get-tuple-element.147), channel_id=1, source_target_pairs={{0,2},{1,3},{2,0},{3,1},{4,6},{5,7},{6,4},{7,5},{8,10},{9,11},{10,... | collective-permute-start | bytes 4718600 | tf_op jit(solution)/shard_map/r_gate/swap2/ppermute | solution.py:158
  297.0 18.3 %collective-permute-start.45 = (bf16[2,128,2048]{2,1,0:T(8,128)(2,1)S(1)}, bf16[2,128,2048]{2,1,0:T(8,128)(2,1)S(1)}, u32[]{:S(2)}, u32[]{:S(2)}) collective-permute-start(bf16[2,128,2048]{2,1,0:T(8,128)(2,1)S(1)} %get-tuple-element.101), channel_id=1, source_target_pairs={{0,1},{1,0},{2,3},{3,2},{4,5},{5,4},{6,7},{7,6},{8,9},{9,8},{10,11... | collective-permute-start | bytes 3145736 | tf_op jit(solution)/shard_map/rs3/swap1/ppermute | solution.py:158
  297.1 63.4 %collective-permute-start.73 = (bf16[2,512,768]{2,1,0:T(8,128)(2,1)S(1)}, bf16[2,512,768]{2,1,0:T(8,128)(2,1)S(1)}, u32[]{:S(2)}, u32[]{:S(2)}) collective-permute-start(bf16[2,512,768]{2,1,0:T(8,128)(2,1)S(1)} %copy-done.109), channel_id=1, source_target_pairs={{0,4},{1,5},{2,6},{3,7},{4,0},{5,1},{6,2},{7,3},{8,12},{9,13},{10,... | collective-permute-start | bytes 4718600 | tf_op jit(solution)/shard_map/r_up/swap4/ppermute | solution.py:158
  313.7 25.4 %collective-permute-start.50 = (bf16[2,32,2048]{2,1,0:T(8,128)(2,1)S(1)}, bf16[2,32,2048]{2,1,0:T(8,128)(2,1)S(1)}, u32[]{:S(2)}, u32[]{:S(2)}) collective-permute-start(bf16[2,32,2048]{2,1,0:T(8,128)(2,1)S(1)} %get-tuple-element.111), channel_id=1, source_target_pairs={{0,8},{1,9},{2,10},{3,11},{4,12},{5,13},{6,14},{7,15},{8,0},{9,1},... | collective-permute-start | bytes 786440 | tf_op jit(solution)/shard_map/rs2/swap8/ppermute | solution.py:158
  315.5 44.9 %collective-permute-start.46 = (bf16[2,64,2048]{2,1,0:T(8,128)(2,1)S(1)}, bf16[2,64,2048]{2,1,0:T(8,128)(2,1)S(1)}, u32[]{:S(2)}, u32[]{:S(2)}) collective-permute-start(bf16[2,64,2048]{2,1,0:T(8,128)(2,1)S(1)} %get-tuple-element.103), channel_id=1, source_target_pairs={{0,16},{16,0},{1,17},{17,1},{2,18},{18,2},{3,19},{19,3},{4,20},{20... | collective-permute-start | bytes 1572872 | tf_op jit(solution)/shard_map/rs3/swaptp/ppermute | solution.py:162
  340.4 18.1 %collective-permute-start.51 = (bf16[64,2048]{1,0:T(8,128)(2,1)S(1)}, bf16[64,2048]{1,0:T(8,128)(2,1)S(1)}, u32[]{:S(2)}, u32[]{:S(2)}) collective-permute-start(bf16[64,2048]{1,0:T(8,128)(2,1)S(1)} %get-tuple-element.112.refs_0_), channel_id=1, source_target_pairs={{0,8},{1,9},{2,10},{3,11},{4,12},{5,13},{6,14},{7,15},{8,0},{9,1},... | collective-permute-start | bytes 786440 | tf_op jit(solution)/shard_map/g_branch/swap8/ppermute | solution.py:158
  344.3 46.8 %collective-permute-start.76 = (bf16[1,4,768,128]{3,2,1,0:T(8,128)(2,1)S(1)}, bf16[1,4,768,128]{3,2,1,0:T(8,128)(2,1)}, u32[]{:S(2)}, u32[]{:S(2)}) collective-permute-start(bf16[1,4,768,128]{3,2,1,0:T(8,128)(2,1)S(1)} %slice.242), channel_id=1, source_target_pairs={{0,4},{1,5},{2,6},{3,7},{4,0},{5,1},{6,2},{7,3},{8,12},{9,13},{10,... | collective-permute-start | bytes 2359304 | tf_op jit(solution)/shard_map/r_down/swap4/ppermute | solution.py:158
  360.5 16.8 %collective-permute-start.55 = (bf16[64,2048]{1,0:T(8,128)(2,1)S(1)}, bf16[64,2048]{1,0:T(8,128)(2,1)S(1)}, u32[]{:S(2)}, u32[]{:S(2)}) collective-permute-start(bf16[64,2048]{1,0:T(8,128)(2,1)S(1)} %collective-permute-done.51.refs_1_), channel_id=1, source_target_pairs={{0,1},{1,0},{2,3},{3,2},{4,5},{5,4},{6,7},{7,6},{8,9},{9,8},{10,11... | collective-permute-start | bytes 786440 | tf_op jit(solution)/shard_map/g_branch/swap1/ppermute | solution.py:158
  373.8 55.7 %collective-permute-start.47 = (bf16[2,32,2048]{2,1,0:T(8,128)(2,1)}, bf16[2,32,2048]{2,1,0:T(8,128)(2,1)}, u32[]{:S(2)}, u32[]{:S(2)}) collective-permute-start(bf16[2,32,2048]{2,1,0:T(8,128)(2,1)} %get-tuple-element.105), channel_id=1, source_target_pairs={{0,8},{1,9},{2,10},{3,11},{4,12},{5,13},{6,14},{7,15},{8,0},{9,1},... | collective-permute-start | bytes 786440 | tf_op jit(solution)/shard_map/rs3/swap8/ppermute | solution.py:158
  377.2 89.9 %collective-permute-start.72 = (bf16[1,512,768]{2,1,0:T(8,128)(2,1)}, bf16[1,512,768]{2,1,0:T(8,128)(2,1)}, u32[]{:S(2)}, u32[]{:S(2)}) collective-permute-start(bf16[1,512,768]{2,1,0:T(8,128)(2,1)} %slice.230), channel_id=1, source_target_pairs={{0,4},{1,5},{2,6},{3,7},{4,0},{5,1},{6,2},{7,3},{8,12},{9,13},{10,... | collective-permute-start | bytes 2359304 | tf_op jit(solution)/shard_map/r_gate/swap4/ppermute | solution.py:158
  377.2 91.5 %collective-permute-start.74 = (bf16[1,512,768]{2,1,0:T(8,128)(2,1)}, bf16[1,512,768]{2,1,0:T(8,128)(2,1)}, u32[]{:S(2)}, u32[]{:S(2)}) collective-permute-start(bf16[1,512,768]{2,1,0:T(8,128)(2,1)} %slice.232), channel_id=1, source_target_pairs={{0,2},{1,3},{2,0},{3,1},{4,6},{5,7},{6,4},{7,5},{8,10},{9,11},{10,... | collective-permute-start | bytes 2359304 | tf_op jit(solution)/shard_map/r_up/swap2/ppermute | solution.py:158
  391.0 20.6 %collective-permute-start.60 = (bf16[2,512,128]{2,1,0:T(8,128)(2,1)}, bf16[2,512,128]{2,1,0:T(8,128)(2,1)}, u32[]{:S(2)}, u32[]{:S(2)}) collective-permute-start(bf16[2,512,128]{2,1,0:T(8,128)(2,1)} %get-tuple-element.120), channel_id=1, source_target_pairs={{0,4},{1,5},{2,6},{3,7},{4,0},{5,1},{6,2},{7,3},{8,12},{9,13},{10,... | collective-permute-start | bytes 786440 | tf_op jit(solution)/shard_map/r_v/swap4/ppermute | solution.py:158
  395.2 54.6 %all-to-all-start.7 = ((bf16[4,768,128]{2,1,0:T(8,128)(2,1)}), bf16[4,768,128]{2,1,0:T(8,128)(2,1)}, u32[]{:S(2)}, u32[]{:S(2)}) async-start(bf16[4,768,128]{2,1,0:T(8,128)(2,1)} %fusion), calls=%async_computation.7 | async-start | bytes 1572864 | tf_op jit(solution)/shard_map/t_ddown/all_to_all | solution.py:166
  402.9 30.8 %collective-permute-start.69 = (bf16[2,4,256,128]{3,2,1,0:T(8,128)(2,1)S(1)}, bf16[2,4,256,128]{3,2,1,0:T(8,128)(2,1)S(1)}, u32[]{:S(2)}, u32[]{:S(2)}) collective-permute-start(bf16[2,4,256,128]{3,2,1,0:T(8,128)(2,1)S(1)} %get-tuple-element.142), channel_id=1, source_target_pairs={{0,2},{1,3},{2,0},{3,1},{4,6},{5,7},{6,4},{7,5},{8,10},{9,11},{10,... | collective-permute-start | bytes 1572872 | tf_op jit(solution)/shard_map/r_out/swap2/ppermute | solution.py:158
  433.7 53.5 %collective-permute-start.62 = (bf16[2,128,2048]{2,1,0:T(8,128)(2,1)}, bf16[2,128,2048]{2,1,0:T(8,128)(2,1)S(1)}, u32[]{:S(2)}, u32[]{:S(2)}) collective-permute-start(bf16[2,128,2048]{2,1,0:T(8,128)(2,1)} %get-tuple-element.124), channel_id=1, source_target_pairs={{0,1},{1,0},{2,3},{3,2},{4,5},{5,4},{6,7},{7,6},{8,9},{9,8},{10,11... | collective-permute-start | bytes 3145736 | tf_op jit(solution)/shard_map/rs4/swap1/ppermute | solution.py:158
  462.9 18.0 %all-to-all-start.4 = ((bf16[4,128,512]{2,1,0:T(8,128)(2,1)}), bf16[4,128,512]{2,1,0:T(8,128)(2,1)}, u32[]{:S(2)}, u32[]{:S(2)}) async-start(bf16[4,128,512]{2,1,0:T(8,128)(2,1)} %pad_maximum_fusion.3), calls=%async_computation.4 | async-start | bytes 1048576 | tf_op jit(solution)/shard_map/t_dqkv/all_to_all | solution.py:166
  480.9 54.0 %all-to-all-start.6 = ((bf16[4,128,1536]{2,1,0:T(8,128)(2,1)}), bf16[4,128,1536]{2,1,0:T(8,128)(2,1)}, u32[]{:S(2)}, u32[]{:S(2)}) async-start(bf16[4,128,1536]{2,1,0:T(8,128)(2,1)} %pad_maximum_fusion), calls=%async_computation.6 | async-start | bytes 3145728 | tf_op jit(solution)/shard_map/t_dgu/all_to_all | solution.py:166
  501.9 29.8 %collective-permute-start.64 = (bf16[2,32,2048]{2,1,0:T(8,128)(2,1)S(1)}, bf16[2,32,2048]{2,1,0:T(8,128)(2,1)S(1)}, u32[]{:S(2)}, u32[]{:S(2)}) collective-permute-start(bf16[2,32,2048]{2,1,0:T(8,128)(2,1)S(1)} %get-tuple-element.128), channel_id=1, source_target_pairs={{0,8},{1,9},{2,10},{3,11},{4,12},{5,13},{6,14},{7,15},{8,0},{9,1},... | collective-permute-start | bytes 786440 | tf_op jit(solution)/shard_map/rs4/swap8/ppermute | solution.py:158
  (152 other events, 2159.4 us)

commit v3 on v2

--- a/solution.py
+++ b/solution.py
@@ -42,27 +42,96 @@
     return (jnp.cos(angles), jnp.sin(angles))
 
 
-def call(body, name, outs, ins, ties=(), scratch=(), limit=32, specs=None):
-    ins, ties = list(ins), list(ties)
-    count = len(ins)
+LARGE = {
+    "enter",
+    "pack1",
+    "project",
+    "attend",
+    "feed",
+    "feed_out",
+    "attend_back",
+    "project_back",
+    "w_down",
+    "w_gate_up",
+    "w_out",
+    "w_qkv",
+}
+
+
+def call(body, name, outs, ins, ties=(), scratch=(), scalars=(), staged=False):
+    scalars, ins, ties = list(scalars), list(ins), list(ties)
+    if name not in LARGE:
+        skip = len(scalars) + len(ins)
+        return pl.pallas_call(
+            lambda *refs: body(*refs[:skip], *refs[skip + len(ties) :]),
+            out_shape=[jax.ShapeDtypeStruct(s, d) for s, d in outs],
+            in_specs=[pl.BlockSpec(memory_space=pltpu.SMEM)] * len(scalars)
+            + [pl.BlockSpec(memory_space=pltpu.VMEM)] * len(ins)
+            + [pl.BlockSpec(memory_space=pl.ANY)] * len(ties),
+            out_specs=[pl.BlockSpec(memory_space=pltpu.VMEM)] * len(outs),
+            scratch_shapes=list(scratch),
+            compiler_params=pltpu.CompilerParams(vmem_limit_bytes=16 * MIB),
+            cost_estimate=pl.CostEstimate(flops=0, bytes_accessed=0, transcendentals=0),
+            name=name,
+        )(*scalars, *ins, *ties)
+    begin, end = len(scalars), len(scalars) + len(ins)
+    n_in, n_out = len(ins), len(outs)
 
     def kernel(*refs):
-        body(*refs[:count], *refs[count + len(ties) :])
-
-    in_specs = [pl.BlockSpec(memory_space=pltpu.VMEM)] * count
-    for at, spec in (specs or {}).items():
-        in_specs[at] = spec
+        scalar_refs, in_refs = refs[:begin], refs[begin:end]
+        rest = refs[end + len(ties) :]
+        out_refs, rest = rest[:n_out], rest[n_out:]
+        in_vmem, out_vmem, rest = rest[:n_in], rest[n_in : n_in + n_out], rest[n_in + n_out :]
+        sems, rest = rest[0], rest[1:]
+        loads = [
+            pltpu.make_async_copy(in_refs[n], in_vmem[n], sems.at[n]) for n in range(n_in)
+        ]
+        stores = [
+            pltpu.make_async_copy(out_vmem[n], out_refs[n], sems.at[n_in + n])
+            for n in range(n_out)
+        ]
+        for load in loads:
+            load.start()
+        waited, sent = set(), set()
+
+        def ready(n):
+            if n not in waited:
+                waited.add(n)
+                loads[n].wait()
+
+        def flush(n):
+            if n not in sent:
+                sent.add(n)
+                stores[n].start()
+
+        if staged:
+            body(ready, flush, *scalar_refs, *in_vmem, *out_vmem, *rest)
+        else:
+            for n in range(n_in):
+                ready(n)
+            body(*scalar_refs, *in_vmem, *out_vmem, *rest)
+        for n in range(n_in):
+            ready(n)
+        for n in range(n_out):
+            flush(n)
+        for store in stores:
+            store.wait()
+
+    anywhere = pl.BlockSpec(memory_space=pl.ANY)
     return pl.pallas_call(
         kernel,
-        grid=(1,) if specs else (),
         out_shape=[jax.ShapeDtypeStruct(s, d) for s, d in outs],
-        in_specs=in_specs + [pl.BlockSpec(memory_space=pl.ANY)] * len(ties),
-        out_specs=[pl.BlockSpec(memory_space=pltpu.VMEM)] * len(outs),
-        scratch_shapes=list(scratch),
-        compiler_params=pltpu.CompilerParams(vmem_limit_bytes=limit * MIB),
+        in_specs=[pl.BlockSpec(memory_space=pltpu.SMEM)] * begin
+        + [anywhere] * (n_in + len(ties)),
+        out_specs=[anywhere] * n_out,
+        scratch_shapes=[pltpu.VMEM(v.shape, v.dtype) for v in ins]
+        + [pltpu.VMEM(s, d) for s, d in outs]
+        + [pltpu.SemaphoreType.DMA((n_in + n_out,))]
+        + list(scratch),
+        compiler_params=pltpu.CompilerParams(vmem_limit_bytes=60 * MIB),
         cost_estimate=pl.CostEstimate(flops=0, bytes_accessed=0, transcendentals=0),
         name=name,
-    )(*ins, *ties)
+    )(*scalars, *ins, *ties)
 
 
 def rms(value):
@@ -211,18 +280,8 @@
         [query_weight, key_matrix, value_matrix, output_weight],
     )
     wide_shape = ((4, piece, wide_f), BF)
+    first_packed = packed
     first = trade(packed, "t_first").reshape(chunk, wide_1)
-    (packed,) = call(pack_columns, "pack2", [wide_shape], [gate_weight])
-    gate = trade(packed, "t_gate").reshape(chunk, wide_f)
-    (packed,) = call(pack_columns, "pack3", [wide_shape], [up_weight], ties=[gate])
-    up = trade(packed, "t_up").reshape(chunk, wide_f)
-    down = trade(down_weight.reshape(4, wide_f, piece), "t_down")
-    q_parts = spread(first[:, :wide_q], near, "s_q")
-    kv_parts = spread(first[:, wide_q : wide_q + wide_k], far, "s_kv")
-    o_parts = spread(first[:, wide_q + wide_k :], near, "s_o")
-    gate_parts = spread(gate, near, "s_gate")
-    up_parts = spread(up, far, "s_up")
-    down_parts = spread(down, near, "s_down")
 
     def gather_rows(value, name):
         held = [value]
@@ -276,7 +335,6 @@
 
     gain_q, gain_k = query_gain[None], key_gain[None]
     row_mask = ways - 1 - CORE - SPLIT
-    where_spec = pl.BlockSpec(memory_space=pltpu.SMEM)
     where = (place & row_mask)[None]
 
     def lanes_of(where_ref, n):
@@ -305,13 +363,13 @@
                 (own_shape, BF),
             ],
             [
-                where,
                 layer_input.reshape(own_shape),
                 cotangent.reshape(own_shape),
                 attn_gain[None],
                 mlp_gain[None],
             ],
-            specs={0: where_spec},
+            scalars=[where],
+            ties=[first_packed],
         )
     else:
         x_own = to_local(layer_input.reshape(own_shape))
@@ -325,7 +383,7 @@
 
         (normed,) = call(first_norm, "norm1", [(own_shape, BF)], [x_own, gain_a])
 
-    def put_back(values, name):
+    def put_back(values, name, ties=()):
         if piece % 128:
             return [from_local(v) for v in values]
 
@@ -336,9 +394,20 @@
                     out_ref[:, lanes_of(where_ref, n)] = in_ref[:, n * piece : (n + 1) * piece]
 
         outs = [(v.shape, v.dtype) for v in values]
-        return call(body, name, outs, [where, *values], specs={0: where_spec})
+        return call(body, name, outs, values, scalars=[where], ties=ties)
 
     normed_parts = gather_rows(normed, "g_norm1")
+    (packed,) = call(pack_columns, "pack2", [wide_shape], [gate_weight], ties=[first, normed_parts[1]])
+    gate = trade(packed, "t_gate").reshape(chunk, wide_f)
+    (packed,) = call(pack_columns, "pack3", [wide_shape], [up_weight], ties=[gate])
+    up = trade(packed, "t_up").reshape(chunk, wide_f)
+    down = trade(down_weight.reshape(4, wide_f, piece), "t_down")
+    q_parts = spread(first[:, :wide_q], near, "s_q")
+    kv_parts = spread(first[:, wide_q : wide_q + wide_k], far, "s_kv")
+    o_parts = spread(first[:, wide_q + wide_k :], near, "s_o")
+    gate_parts = spread(gate, near, "s_gate")
+    up_parts = spread(up, far, "s_up")
+    down_parts = spread(down, near, "s_down")
     c_parts = gather_rows(c_own, "g_cot")
 
     def project(*refs):
@@ -452,7 +521,6 @@
             pltpu.VMEM((segments * groups, block, 2 * HEAD_SIZE), BF),
             pltpu.VMEM((wide_q, width), BF),
         ],
-        limit=40,
     )
     kept, got = scatter_rows(
         sent, kept, "rs1", [gate_parts[slot[near[0]]]], [down, c_parts[1], gate_parts[slot[far[0]]]]
@@ -526,11 +594,10 @@
         ],
         [*normed2_parts, *c_parts, *gate_parts, *up_parts, *down_parts],
         scratch=[pltpu.VMEM((wide_f, width), BF)],
-        limit=52,
     )
     kept, got = scatter_rows(sent, kept, "rs2")
 
-    def grad_in(x_all, grads, orders, name):
+    def grad_in(x_all, grads, orders, name, ties=()):
         lists = [mix_list(order) for order in orders]
 
         def body(*refs):
@@ -547,7 +614,7 @@
         outs = []
         for g in grads:
             outs += [((groups // 2, chunk, g.shape[1]), BF)] * 2
-        return call(body, name, outs, [x_all, *grads], limit=48)
+        return call(body, name, outs, [x_all, *grads], ties=ties)
 
     def grad_out(left, c_value, order, name):
         mix = mix_list(order)
@@ -567,33 +634,43 @@
                         sent_ref[at - groups // 2, n] = part
 
         return call(
-            body, name, [((groups // 2, 4, tall, piece), BF)] * 2, [left, c_value], limit=48
+            body, name, [((groups // 2, 4, tall, piece), BF)] * 2, [left, c_value]
         )
 
-    def reduce_groups(sent, kept, order, name):
+    def reduce_to_pair(sent, kept, order, name):
         with jax.named_scope(name):
             for bit in order[:-1]:
                 total = kept.astype(F32) + swap(sent, bit).astype(F32)
                 count = total.shape[0] // 2
                 kept, sent = total[:count].astype(BF), total[count:].astype(BF)
-            return (kept.astype(F32) + swap(sent, order[-1]).astype(F32))[0]
-
-    down_sums = reduce_groups(*grad_out(active, c_all, near, "w_down"), near, "r_down")
+            return kept, swap(sent, order[-1])
+
+    def reduce_groups(sent, kept, order, name):
+        kept, got = reduce_to_pair(sent, kept, order, name)
+        return (kept.astype(F32) + got.astype(F32))[0]
+
+    def add_joined(pairs, name, ties):
+        shape = pairs[0][0].shape[1:]
+        wide = [kept.shape[-1] for kept, _ in pairs]
+
+        def body(*refs):
+            at = 0
+            for n in range(len(pairs)):
+                value = refs[2 * n][0].astype(F32) + refs[2 * n + 1][0].astype(F32)
+                refs[-1][..., at : at + wide[n]] = value.astype(BF)
+                at += wide[n]
+
+        ins = [v for pair in pairs for v in pair]
+        return call(body, name, [((*shape[:-1], sum(wide)), BF)], ins, ties=ties)[0]
+
+    down_sent, down_kept = grad_out(active, c_all, near, "w_down")
+    down_sums = reduce_groups(down_sent, down_kept, near, "r_down")
     gate_sent, gate_kept, up_sent, up_kept = grad_in(
         normed2_all, [d_gate, d_upper], [near, far], "w_gate_up"
     )
-    gate_sums = reduce_groups(gate_sent, gate_kept, near, "r_gate")
-    up_sums = reduce_groups(up_sent, up_kept, far, "r_up")
+    gate_pair = reduce_to_pair(gate_sent, gate_kept, near, "r_gate")
+    up_pair = reduce_to_pair(up_sent, up_kept, far, "r_up")
     down_grad = trade(down_sums.astype(BF), "t_ddown").astype(F32).reshape(4 * wide_f, piece)
-    gate_up = jnp.concatenate([gate_sums, up_sums], axis=1).astype(BF)
-    gate_up = trade(gate_up.reshape(4, piece, 2 * wide_f), "t_dgu").astype(F32)
-
-    def join(value, start, stop):
-        return jnp.concatenate([value[n, :, start:stop] for n in range(4)], axis=1)
-
-    gate_grad = join(gate_up, 0, wide_f)
-    up_grad = join(gate_up, wide_f, 2 * wide_f)
-
     def norm_step_back(kept_ref, got_ref, mid_ref, gain_ref, c_ref, d_ref, low_ref, gain_out):
         grad = kept_ref[...].astype(F32) + got_ref[...].astype(F32)
         back, gain_grad = norm_back(grad, mid_ref[...], gain_ref[...])
@@ -607,6 +684,7 @@
         "norm2_back",
         [((own, width), F32), ((own, width), BF), ((1, width), F32)],
         [kept, got, middle, gain_m, c_own],
+        ties=[gate_sent, down_sent],
     )
     d_parts = gather_rows(d_branch, "g_branch")
 
@@ -629,9 +707,9 @@
         ties=[],
         scratch=[pltpu.VMEM((wide_f, width), BF)],
     )
-    out_kept, out_got = scatter_rows(out_sent, out_kept, "rs3")
-    layer_output = (middle + (out_kept.astype(F32) + out_got.astype(F32))).astype(BF)
-    layer_output = put_back([layer_output], "leave1")[0].reshape(layer_input.shape)
+    with jax.named_scope("rs3"):
+        out_sent, out_kept = add_split(out_kept, swap(out_sent, CORE), "rs3_c")
+        out_got = swap_tp(out_sent)
 
     key_mix, value_mix = mix_list(near), mix_list(far)
 
@@ -654,10 +732,13 @@
             k_kept,
             v_sent,
             v_kept,
+            o_sent,
+            o_kept,
             keys,
             w_out,
             sums,
         ) = refs[8 + 2 * groups :]
+        out_mix = mix_list(near)
         assemble(parts, d_all_ref, segments, rows)
         load_keys(kv_refs, keys)
         load_out_weight(wo, w_out)
@@ -716,9 +797,20 @@
                         kept_ref[n, rows_at, :] = value
                     else:
                         sent_ref[n - groups // 2, rows_at, :] = value
+        heads = out_ref[...].astype(BF)
+        for n, which in enumerate(out_mix):
+            j = slot[which]
+            value = dot_tn(heads, d_all_ref[:, j * chunk : (j + 1) * chunk]).astype(BF)
+            for f in range(4):
+                part = value[:, f * piece : (f + 1) * piece]
+                if n < groups // 2:
+                    o_kept[n, f] = part
+                else:
+                    o_sent[n - groups // 2, f] = part
 
     part_shape = ((groups // 2, all_rows, HEAD_SIZE), BF)
-    d_all, d_q, d_gain_q, k_sent, k_kept, v_sent, v_kept = call(
+    o_shape = ((groups // 2, 4, wide_q, piece), BF)
+    d_all, d_q, d_gain_q, k_sent, k_kept, v_sent, v_kept, o_sent, o_kept = call(
         attend_back,
         "attend_back",
         [
@@ -729,6 +821,8 @@
             part_shape,
             part_shape,
             part_shape,
+            o_shape,
+            o_shape,
         ],
         [
             *d_parts,
@@ -744,19 +838,25 @@
             sine,
             gain_q,
         ],
+        ties=[out_sent],
         scratch=[
             pltpu.VMEM((segments * groups, block, 2 * HEAD_SIZE), BF),
             pltpu.VMEM((wide_q, width), BF),
             pltpu.VMEM((segments * groups, block, 2 * HEAD_SIZE), F32),
         ],
-        limit=52,
-    )
-
-    out_sums = reduce_groups(*grad_out(attended, d_all, near, "w_out"), near, "r_out")
-    output_grad = trade(out_sums.astype(BF), "t_dout").astype(F32).reshape(4 * wide_q, piece)
-
+    )
+
+    out_pair = reduce_to_pair(o_sent, o_kept, near, "r_out")
+
+    with jax.named_scope("rs3"):
+        out_sent, out_kept = add_split(out_kept, out_got, "rs3_t", [k_sent])
+        out_kept, out_got = out_kept.reshape(own, width), swap(out_sent, SPLIT)
+        out_got = out_got.reshape(own, width)
     d_keys = reduce_groups(k_sent, k_kept, near, "r_k")
     d_values = reduce_groups(v_sent, v_kept, far, "r_v")
+
+    gate_up_sums = add_joined([gate_pair, up_pair], "sum_gu", [k_sent])
+    gate_up = trade(gate_up_sums.reshape(4, piece, 2 * wide_f), "t_dgu")
 
     def key_back(dk_ref, dv_ref, raw_ref, cos_ref, sin_ref, gain_ref, out_ref, gain_out):
         d_raw, d_gain = rope_back(
@@ -771,52 +871,90 @@
         "key_back",
         [((all_rows, 2 * HEAD_SIZE), BF), ((1, HEAD_SIZE), F32)],
         [d_keys, d_values, k_raw, cosine, sine, gain_k],
+        ties=[o_sent, out_sent, gate_up_sums],
     )
 
     def project_back(*refs):
         wq, wkv, refs = refs[:groups], refs[groups : 2 * groups], refs[2 * groups :]
-        dq_ref, dkv_ref, sent_ref, kept_ref = refs
-        for s in range(segments):
-            at = slice(s * block, (s + 1) * block)
-            for j in range(groups):
+        dq_ref, dkv_ref, x_ref, gain_ref, sent_ref, kept_ref, gain_out, *outs = refs
+        for n, (g_ref, order) in enumerate(((dq_ref, near), (dkv_ref, far))):
+            for at, which in enumerate(mix_list(order)):
+                j = slot[which]
+                value = dot_tn(x_ref[:, j * chunk : (j + 1) * chunk], g_ref[...]).astype(BF)
+                if at < groups // 2:
+                    outs[2 * n + 1][at] = value
+                else:
+                    outs[2 * n][at - groups // 2] = value
+        for j in range(groups):
+            lanes = slice(j * chunk, (j + 1) * chunk)
+            gain_sum = jnp.zeros((1, chunk), F32)
+            for s in range(segments):
+                at = slice(s * block, (s + 1) * block)
                 value = dot_nt(dq_ref[at, :], wq[j][...]) + dot_nt(dkv_ref[at, :], wkv[j][...])
                 store_pair(sent_ref, kept_ref, s, value, j * chunk)
-
-    sent, kept = call(
-        project_back, "project_back", pair, [*q_parts, *kv_parts, d_q, d_kv]
-    )
-    kept, got = scatter_rows(sent, kept, "rs4")
-
-    q_sent, q_kept, kv_sent, kv_kept = grad_in(
-        normed_all, [d_q, d_kv], [near, far], "w_qkv"
-    )
-    q_sums = reduce_groups(q_sent, q_kept, near, "r_q")
-    kv_sums = reduce_groups(kv_sent, kv_kept, far, "r_kv")
-    qkv_sums = jnp.concatenate([q_sums, kv_sums], axis=1).astype(BF)
+                gain_sum = gain_sum + jnp.sum(
+                    value * x_ref[at, lanes].astype(F32), axis=0, keepdims=True
+                )
+            gain_out[:, lanes] = gain_sum / gain_ref[:, lanes]
+
+    sent, kept, d_gain_a, q_sent, q_kept, kv_sent, kv_kept = call(
+        project_back,
+        "project_back",
+        [
+            *pair,
+            (line_shape, F32),
+            *[((groups // 2, chunk, wide_q), BF)] * 2,
+            *[((groups // 2, chunk, 2 * HEAD_SIZE), BF)] * 2,
+        ],
+        [*q_parts, *kv_parts, d_q, d_kv, normed_all, gain_a],
+    )
+    with jax.named_scope("rs4"):
+        got = swap(sent, CORE)
+    with jax.named_scope("rs4"):
+        sent, kept = add_split(kept, got, "rs4_c")
+        got = swap_tp(sent)
+    with jax.named_scope("rs4"):
+        sent, kept = add_split(kept, got, "rs4_t")
+        kept, got = kept.reshape(own, width), swap(sent, SPLIT).reshape(own, width)
+    q_pair = reduce_to_pair(q_sent, q_kept, near, "r_q")
+    kv_pair = reduce_to_pair(kv_sent, kv_kept, far, "r_kv")
+    qkv_sums = add_joined([q_pair, kv_pair], "sum_qkv", [sent, gate_up])
+    out_sums = add_joined([out_pair], "sum_out", [sent, gate_up])
+    output_grad = trade(out_sums, "t_dout").astype(F32).reshape(4 * wide_q, piece)
     qkv_sums = trade(qkv_sums.reshape(4, piece, qkv_sums.shape[1]), "t_dqkv").astype(F32)
+
+    def join(value, start, stop):
+        return jnp.concatenate([value[n, :, start:stop] for n in range(4)], axis=1)
+
+    gate_up = gate_up.astype(F32)
+    gate_grad = join(gate_up, 0, wide_f)
+    up_grad = join(gate_up, wide_f, 2 * wide_f)
     query_grad = join(qkv_sums, 0, wide_q)
     key_grad = join(qkv_sums, wide_q, wide_q + HEAD_SIZE)
     value_grad = join(qkv_sums, wide_q + HEAD_SIZE, wide_q + 2 * HEAD_SIZE)
 
-    def last_back(kept_ref, got_ref, x_ref, gain_ref, d_ref, out_ref, gain_out):
+    layer_output = (middle + (out_kept.astype(F32) + out_got.astype(F32))).astype(BF)
+    layer_output = put_back([layer_output], "leave1", [sent])[0].reshape(layer_input.shape)
+
+    def last_back(kept_ref, got_ref, x_ref, gain_ref, d_ref, out_ref):
         grad = kept_ref[...].astype(F32) + got_ref[...].astype(F32)
-        back, gain_grad = norm_back(grad, x_ref[...].astype(F32), gain_ref[...])
+        back, _ = norm_back(grad, x_ref[...].astype(F32), gain_ref[...])
         out_ref[...] = (d_ref[...] + back).astype(BF)
-        gain_out[...] = gain_grad
-
-    d_x, d_gain_a = call(
+
+    (d_x,) = call(
         last_back,
         "norm1_back",
-        [((own, width), BF), ((1, width), F32)],
+        [((own, width), BF)],
         [kept, got, x_own, gain_a, d_middle],
     )
-    d_x, d_gain_a, d_gain_m = put_back([d_x, d_gain_a, d_gain_m], "leave2")
-    input_grad = d_x.reshape(layer_input.shape)
-
+    input_grad = put_back([d_x], "leave2")[0].reshape(layer_input.shape)
+
+    d_gain_a, d_gain_m = put_back([d_gain_a, d_gain_m], "leave3", [got])
     gains = jnp.concatenate([d_gain_a, d_gain_m, d_gain_q, d_gain_k], axis=1).reshape(-1, 128)
-    for bit in [CORE, SPLIT] + row_bits:
+    for bit in [CORE] + row_bits:
         gains = gains + swap(gains, bit)
-    gains = (gains + swap_tp(gains)).reshape(-1)
+    gains = gains + swap_tp(gains)
+    gains = (gains + swap(gains, SPLIT)).reshape(-1)
     return (
         layer_output,
         input_grad,

time: 557 us -> 536 us (0.962)
  Pallas kernels: 57.1 us -> 82.6 us
  waiting for transfers between devices: 320 us -> 297 us
  starting transfers between devices: 111 us -> 102 us
  local copies, waits for them, and re-layouts: 30.7 us -> 22.1 us
    pallas_call x28 -> x30, Pallas kernels: 57.1 us -> 82.6 us  [the longest x10 69.8 us: call(): pl.pallas_call(kernel, out_shape=[jax.ShapeDtypeStruct(s, d) for s, d in...]
    ppermute x13, waiting for transfers between devices: 60.1 us -> 38.4 us  [swap_tp(): return lax.ppermute(value, 'tp', [(0, 1), (1, 0)])]
    unnamed x220 -> x192, local copies, waits for them, and re-layouts: 24.4 us -> 13.6 us
    all_to_all x8, waiting for transfers between devices: 34.6 us -> 24.8 us  [trade(): lax.all_to_all(value, 'dp', 0, 0, axis_index_groups=quads, tiled=True)]
    ppermute x69, waiting for transfers between devices: 226 us -> 234 us  [swap(): return lax.ppermute(value, 'dp', [(i, i ^ bit) for i in range(ways)])]
  transfers between devices with their start and end apart: 90 -> 90, of which waited for: 44 -> 38; matrix products, arithmetic and copies ran while one was open for 6% -> 6% of each run, Pallas kernels for 7% -> 12%
where the time goes in v3:
time: 536 us; the launch traced here: 531 us
  waiting for transfers between devices  297 us (55%)
  starting transfers between devices  102 us (19%)
  Pallas kernels  82.6 us (15%)
  other arithmetic  24.7 us (5%)
  local copies, waits for them, and re-layouts  22.1 us (4%)
    ppermute x69, waiting for transfers between devices, swap(): return lax.ppermute(value, 'dp', [(i, i ^ bit) for i in range(ways)])  234 us
    pallas_call x10, Pallas kernels, call(): pl.pallas_call(kernel, out_shape=[jax.ShapeDtypeStruct(s, d) for s, d in...  69.8 us
    ppermute x69, starting transfers between devices, swap(): return lax.ppermute(value, 'dp', [(i, i ^ bit) for i in range(ways)])  58.3 us
    ppermute x13, waiting for transfers between devices, swap_tp(): return lax.ppermute(value, 'tp', [(0, 1), (1, 0)])  38.4 us
    all_to_all x8, starting transfers between devices, trade(): lax.all_to_all(value, 'dp', 0, 0, axis_index_groups=quads, tiled=True)  31.9 us
    all_to_all x8, waiting for transfers between devices, trade(): lax.all_to_all(value, 'dp', 0, 0, axis_index_groups=quads, tiled=True)  24.8 us
    unnamed x192, local copies, waits for them, and re-layouts  13.6 us
    pallas_call x20, Pallas kernels, call(): pl.pallas_call(lambda *refs: body(*refs[:skip], *refs[skip + len(ties):])...  12.8 us
  transfers between devices with their start and end apart: 90, of which 38 were waited for; matrix products, arithmetic and copies ran while one was open for 6% of the time, Pallas kernels for 12%

profile of v3, /device:TPU:0, one launch (start us, length us, event | category | flops | bytes accessed | tf_op | source)
XLA Modules:
  0.0 530.7 jit_solution(5949008166294864949)
XLA Ops:
  2.8 5.4 %all-to-all-start = ((bf16[4,128,768]{2,1,0:T(8,128)(2,1)}), bf16[4,128,768]{2,1,0:T(8,128)(2,1)S(1)}, u32[]{:S(2)}, u32[]{:S(2)}) async-start(bf16[4,128,768]{2,1,0:T(8,128)(2,1)} %pack1.1.refs_5_), calls=%async_computation | async-start | bytes 1572864 | tf_op jit(solution)/shard_map/t_first/all_to_all | solution.py:235
  10.4 3.0 collective-permute-start
  13.4 27.1 %collective-permute-done.refs_2_.refs_1_ = bf16[64,2048]{1,0:T(8,128)(2,1)S(1)} collective-permute-done((bf16[64,2048]{1,0:T(8,128)(2,1)}, bf16[64,2048]{1,0:T(8,128)(2,1)S(1)}, u32[]{:S(2)}, u32[]{:S(2)}) %collective-permute-start) | collective-permute-done | bytes 262176 | tf_op jit(solution)/shard_map/g_norm1/swap8/ppermute | solution.py:227
  41.5 3.5 all-to-all-start.1
  47.6 6.6 %collective-permute-done.1.refs_2_ = bf16[64,2048]{1,0:T(8,128)(2,1)S(1)} collective-permute-done((bf16[64,2048]{1,0:T(8,128)(2,1)S(1)}, bf16[64,2048]{1,0:T(8,128)(2,1)S(1)}, u32[]{:S(2)}, u32[]{:S(2)}) %collective-permute-start.1) | collective-permute-done | bytes 262176 | tf_op jit(solution)/shard_map/g_norm1/swaptp/ppermute | solution.py:231
  54.2 10.8 %all-to-all-done.1 = bf16[4,128,768]{2,1,0:T(8,128)(2,1)S(1)} async-done(((bf16[4,128,768]{2,1,0:T(8,128)(2,1)}), bf16[4,128,768]{2,1,0:T(8,128)(2,1)S(1)}, u32[]{:S(2)}, u32[]{:S(2)}) %all-to-all-start.1) | async-done | bytes 786464 | tf_op jit(solution)/shard_map/t_gate/all_to_all | solution.py:235
  66.1 3.5 all-to-all-start.2
  74.0 11.0 %collective-permute-done.10.refs_13_.refs_5_ = bf16[512,256]{1,0:T(8,128)(2,1)S(1)} collective-permute-done((bf16[512,256]{1,0:T(8,128)(2,1)S(1)}, bf16[512,256]{1,0:T(8,128)(2,1)S(1)}, u32[]{:S(2)}, u32[]{:S(2)}) %collective-permute-start.10) | collective-permute-done | bytes 262176 | tf_op jit(solution)/shard_map/s_kv/swap4/ppermute | solution.py:227
  93.1 5.0 collective-permute-done.9.refs_11_.refs_3_
  98.8 5.3 %project.1 = (bf16[512,2048]{1,0:T(8,128)(2,1)}, bf16[512,256]{1,0:T(8,128)(2,1)}, bf16[512,256]{1,0:T(8,128)(2,1)}, f32[512,256]{1,0:T(8,128)}, f32[512,128]{1,0:T(8,128)}) custom-call(bf16[64,2048]{1,0:T(8,128)(2,1)} %get-tuple-element.83.refs_0_, bf16[64,2048]{1,0:T(8,128)(2,1)} %copy-done.15, bf16[64,2048]{1,0:T(8,128)(2,1)} %copy-done.77, ...), custom_call_target="tpu_custom_call" | custom-call | tf_op jit(solution)/shard_map/project/pallas_call | solution.py:121
  108.3 4.1 collective-permute-done.14.refs_2_.refs_10_
  113.0 3.7 all-to-all-start.3
  118.2 9.5 %collective-permute-done.18.refs_7_.refs_15_ = bf16[512,256]{1,0:T(8,128)(2,1)S(1)} collective-permute-done((bf16[512,256]{1,0:T(8,128)(2,1)S(1)}, bf16[512,256]{1,0:T(8,128)(2,1)S(1)}, u32[]{:S(2)}, u32[]{:S(2)}) %collective-permute-start.18) | collective-permute-done | bytes 262176 | tf_op jit(solution)/shard_map/s_o/swap4/ppermute | solution.py:227
  127.7 7.0 %collective-permute-done.13.refs_1_.refs_9_ = bf16[512,256]{1,0:T(8,128)(2,1)S(1)} collective-permute-done((bf16[512,256]{1,0:T(8,128)(2,1)}, bf16[512,256]{1,0:T(8,128)(2,1)S(1)}, u32[]{:S(2)}, u32[]{:S(2)}) %collective-permute-start.13) | collective-permute-done | bytes 262176 | tf_op jit(solution)/shard_map/s_keys/swap4/ppermute | solution.py:227
  134.8 4.0 collective-permute-done.15.refs_3_.refs_11_
  139.5 7.4 %attend.1 = (f32[512,256]{1,0:T(8,128)}, f32[2,512,1]{2,1,0:T(8,128)}, bf16[2,128,2048]{2,1,0:T(8,128)(2,1)}, bf16[2,128,2048]{2,1,0:T(8,128)(2,1)}) custom-call(bf16[512,256]{1,0:T(8,128)(2,1)} %get-tuple-element.84.refs_0_.refs_8_, bf16[512,256]{1,0:T(8,128)(2,1)} %copy-done.69, bf16[512,256]{1,0:T(8,128)(2,1)} %copy-done.66, bf16[512,256]{1,0:T(8,128)(2,1)} %copy-done.70, ...), custom_call_target="tpu_custom_call" | custom-call | tf_op jit(solution)/shard_map/attend/pallas_call | solution.py:121
  149.0 7.0 %collective-permute-done.25.refs_6_.refs_10_ = bf16[64,2048]{1,0:T(8,128)(2,1)} collective-permute-done((bf16[64,2048]{1,0:T(8,128)(2,1)S(1)}, bf16[64,2048]{1,0:T(8,128)(2,1)}, u32[]{:S(2)}, u32[]{:S(2)}) %collective-permute-start.25) | collective-permute-done | bytes 262176 | tf_op jit(solution)/shard_map/g_cot/swaptp/ppermute | solution.py:231
  156.0 6.7 %collective-permute-done.22.refs_3_.refs_5_.refs_9_ = bf16[64,2048]{1,0:T(8,128)(2,1)} collective-permute-done((bf16[64,2048]{1,0:T(8,128)(2,1)S(1)}, bf16[64,2048]{1,0:T(8,128)(2,1)}, u32[]{:S(2)}, u32[]{:S(2)}) %collective-permute-start.22) | collective-permute-done | bytes 262176 | tf_op jit(solution)/shard_map/g_cot/swap8/ppermute | solution.py:227
  162.6 4.2 collective-permute-done.20.refs_2_.refs_14_.refs_18_
  176.2 10.9 %collective-permute-done.21.refs_1_ = bf16[2,64,2048]{2,1,0:T(8,128)(2,1)S(1)} collective-permute-done((bf16[2,64,2048]{2,1,0:T(8,128)(2,1)}, bf16[2,64,2048]{2,1,0:T(8,128)(2,1)S(1)}, u32[]{:S(2)}, u32[]{:S(2)}) %collective-permute-start.21) | collective-permute-done | bytes 524320 | tf_op jit(solution)/shard_map/rs1/swaptp/ppermute | solution.py:231
  191.9 6.9 %collective-permute-done.31.refs_15_.refs_19_ = bf16[512,768]{1,0:T(8,128)(2,1)S(1)} collective-permute-done((bf16[512,768]{1,0:T(8,128)(2,1)S(1)}, bf16[512,768]{1,0:T(8,128)(2,1)S(1)}, u32[]{:S(2)}, u32[]{:S(2)}) %collective-permute-start.31) | collective-permute-done | bytes 786464 | tf_op jit(solution)/shard_map/s_gate/swap4/ppermute | solution.py:227
  200.4 15.3 %collective-permute-done.32.refs_16_.refs_21_ = bf16[512,768]{1,0:T(8,128)(2,1)S(1)} collective-permute-done((bf16[512,768]{1,0:T(8,128)(2,1)}, bf16[512,768]{1,0:T(8,128)(2,1)S(1)}, u32[]{:S(2)}, u32[]{:S(2)}) %collective-permute-start.32) | collective-permute-done | bytes 786464 | tf_op jit(solution)/shard_map/s_up/swap4/ppermute | solution.py:227
  217.2 12.8 %collective-permute-done.24 = bf16[2,32,2048]{2,1,0:T(8,128)(2,1)S(1)} collective-permute-done((bf16[2,32,2048]{2,1,0:T(8,128)(2,1)S(1)}, bf16[2,32,2048]{2,1,0:T(8,128)(2,1)S(1)}, u32[]{:S(2)}, u32[]{:S(2)}) %collective-permute-start.24) | collective-permute-done | bytes 262176 | tf_op jit(solution)/shard_map/rs1/swap8/ppermute | solution.py:227
  230.4 3.5 collective-permute-start.36
  234.4 17.4 %collective-permute-done.36.refs_1_ = bf16[64,2048]{1,0:T(8,128)(2,1)S(1)} collective-permute-done((bf16[64,2048]{1,0:T(8,128)(2,1)S(1)}, bf16[64,2048]{1,0:T(8,128)(2,1)S(1)}, u32[]{:S(2)}, u32[]{:S(2)}) %collective-permute-start.36) | collective-permute-done | bytes 262176 | tf_op jit(solution)/shard_map/g_norm2/swap8/ppermute | solution.py:227
  254.5 4.7 collective-permute-done.38.refs_3_
  261.6 15.7 %feed.1 = (bf16[512,2048]{1,0:T(8,128)(2,1)}, bf16[512,2048]{1,0:T(8,128)(2,1)}, bf16[512,768]{1,0:T(8,128)(2,1)}, bf16[512,768]{1,0:T(8,128)(2,1)}, bf16[512,76...) custom-call(bf16[64,2048]{1,0:T(8,128)(2,1)} %copy-done.43, ...), custom_call_target="tpu_custom_call" | custom-call | tf_op jit(solution)/shard_map/feed/pallas_call | solution.py:121
  277.9 7.3 %w_gate_up.1 = (bf16[2,512,768]{2,1,0:T(8,128)(2,1)}, bf16[2,512,768]{2,1,0:T(8,128)(2,1)}, bf16[2,512,768]{2,1,0:T(8,128)(2,1)}, bf16[2,512,768]{2,1,0:T(8,128)(2,1)}) custom-call(bf16[512,2048]{1,0:T(8,128)(2,1)} %get-tuple-element.107.refs_0_, bf16[512,768]{1,0:T(8,128)(2,1)} %get-tuple-element.108.refs_1_, bf16[512,768]{1,0:T(8,128)(2,1)} %get-tuple-element.109.refs_2_), custom_call_target="tpu_custom_call" | custom-call | tf_op jit(solution)/shard_map/w_gate_up/pallas_call | solution.py:121
  289.0 5.4 %feed_out.1 = (bf16[2,128,2048]{2,1,0:T(8,128)(2,1)}, bf16[2,128,2048]{2,1,0:T(8,128)(2,1)}) custom-call(bf16[4,768,128]{2,1,0:T(8,128)(2,1)} %copy-done.2, bf16[4,768,128]{2,1,0:T(8,128)(2,1)} %copy-done.53, bf16[4,768,128]{2,1,0:T(8,128)(2,1)} %copy-done.52, bf16[4,768,128]{2,1,0:T(8,128)(2,1)} %copy-done.54, ...), custom_call_target="tpu_custom_call" | custom-call | tf_op jit(solution)/shard_map/feed_out/pallas_call | solution.py:121
  294.4 5.5 %w_down.1 = (bf16[2,4,768,128]{3,2,1,0:T(8,128)(2,1)}, bf16[2,4,768,128]{3,2,1,0:T(8,128)(2,1)}) custom-call(bf16[512,768]{1,0:T(8,128)(2,1)} %get-tuple-element.96.refs_4_.refs_0_, bf16[512,2048]{1,0:T(8,128)(2,1)} %get-tuple-element.111.refs_1_), custom_call_target="tpu_custom_call" | custom-call | tf_op jit(solution)/shard_map/w_down/pallas_call | solution.py:121
  304.4 23.2 %collective-permute-done.64 = bf16[2,512,768]{2,1,0:T(8,128)(2,1)} collective-permute-done((bf16[2,512,768]{2,1,0:T(8,128)(2,1)}, bf16[2,512,768]{2,1,0:T(8,128)(2,1)}, u32[]{:S(2)}, u32[]{:S(2)}) %collective-permute-start.64) | collective-permute-done | bytes 1572896 | tf_op jit(solution)/shard_map/r_up/swap4/ppermute | solution.py:227
  336.4 11.5 %collective-permute-done.50.refs_1_ = bf16[64,2048]{1,0:T(8,128)(2,1)S(1)} collective-permute-done((bf16[64,2048]{1,0:T(8,128)(2,1)S(1)}, bf16[64,2048]{1,0:T(8,128)(2,1)S(1)}, u32[]{:S(2)}, u32[]{:S(2)}) %collective-permute-start.50) | collective-permute-done | bytes 262176 | tf_op jit(solution)/shard_map/g_branch/swap8/ppermute | solution.py:227
  353.3 3.4 collective-permute-done.52.refs_3_
  362.0 11.6 %attend_back.1 = (bf16[512,2048]{1,0:T(8,128)(2,1)}, bf16[512,256]{1,0:T(8,128)(2,1)}, f32[1,128]{1,0:T(1,128)}, bf16[2,512,128]{2,1,0:T(8,128)(2,1)}, bf16[2,51...) custom-call(bf16[64,2048]{1,0:T(8,128)(2,1)} %copy-done.36, ...), custom_call_target="tpu_custom_call" | custom-call | tf_op jit(solution)/shard_map/attend_back/pallas_call | solution.py:121
  385.0 3.5 collective-permute-done.61
  388.5 13.5 %collective-permute-done.59 = bf16[1,512,128]{2,1,0:T(8,128)(2,1)S(1)} collective-permute-done((bf16[1,512,128]{2,1,0:T(8,128)(2,1)S(1)}, bf16[1,512,128]{2,1,0:T(8,128)(2,1)S(1)}, u32[]{:S(2)}, u32[]{:S(2)}) %collective-permute-start.59) | collective-permute-done | bytes 131104 | tf_op jit(solution)/shard_map/r_k/swap4/ppermute | solution.py:227
  403.1 7.2 %project_back.1 = (bf16[2,128,2048]{2,1,0:T(8,128)(2,1)}, bf16[2,128,2048]{2,1,0:T(8,128)(2,1)}, f32[1,2048]{1,0:T(1,128)}, bf16[2,512,256]{2,1,0:T(8,128)(2,1)}...) custom-call(bf16[512,256]{1,0:T(8,128)(2,1)} %copy-done.56, ...), custom_call_target="tpu_custom_call" | custom-call | tf_op jit(solution)/shard_map/project_back/pallas_call | solution.py:121
  414.6 4.2 all-to-all-start.7
  420.9 13.4 %collective-permute-done.57 = bf16[2,32,2048]{2,1,0:T(8,128)(2,1)S(1)} collective-permute-done((bf16[2,32,2048]{2,1,0:T(8,128)(2,1)S(1)}, bf16[2,32,2048]{2,1,0:T(8,128)(2,1)S(1)}, u32[]{:S(2)}, u32[]{:S(2)}) %collective-permute-start.57) | collective-permute-done | bytes 262176 | tf_op jit(solution)/shard_map/rs3/swap8/ppermute | solution.py:227
  440.3 13.5 %collective-permute-done.68 = bf16[2,32,2048]{2,1,0:T(8,128)(2,1)S(1)} collective-permute-done((bf16[2,32,2048]{2,1,0:T(8,128)(2,1)S(1)}, bf16[2,32,2048]{2,1,0:T(8,128)(2,1)S(1)}, u32[]{:S(2)}, u32[]{:S(2)}) %collective-permute-start.68) | collective-permute-done | bytes 262176 | tf_op jit(solution)/shard_map/rs4/swap8/ppermute | solution.py:227
  453.9 4.7 all-to-all-start.4
  468.0 9.3 %collective-permute-done.79 = f32[34,128]{1,0:T(8,128)S(1)} collective-permute-done((f32[34,128]{1,0:T(8,128)S(1)}, f32[34,128]{1,0:T(8,128)S(1)}, u32[]{:S(2)}, u32[]{:S(2)}) %collective-permute-start.79) | collective-permute-done | bytes 17440 | tf_op jit(solution)/shard_map/swap4/ppermute | solution.py:227
  481.1 5.5 %collective-permute-start.81 = (f32[34,128]{1,0:T(8,128)S(1)}, f32[34,128]{1,0:T(8,128)S(1)}, u32[]{:S(2)}, u32[]{:S(2)}) collective-permute-start(f32[34,128]{1,0:T(8,128)S(1)} %add.564), channel_id=1, source_target_pairs={{0,8},{1,9},{2,10},{3,11},{4,12},{5,13},{6,14},{7,15},{8,0},{9,1},... | collective-permute-start | bytes 52232 | tf_op jit(solution)/shard_map/swap8/ppermute | solution.py:227
  490.2 7.2 %collective-permute-done.81 = f32[34,128]{1,0:T(8,128)S(1)} collective-permute-done((f32[34,128]{1,0:T(8,128)S(1)}, f32[34,128]{1,0:T(8,128)S(1)}, u32[]{:S(2)}, u32[]{:S(2)}) %collective-permute-start.81) | collective-permute-done | bytes 17440 | tf_op jit(solution)/shard_map/swap8/ppermute | solution.py:227
  498.8 3.4 all-to-all-start.6
  506.2 4.9 all-to-all-done.6
  511.0 3.5 all-to-all-start.5
  519.0 9.1 %all-to-all-done.5 = bf16[4,128,512]{2,1,0:T(8,128)(2,1)S(1)} async-done(((bf16[4,128,512]{2,1,0:T(8,128)(2,1)}), bf16[4,128,512]{2,1,0:T(8,128)(2,1)S(1)}, u32[]{:S(2)}, u32[]{:S(2)}) %all-to-all-start.5) | async-done | bytes 524320 | tf_op jit(solution)/shard_map/t_dqkv/all_to_all | solution.py:235
  (405 shorter events, 135.9 us)
Async XLA Ops:
  2.8 37.7 %all-to-all-start = ((bf16[4,128,768]{2,1,0:T(8,128)(2,1)}), bf16[4,128,768]{2,1,0:T(8,128)(2,1)S(1)}, u32[]{:S(2)}, u32[]{:S(2)}) async-start(bf16[4,128,768]{2,1,0:T(8,128)(2,1)} %pack1.1.refs_5_), calls=%async_computation | async-start | bytes 1572864 | tf_op jit(solution)/shard_map/t_first/all_to_all | solution.py:235
  10.4 30.1 %collective-permute-start = (bf16[64,2048]{1,0:T(8,128)(2,1)}, bf16[64,2048]{1,0:T(8,128)(2,1)S(1)}, u32[]{:S(2)}, u32[]{:S(2)}) collective-permute-start(bf16[64,2048]{1,0:T(8,128)(2,1)} %get-tuple-element.83.refs_0_), channel_id=1, source_target_pairs={{0,8},{1,9},{2,10},{3,11},{4,12},{5,13},{6,14},{7,15},{8,0},{9,1},... | collective-permute-start | bytes 786440 | tf_op jit(solution)/shard_map/g_norm1/swap8/ppermute | solution.py:227
  41.5 23.5 %all-to-all-start.1 = ((bf16[4,128,768]{2,1,0:T(8,128)(2,1)}), bf16[4,128,768]{2,1,0:T(8,128)(2,1)S(1)}, u32[]{:S(2)}, u32[]{:S(2)}) async-start(bf16[4,128,768]{2,1,0:T(8,128)(2,1)} %pack2.1), calls=%async_computation.1 | async-start | bytes 1572864 | tf_op jit(solution)/shard_map/t_gate/all_to_all | solution.py:235
  46.5 23.3 %collective-permute-start.3 = (bf16[64,2048]{1,0:T(8,128)(2,1)S(1)}, bf16[64,2048]{1,0:T(8,128)(2,1)}, u32[]{:S(2)}, u32[]{:S(2)}) collective-permute-start(bf16[64,2048]{1,0:T(8,128)(2,1)S(1)} %copy-done.76), channel_id=1, source_target_pairs={{0,1},{1,0},{2,3},{3,2},{4,5},{5,4},{6,7},{7,6},{8,9},{9,8},{10,11... | collective-permute-start | bytes 786440 | tf_op jit(solution)/shard_map/g_norm1/swap1/ppermute | solution.py:227
  46.7 25.5 %collective-permute-start.4 = (bf16[64,2048]{1,0:T(8,128)(2,1)S(1)}, bf16[64,2048]{1,0:T(8,128)(2,1)}, u32[]{:S(2)}, u32[]{:S(2)}) collective-permute-start(bf16[64,2048]{1,0:T(8,128)(2,1)S(1)} %collective-permute-done.refs_2_.refs_1_), channel_id=1, source_target_pairs={{0,1},{1,0},{2,3},{3,2},{4,5},{5,4},{6,7},{7,6},{8,9},{9,8},{10,11... | collective-permute-start | bytes 786440 | tf_op jit(solution)/shard_map/g_norm1/swap1/ppermute | solution.py:227
  47.1 24.4 %collective-permute-start.2 = (bf16[64,2048]{1,0:T(8,128)(2,1)S(1)}, bf16[64,2048]{1,0:T(8,128)(2,1)}, u32[]{:S(2)}, u32[]{:S(2)}) collective-permute-start(bf16[64,2048]{1,0:T(8,128)(2,1)S(1)} %collective-permute-done.refs_2_.refs_1_), channel_id=1, source_target_pairs={{0,16},{16,0},{1,17},{17,1},{2,18},{18,2},{3,19},{19,3},{4,20},{20... | collective-permute-start | bytes 786440 | tf_op jit(solution)/shard_map/g_norm1/swaptp/ppermute | solution.py:231
  54.2 17.5 %collective-permute-start.5 = (bf16[64,2048]{1,0:T(8,128)(2,1)S(1)}, bf16[64,2048]{1,0:T(8,128)(2,1)}, u32[]{:S(2)}, u32[]{:S(2)}) collective-permute-start(bf16[64,2048]{1,0:T(8,128)(2,1)S(1)} %collective-permute-done.1.refs_2_), channel_id=1, source_target_pairs={{0,1},{1,0},{2,3},{3,2},{4,5},{5,4},{6,7},{7,6},{8,9},{9,8},{10,11... | collective-permute-start | bytes 786440 | tf_op jit(solution)/shard_map/g_norm1/swap1/ppermute | solution.py:227
  66.1 46.8 %all-to-all-start.2 = ((bf16[4,128,768]{2,1,0:T(8,128)(2,1)}), bf16[4,128,768]{2,1,0:T(8,128)(2,1)S(1)}, u32[]{:S(2)}, u32[]{:S(2)}) async-start(bf16[4,128,768]{2,1,0:T(8,128)(2,1)} %pack3.1), calls=%async_computation.2 | async-start | bytes 1572864 | tf_op jit(solution)/shard_map/t_up/all_to_all | solution.py:235
  71.4 19.5 %collective-permute-start.6 = (bf16[64,2048]{1,0:T(8,128)(2,1)}, bf16[64,2048]{1,0:T(8,128)(2,1)S(1)}, u32[]{:S(2)}, u32[]{:S(2)}) collective-permute-start(bf16[64,2048]{1,0:T(8,128)(2,1)} %collective-permute-done.2.refs_3_), channel_id=1, source_target_pairs={{0,1},{1,0},{2,3},{3,2},{4,5},{5,4},{6,7},{7,6},{8,9},{9,8},{10,11... | collective-permute-start | bytes 786440 | tf_op jit(solution)/shard_map/g_norm1/swap1/ppermute | solution.py:227
  71.7 19.8 %collective-permute-start.11 = (bf16[512,256]{1,0:T(8,128)(2,1)S(1)}, bf16[512,256]{1,0:T(8,128)(2,1)S(1)}, u32[]{:S(2)}, u32[]{:S(2)}) collective-permute-start(bf16[512,256]{1,0:T(8,128)(2,1)S(1)} %get-tuple-element.189.refs_12_.refs_4_), channel_id=1, source_target_pairs={{0,2},{1,3},{2,0},{3,1},{4,6},{5,7},{6,4},{7,5},{8,10},{9,11},{10,... | collective-permute-start | bytes 786440 | tf_op jit(solution)/shard_map/s_kv/swap2/ppermute | solution.py:227
  72.2 20.7 %collective-permute-start.7 = (bf16[512,256]{1,0:T(8,128)(2,1)S(1)}, bf16[512,256]{1,0:T(8,128)(2,1)S(1)}, u32[]{:S(2)}, u32[]{:S(2)}) collective-permute-start(bf16[512,256]{1,0:T(8,128)(2,1)S(1)} %get-tuple-element.190.refs_8_.refs_0_), channel_id=1, source_target_pairs={{0,4},{1,5},{2,6},{3,7},{4,0},{5,1},{6,2},{7,3},{8,12},{9,13},{10,... | collective-permute-start | bytes 786440 | tf_op jit(solution)/shard_map/s_q/swap4/ppermute | solution.py:227
  106.2 21.5 %collective-permute-start.18 = (bf16[512,256]{1,0:T(8,128)(2,1)S(1)}, bf16[512,256]{1,0:T(8,128)(2,1)S(1)}, u32[]{:S(2)}, u32[]{:S(2)}) collective-permute-start(bf16[512,256]{1,0:T(8,128)(2,1)S(1)} %collective-permute-done.17.refs_6_.refs_14_), channel_id=1, source_target_pairs={{0,4},{1,5},{2,6},{3,7},{4,0},{5,1},{6,2},{7,3},{8,12},{9,13},{10,... | collective-permute-start | bytes 786440 | tf_op jit(solution)/shard_map/s_o/swap4/ppermute | solution.py:227
  107.9 26.9 %collective-permute-start.13 = (bf16[512,256]{1,0:T(8,128)(2,1)}, bf16[512,256]{1,0:T(8,128)(2,1)S(1)}, u32[]{:S(2)}, u32[]{:S(2)}) collective-permute-start(bf16[512,256]{1,0:T(8,128)(2,1)} %get-tuple-element.84.refs_0_.refs_8_), channel_id=1, source_target_pairs={{0,4},{1,5},{2,6},{3,7},{4,0},{5,1},{6,2},{7,3},{8,12},{9,13},{10,... | collective-permute-start | bytes 786440 | tf_op jit(solution)/shard_map/s_keys/swap4/ppermute | solution.py:227
  112.3 26.4 %collective-permute-start.15 = (bf16[512,256]{1,0:T(8,128)(2,1)S(1)}, bf16[512,256]{1,0:T(8,128)(2,1)S(1)}, u32[]{:S(2)}, u32[]{:S(2)}) collective-permute-start(bf16[512,256]{1,0:T(8,128)(2,1)S(1)} %collective-permute-done.14.refs_2_.refs_10_), channel_id=1, source_target_pairs={{0,4},{1,5},{2,6},{3,7},{4,0},{5,1},{6,2},{7,3},{8,12},{9,13},{10,... | collective-permute-start | bytes 786440 | tf_op jit(solution)/shard_map/s_keys/swap4/ppermute | solution.py:227
  113.0 59.2 %all-to-all-start.3 = ((bf16[4,768,128]{2,1,0:T(8,128)(2,1)}), bf16[4,768,128]{2,1,0:T(8,128)(2,1)S(1)}, u32[]{:S(2)}, u32[]{:S(2)}) async-start(bf16[4,768,128]{2,1,0:T(8,128)(2,1)} %bitcast.114), calls=%async_computation.3 | async-start | bytes 1572864 | tf_op jit(solution)/shard_map/t_down/all_to_all | solution.py:235
  146.8 20.0 %collective-permute-start.19 = (bf16[2,128,2048]{2,1,0:T(8,128)(2,1)}, bf16[2,128,2048]{2,1,0:T(8,128)(2,1)S(1)}, u32[]{:S(2)}, u32[]{:S(2)}) collective-permute-start(bf16[2,128,2048]{2,1,0:T(8,128)(2,1)} %get-tuple-element.87), channel_id=1, source_target_pairs={{0,1},{1,0},{2,3},{3,2},{4,5},{5,4},{6,7},{7,6},{8,9},{9,8},{10,11... | collective-permute-start | bytes 3145736 | tf_op jit(solution)/shard_map/rs1/swap1/ppermute | solution.py:227
  146.9 20.0 %collective-permute-start.20 = (bf16[512,768]{1,0:T(8,128)(2,1)S(1)}, bf16[512,768]{1,0:T(8,128)(2,1)S(1)}, u32[]{:S(2)}, u32[]{:S(2)}) collective-permute-start(bf16[512,768]{1,0:T(8,128)(2,1)S(1)} %bitcast.96), channel_id=1, source_target_pairs={{0,2},{1,3},{2,0},{3,1},{4,6},{5,7},{6,4},{7,5},{8,10},{9,11},{10,... | collective-permute-start | bytes 2359304 | tf_op jit(solution)/shard_map/s_gate/swap2/ppermute | solution.py:227
  149.0 27.1 %collective-permute-start.23 = (bf16[512,768]{1,0:T(8,128)(2,1)S(1)}, bf16[512,768]{1,0:T(8,128)(2,1)S(1)}, u32[]{:S(2)}, u32[]{:S(2)}) collective-permute-start(bf16[512,768]{1,0:T(8,128)(2,1)S(1)} %bitcast.97), channel_id=1, source_target_pairs={{0,4},{1,5},{2,6},{3,7},{4,0},{5,1},{6,2},{7,3},{8,12},{9,13},{10,... | collective-permute-start | bytes 2359304 | tf_op jit(solution)/shard_map/s_gate/swap4/ppermute | solution.py:227
  172.2 19.7 %collective-permute-start.34 = (bf16[4,768,128]{2,1,0:T(8,128)(2,1)S(1)}, bf16[4,768,128]{2,1,0:T(8,128)(2,1)S(1)}, u32[]{:S(2)}, u32[]{:S(2)}) collective-permute-start(bf16[4,768,128]{2,1,0:T(8,128)(2,1)S(1)} %all-to-all-done.3.refs_2_.refs_24_.refs_0_), channel_id=1, source_target_pairs={{0,2},{1,3},{2,0},{3,1},{4,6},{5,7},{6,4},{7,5},{8,10},{9,11},{10,... | collective-permute-start | bytes 2359304 | tf_op jit(solution)/shard_map/s_down/swap2/ppermute | solution.py:227
  172.8 26.0 %collective-permute-start.31 = (bf16[512,768]{1,0:T(8,128)(2,1)S(1)}, bf16[512,768]{1,0:T(8,128)(2,1)S(1)}, u32[]{:S(2)}, u32[]{:S(2)}) collective-permute-start(bf16[512,768]{1,0:T(8,128)(2,1)S(1)} %collective-permute-done.20.refs_2_.refs_14_.refs_18_), channel_id=1, source_target_pairs={{0,4},{1,5},{2,6},{3,7},{4,0},{5,1},{6,2},{7,3},{8,12},{9,13},{10,... | collective-permute-start | bytes 2359304 | tf_op jit(solution)/shard_map/s_gate/swap4/ppermute | solution.py:227
  176.1 39.6 %collective-permute-start.32 = (bf16[512,768]{1,0:T(8,128)(2,1)}, bf16[512,768]{1,0:T(8,128)(2,1)S(1)}, u32[]{:S(2)}, u32[]{:S(2)}) collective-permute-start(bf16[512,768]{1,0:T(8,128)(2,1)} %bitcast.111), channel_id=1, source_target_pairs={{0,4},{1,5},{2,6},{3,7},{4,0},{5,1},{6,2},{7,3},{8,12},{9,13},{10,... | collective-permute-start | bytes 2359304 | tf_op jit(solution)/shard_map/s_up/swap4/ppermute | solution.py:227
  187.1 46.8 %collective-permute-start.33 = (bf16[4,768,128]{2,1,0:T(8,128)(2,1)S(1)}, bf16[4,768,128]{2,1,0:T(8,128)(2,1)S(1)}, u32[]{:S(2)}, u32[]{:S(2)}) collective-permute-start(bf16[4,768,128]{2,1,0:T(8,128)(2,1)S(1)} %all-to-all-done.3.refs_2_.refs_24_.refs_0_), channel_id=1, source_target_pairs={{0,4},{1,5},{2,6},{3,7},{4,0},{5,1},{6,2},{7,3},{8,12},{9,13},{10,... | collective-permute-start | bytes 2359304 | tf_op jit(solution)/shard_map/s_down/swap4/ppermute | solution.py:227
  189.7 40.4 %collective-permute-start.24 = (bf16[2,32,2048]{2,1,0:T(8,128)(2,1)S(1)}, bf16[2,32,2048]{2,1,0:T(8,128)(2,1)S(1)}, u32[]{:S(2)}, u32[]{:S(2)}) collective-permute-start(bf16[2,32,2048]{2,1,0:T(8,128)(2,1)S(1)} %get-tuple-element.92), channel_id=1, source_target_pairs={{0,8},{1,9},{2,10},{3,11},{4,12},{5,13},{6,14},{7,15},{8,0},{9,1},... | collective-permute-start | bytes 786440 | tf_op jit(solution)/shard_map/rs1/swap8/ppermute | solution.py:227
  191.9 62.0 %collective-permute-start.35 = (bf16[4,768,128]{2,1,0:T(8,128)(2,1)S(1)}, bf16[4,768,128]{2,1,0:T(8,128)(2,1)S(1)}, u32[]{:S(2)}, u32[]{:S(2)}) collective-permute-start(bf16[4,768,128]{2,1,0:T(8,128)(2,1)S(1)} %collective-permute-done.34.refs_26_.refs_2_), channel_id=1, source_target_pairs={{0,4},{1,5},{2,6},{3,7},{4,0},{5,1},{6,2},{7,3},{8,12},{9,13},{10,... | collective-permute-start | bytes 2359304 | tf_op jit(solution)/shard_map/s_down/swap4/ppermute | solution.py:227
  198.9 55.1 %collective-permute-start.43 = (bf16[512,768]{1,0:T(8,128)(2,1)S(1)}, bf16[512,768]{1,0:T(8,128)(2,1)S(1)}, u32[]{:S(2)}, u32[]{:S(2)}) collective-permute-start(bf16[512,768]{1,0:T(8,128)(2,1)S(1)} %bitcast.113), channel_id=1, source_target_pairs={{0,2},{1,3},{2,0},{3,1},{4,6},{5,7},{6,4},{7,5},{8,10},{9,11},{10,... | collective-permute-start | bytes 2359304 | tf_op jit(solution)/shard_map/s_up/swap2/ppermute | solution.py:227
  215.7 43.6 %collective-permute-start.44 = (bf16[512,768]{1,0:T(8,128)(2,1)S(1)}, bf16[512,768]{1,0:T(8,128)(2,1)S(1)}, u32[]{:S(2)}, u32[]{:S(2)}) collective-permute-start(bf16[512,768]{1,0:T(8,128)(2,1)S(1)} %collective-permute-done.32.refs_16_.refs_21_), channel_id=1, source_target_pairs={{0,2},{1,3},{2,0},{3,1},{4,6},{5,7},{6,4},{7,5},{8,10},{9,11},{10,... | collective-permute-start | bytes 2359304 | tf_op jit(solution)/shard_map/s_up/swap2/ppermute | solution.py:227
  230.4 21.4 %collective-permute-start.36 = (bf16[64,2048]{1,0:T(8,128)(2,1)S(1)}, bf16[64,2048]{1,0:T(8,128)(2,1)S(1)}, u32[]{:S(2)}, u32[]{:S(2)}) collective-permute-start(bf16[64,2048]{1,0:T(8,128)(2,1)S(1)} %get-tuple-element.95.refs_0_), channel_id=1, source_target_pairs={{0,8},{1,9},{2,10},{3,11},{4,12},{5,13},{6,14},{7,15},{8,0},{9,1},... | collective-permute-start | bytes 786440 | tf_op jit(solution)/shard_map/g_norm2/swap8/ppermute | solution.py:227
  233.8 20.6 %collective-permute-start.37 = (bf16[64,2048]{1,0:T(8,128)(2,1)S(1)}, bf16[64,2048]{1,0:T(8,128)(2,1)S(1)}, u32[]{:S(2)}, u32[]{:S(2)}) collective-permute-start(bf16[64,2048]{1,0:T(8,128)(2,1)S(1)} %get-tuple-element.95.refs_0_), channel_id=1, source_target_pairs={{0,16},{16,0},{1,17},{17,1},{2,18},{18,2},{3,19},{19,3},{4,20},{20... | collective-permute-start | bytes 786440 | tf_op jit(solution)/shard_map/g_norm2/swaptp/ppermute | solution.py:231
  285.3 42.3 %collective-permute-start.64 = (bf16[2,512,768]{2,1,0:T(8,128)(2,1)}, bf16[2,512,768]{2,1,0:T(8,128)(2,1)}, u32[]{:S(2)}, u32[]{:S(2)}) collective-permute-start(bf16[2,512,768]{2,1,0:T(8,128)(2,1)} %get-tuple-element.128), channel_id=1, source_target_pairs={{0,4},{1,5},{2,6},{3,7},{4,0},{5,1},{6,2},{7,3},{8,12},{9,13},{10,... | collective-permute-start | bytes 4718600 | tf_op jit(solution)/shard_map/r_up/swap4/ppermute | solution.py:227
  286.6 43.4 %collective-permute-start.62 = (bf16[2,512,768]{2,1,0:T(8,128)(2,1)}, bf16[2,512,768]{2,1,0:T(8,128)(2,1)}, u32[]{:S(2)}, u32[]{:S(2)}) collective-permute-start(bf16[2,512,768]{2,1,0:T(8,128)(2,1)} %get-tuple-element.110.refs_5_), channel_id=1, source_target_pairs={{0,2},{1,3},{2,0},{3,1},{4,6},{5,7},{6,4},{7,5},{8,10},{9,11},{10,... | collective-permute-start | bytes 4718600 | tf_op jit(solution)/shard_map/r_gate/swap2/ppermute | solution.py:227
  294.4 53.5 %collective-permute-start.45 = (bf16[2,128,2048]{2,1,0:T(8,128)(2,1)}, bf16[2,128,2048]{2,1,0:T(8,128)(2,1)}, u32[]{:S(2)}, u32[]{:S(2)}) collective-permute-start(bf16[2,128,2048]{2,1,0:T(8,128)(2,1)} %get-tuple-element.98), channel_id=1, source_target_pairs={{0,1},{1,0},{2,3},{3,2},{4,5},{5,4},{6,7},{7,6},{8,9},{9,8},{10,11... | collective-permute-start | bytes 3145736 | tf_op jit(solution)/shard_map/rs3/swap1/ppermute | solution.py:227
  299.9 73.8 %collective-permute-start.75 = (bf16[2,4,768,128]{3,2,1,0:T(8,128)(2,1)}, bf16[2,4,768,128]{3,2,1,0:T(8,128)(2,1)}, u32[]{:S(2)}, u32[]{:S(2)}) collective-permute-start(bf16[2,4,768,128]{3,2,1,0:T(8,128)(2,1)} %get-tuple-element.112.refs_6_), channel_id=1, source_target_pairs={{0,2},{1,3},{2,0},{3,1},{4,6},{5,7},{6,4},{7,5},{8,10},{9,11},{10,... | collective-permute-start | bytes 4718600 | tf_op jit(solution)/shard_map/r_down/swap2/ppermute | solution.py:227
  301.9 30.2 %collective-permute-start.49 = (bf16[2,32,2048]{2,1,0:T(8,128)(2,1)S(1)}, bf16[2,32,2048]{2,1,0:T(8,128)(2,1)S(1)}, u32[]{:S(2)}, u32[]{:S(2)}) collective-permute-start(bf16[2,32,2048]{2,1,0:T(8,128)(2,1)S(1)} %get-tuple-element.106), channel_id=1, source_target_pairs={{0,8},{1,9},{2,10},{3,11},{4,12},{5,13},{6,14},{7,15},{8,0},{9,1},... | collective-permute-start | bytes 786440 | tf_op jit(solution)/shard_map/rs2/swap8/ppermute | solution.py:227
  351.8 30.0 %collective-permute-start.65 = (bf16[1,512,768]{2,1,0:T(8,128)(2,1)}, bf16[1,512,768]{2,1,0:T(8,128)(2,1)S(1)}, u32[]{:S(2)}, u32[]{:S(2)}) collective-permute-start(bf16[1,512,768]{2,1,0:T(8,128)(2,1)} %get-tuple-element.172), channel_id=1, source_target_pairs={{0,2},{1,3},{2,0},{3,1},{4,6},{5,7},{6,4},{7,5},{8,10},{9,11},{10,... | collective-permute-start | bytes 2359304 | tf_op jit(solution)/shard_map/r_up/swap2/ppermute | solution.py:227
  353.3 28.5 %collective-permute-start.63 = (bf16[1,512,768]{2,1,0:T(8,128)(2,1)}, bf16[1,512,768]{2,1,0:T(8,128)(2,1)S(1)}, u32[]{:S(2)}, u32[]{:S(2)}) collective-permute-start(bf16[1,512,768]{2,1,0:T(8,128)(2,1)} %get-tuple-element.174), channel_id=1, source_target_pairs={{0,4},{1,5},{2,6},{3,7},{4,0},{5,1},{6,2},{7,3},{8,12},{9,13},{10,... | collective-permute-start | bytes 2359304 | tf_op jit(solution)/shard_map/r_gate/swap4/ppermute | solution.py:227
  359.8 18.8 %collective-permute-start.46 = (bf16[2,64,2048]{2,1,0:T(8,128)(2,1)S(1)}, bf16[2,64,2048]{2,1,0:T(8,128)(2,1)}, u32[]{:S(2)}, u32[]{:S(2)}) collective-permute-start(bf16[2,64,2048]{2,1,0:T(8,128)(2,1)S(1)} %get-tuple-element.100.refs_25_), channel_id=1, source_target_pairs={{0,16},{16,0},{1,17},{17,1},{2,18},{18,2},{3,19},{19,3},{4,20},{20... | collective-permute-start | bytes 1572872 | tf_op jit(solution)/shard_map/rs3/swaptp/ppermute | solution.py:231
  378.6 33.5 %collective-permute-start.76 = (bf16[1,4,768,128]{3,2,1,0:T(8,128)(2,1)}, bf16[1,4,768,128]{3,2,1,0:T(8,128)(2,1)}, u32[]{:S(2)}, u32[]{:S(2)}) collective-permute-start(bf16[1,4,768,128]{3,2,1,0:T(8,128)(2,1)} %slice.242), channel_id=1, source_target_pairs={{0,4},{1,5},{2,6},{3,7},{4,0},{5,1},{6,2},{7,3},{8,12},{9,13},{10,... | collective-permute-start | bytes 2359304 | tf_op jit(solution)/shard_map/r_down/swap4/ppermute | solution.py:227
  384.9 17.1 %collective-permute-start.59 = (bf16[1,512,128]{2,1,0:T(8,128)(2,1)S(1)}, bf16[1,512,128]{2,1,0:T(8,128)(2,1)S(1)}, u32[]{:S(2)}, u32[]{:S(2)}) collective-permute-start(bf16[1,512,128]{2,1,0:T(8,128)(2,1)S(1)} %slice.208), channel_id=1, source_target_pairs={{0,4},{1,5},{2,6},{3,7},{4,0},{5,1},{6,2},{7,3},{8,12},{9,13},{10,... | collective-permute-start | bytes 393224 | tf_op jit(solution)/shard_map/r_k/swap4/ppermute | solution.py:227
  410.5 23.9 %collective-permute-start.57 = (bf16[2,32,2048]{2,1,0:T(8,128)(2,1)S(1)}, bf16[2,32,2048]{2,1,0:T(8,128)(2,1)S(1)}, u32[]{:S(2)}, u32[]{:S(2)}) collective-permute-start(bf16[2,32,2048]{2,1,0:T(8,128)(2,1)S(1)} %copy-done.42), channel_id=1, source_target_pairs={{0,8},{1,9},{2,10},{3,11},{4,12},{5,13},{6,14},{7,15},{8,0},{9,1},... | collective-permute-start | bytes 786440 | tf_op jit(solution)/shard_map/rs3/swap8/ppermute | solution.py:227
  414.6 39.3 %all-to-all-start.7 = ((bf16[4,768,128]{2,1,0:T(8,128)(2,1)}), bf16[4,768,128]{2,1,0:T(8,128)(2,1)}, u32[]{:S(2)}, u32[]{:S(2)}) async-start(bf16[4,768,128]{2,1,0:T(8,128)(2,1)} %fusion), calls=%async_computation.7 | async-start | bytes 1572864 | tf_op jit(solution)/shard_map/t_ddown/all_to_all | solution.py:235
  418.8 20.6 %collective-permute-start.73 = (bf16[2,4,256,128]{3,2,1,0:T(8,128)(2,1)S(1)}, bf16[2,4,256,128]{3,2,1,0:T(8,128)(2,1)S(1)}, u32[]{:S(2)}, u32[]{:S(2)}) collective-permute-start(bf16[2,4,256,128]{3,2,1,0:T(8,128)(2,1)S(1)} %copy-done.33), channel_id=1, source_target_pairs={{0,2},{1,3},{2,0},{3,1},{4,6},{5,7},{6,4},{7,5},{8,10},{9,11},{10,... | collective-permute-start | bytes 1572872 | tf_op jit(solution)/shard_map/r_out/swap2/ppermute | solution.py:227
  434.5 27.7 %collective-permute-start.69 = (bf16[2,512,256]{2,1,0:T(8,128)(2,1)}, bf16[2,512,256]{2,1,0:T(8,128)(2,1)}, u32[]{:S(2)}, u32[]{:S(2)}) collective-permute-start(bf16[2,512,256]{2,1,0:T(8,128)(2,1)} %get-tuple-element.140), channel_id=1, source_target_pairs={{0,2},{1,3},{2,0},{3,1},{4,6},{5,7},{6,4},{7,5},{8,10},{9,11},{10,... | collective-permute-start | bytes 1572872 | tf_op jit(solution)/shard_map/r_q/swap2/ppermute | solution.py:227
  435.6 42.2 %collective-permute-start.71 = (bf16[2,512,256]{2,1,0:T(8,128)(2,1)}, bf16[2,512,256]{2,1,0:T(8,128)(2,1)}, u32[]{:S(2)}, u32[]{:S(2)}) collective-permute-start(bf16[2,512,256]{2,1,0:T(8,128)(2,1)} %get-tuple-element.142), channel_id=1, source_target_pairs={{0,4},{1,5},{2,6},{3,7},{4,0},{5,1},{6,2},{7,3},{8,12},{9,13},{10,... | collective-permute-start | bytes 1572872 | tf_op jit(solution)/shard_map/r_kv/swap4/ppermute | solution.py:227
  436.4 17.3 %collective-permute-start.68 = (bf16[2,32,2048]{2,1,0:T(8,128)(2,1)S(1)}, bf16[2,32,2048]{2,1,0:T(8,128)(2,1)S(1)}, u32[]{:S(2)}, u32[]{:S(2)}) collective-permute-start(bf16[2,32,2048]{2,1,0:T(8,128)(2,1)S(1)} %get-tuple-element.136.refs_2_.refs_4_), channel_id=1, source_target_pairs={{0,8},{1,9},{2,10},{3,11},{4,12},{5,13},{6,14},{7,15},{8,0},{9,1},... | collective-permute-start | bytes 786440 | tf_op jit(solution)/shard_map/rs4/swap8/ppermute | solution.py:227
  440.3 57.8 %collective-permute-start.74 = (bf16[1,4,256,128]{3,2,1,0:T(8,128)(2,1)}, bf16[1,4,256,128]{3,2,1,0:T(8,128)(2,1)S(1)}, u32[]{:S(2)}, u32[]{:S(2)}) collective-permute-start(bf16[1,4,256,128]{3,2,1,0:T(8,128)(2,1)} %get-tuple-element.191), channel_id=1, source_target_pairs={{0,4},{1,5},{2,6},{3,7},{4,0},{5,1},{6,2},{7,3},{8,12},{9,13},{10,... | collective-permute-start | bytes 786440 | tf_op jit(solution)/shard_map/r_out/swap4/ppermute | solution.py:227
  453.9 44.1 %all-to-all-start.4 = ((bf16[4,128,1536]{2,1,0:T(8,128)(2,1)}), bf16[4,128,1536]{2,1,0:T(8,128)(2,1)S(1)}, u32[]{:S(2)}, u32[]{:S(2)}) async-start(bf16[4,128,1536]{2,1,0:T(8,128)(2,1)} %bitcast.24), calls=%async_computation.4 | async-start | bytes 3145728 | tf_op jit(solution)/shard_map/t_dgu/all_to_all | solution.py:235
  468.0 35.2 %collective-permute-start.70 = (bf16[1,512,256]{2,1,0:T(8,128)(2,1)}, bf16[1,512,256]{2,1,0:T(8,128)(2,1)}, u32[]{:S(2)}, u32[]{:S(2)}) collective-permute-start(bf16[1,512,256]{2,1,0:T(8,128)(2,1)} %get-tuple-element.195), channel_id=1, source_target_pairs={{0,4},{1,5},{2,6},{3,7},{4,0},{5,1},{6,2},{7,3},{8,12},{9,13},{10,... | collective-permute-start | bytes 786440 | tf_op jit(solution)/shard_map/r_q/swap4/ppermute | solution.py:227
  511.0 17.0 %all-to-all-start.5 = ((bf16[4,128,512]{2,1,0:T(8,128)(2,1)}), bf16[4,128,512]{2,1,0:T(8,128)(2,1)S(1)}, u32[]{:S(2)}, u32[]{:S(2)}) async-start(bf16[4,128,512]{2,1,0:T(8,128)(2,1)} %bitcast.25), calls=%async_computation.5 | async-start | bytes 1048576 | tf_op jit(solution)/shard_map/t_dqkv/all_to_all | solution.py:235
  (138 other events, 1811.2 us)

commit v4 on v3

--- a/solution.py
+++ b/solution.py
@@ -802,14 +802,13 @@
             j = slot[which]
             value = dot_tn(heads, d_all_ref[:, j * chunk : (j + 1) * chunk]).astype(BF)
             for f in range(4):
-                part = value[:, f * piece : (f + 1) * piece]
-                if n < groups // 2:
-                    o_kept[n, f] = part
-                else:
-                    o_sent[n - groups // 2, f] = part
+                ref, at = (o_kept, n) if n < groups // 2 else (o_sent, n - groups // 2)
+                lines = slice(f * piece, (f + 1) * piece)
+                for b in range(0, wide_q, piece):
+                    ref[at, lines, b : b + piece] = value[b : b + piece, lines]
 
     part_shape = ((groups // 2, all_rows, HEAD_SIZE), BF)
-    o_shape = ((groups // 2, 4, wide_q, piece), BF)
+    o_shape = ((groups // 2, chunk, wide_q), BF)
     d_all, d_q, d_gain_q, k_sent, k_kept, v_sent, v_kept, o_sent, o_kept = call(
         attend_back,
         "attend_back",
@@ -918,9 +917,7 @@
         kept, got = kept.reshape(own, width), swap(sent, SPLIT).reshape(own, width)
     q_pair = reduce_to_pair(q_sent, q_kept, near, "r_q")
     kv_pair = reduce_to_pair(kv_sent, kv_kept, far, "r_kv")
-    qkv_sums = add_joined([q_pair, kv_pair], "sum_qkv", [sent, gate_up])
-    out_sums = add_joined([out_pair], "sum_out", [sent, gate_up])
-    output_grad = trade(out_sums, "t_dout").astype(F32).reshape(4 * wide_q, piece)
+    qkv_sums = add_joined([q_pair, kv_pair, out_pair], "sum_qkv", [sent, gate_up])
     qkv_sums = trade(qkv_sums.reshape(4, piece, qkv_sums.shape[1]), "t_dqkv").astype(F32)
 
     def join(value, start, stop):
@@ -932,6 +929,9 @@
     query_grad = join(qkv_sums, 0, wide_q)
     key_grad = join(qkv_sums, wide_q, wide_q + HEAD_SIZE)
     value_grad = join(qkv_sums, wide_q + HEAD_SIZE, wide_q + 2 * HEAD_SIZE)
+    output_grad = qkv_sums[:, :, wide_q + 2 * HEAD_SIZE :]
+    output_grad = output_grad.reshape(4, piece, wide_q // piece, piece).transpose(0, 2, 1, 3)
+    output_grad = output_grad.reshape(4 * wide_q, piece)
 
     layer_output = (middle + (out_kept.astype(F32) + out_got.astype(F32))).astype(BF)
     layer_output = put_back([layer_output], "leave1", [sent])[0].reshape(layer_input.shape)

time: 536 us -> 535 us (level)
    unnamed x192 -> x196, local copies, waits for them, and re-layouts: 13.6 us -> 16.9 us
    all_to_all x8 -> x7, starting transfers between devices: 31.9 us -> 28.7 us  [trade(): lax.all_to_all(value, 'dp', 0, 0, axis_index_groups=quads, tiled=True)]
    all_to_all x8 -> x7, waiting for transfers between devices: 24.8 us -> 26.9 us  [trade(): lax.all_to_all(value, 'dp', 0, 0, axis_index_groups=quads, tiled=True)]
    pallas_call x20 -> x19, Pallas kernels: 12.8 us -> 11.2 us  [call(): pl.pallas_call(lambda *refs: body(*refs[:skip], *refs[skip + len(ties):])...]
  transfers between devices with their start and end apart: 90 -> 89, of which waited for: 38 -> 37; matrix products, arithmetic and copies ran while one was open for 6% -> 5% of each run, Pallas kernels for 12% -> 12%
where the time goes in v4:
time: 535 us; the launch traced here: 530 us
  waiting for transfers between devices  298 us (56%)
  starting transfers between devices  101 us (19%)
  Pallas kernels  80.9 us (15%)
  local copies, waits for them, and re-layouts  24 us (4%)
  other arithmetic  22.8 us (4%)
    ppermute x69, waiting for transfers between devices, swap(): return lax.ppermute(value, 'dp', [(i, i ^ bit) for i in range(ways)])  233 us
    pallas_call x10, Pallas kernels, call(): pl.pallas_call(kernel, out_shape=[jax.ShapeDtypeStruct(s, d) for s, d in...  69.8 us
    ppermute x69, starting transfers between devices, swap(): return lax.ppermute(value, 'dp', [(i, i ^ bit) for i in range(ways)])  60.5 us
    ppermute x13, waiting for transfers between devices, swap_tp(): return lax.ppermute(value, 'tp', [(0, 1), (1, 0)])  38.6 us
    all_to_all x7, starting transfers between devices, trade(): lax.all_to_all(value, 'dp', 0, 0, axis_index_groups=quads, tiled=True)  28.7 us
    all_to_all x7, waiting for transfers between devices, trade(): lax.all_to_all(value, 'dp', 0, 0, axis_index_groups=quads, tiled=True)  26.9 us
    unnamed x196, local copies, waits for them, and re-layouts  16.9 us
    ppermute x13, starting transfers between devices, swap_tp(): return lax.ppermute(value, 'tp', [(0, 1), (1, 0)])  12.1 us
  transfers between devices with their start and end apart: 89, of which 37 were waited for; matrix products, arithmetic and copies ran while one was open for 5% of the time, Pallas kernels for 12%

profile of v4, /device:TPU:0, one launch (start us, length us, event | category | flops | bytes accessed | tf_op | source)
XLA Modules:
  0.0 529.6 jit_solution(13576114957168813164)
XLA Ops:
  2.8 5.4 %all-to-all-start = ((bf16[4,128,768]{2,1,0:T(8,128)(2,1)}), bf16[4,128,768]{2,1,0:T(8,128)(2,1)S(1)}, u32[]{:S(2)}, u32[]{:S(2)}) async-start(bf16[4,128,768]{2,1,0:T(8,128)(2,1)} %pack1.1.refs_5_), calls=%async_computation | async-start | bytes 1572864 | tf_op jit(solution)/shard_map/t_first/all_to_all | solution.py:235
  10.4 3.0 collective-permute-start
  13.4 27.1 %collective-permute-done.refs_2_.refs_1_ = bf16[64,2048]{1,0:T(8,128)(2,1)S(1)} collective-permute-done((bf16[64,2048]{1,0:T(8,128)(2,1)}, bf16[64,2048]{1,0:T(8,128)(2,1)S(1)}, u32[]{:S(2)}, u32[]{:S(2)}) %collective-permute-start) | collective-permute-done | bytes 262176 | tf_op jit(solution)/shard_map/g_norm1/swap8/ppermute | solution.py:227
  41.5 3.5 all-to-all-start.1
  47.6 6.6 %collective-permute-done.1.refs_2_ = bf16[64,2048]{1,0:T(8,128)(2,1)S(1)} collective-permute-done((bf16[64,2048]{1,0:T(8,128)(2,1)S(1)}, bf16[64,2048]{1,0:T(8,128)(2,1)S(1)}, u32[]{:S(2)}, u32[]{:S(2)}) %collective-permute-start.1) | collective-permute-done | bytes 262176 | tf_op jit(solution)/shard_map/g_norm1/swaptp/ppermute | solution.py:231
  54.2 10.8 %all-to-all-done.1 = bf16[4,128,768]{2,1,0:T(8,128)(2,1)S(1)} async-done(((bf16[4,128,768]{2,1,0:T(8,128)(2,1)}), bf16[4,128,768]{2,1,0:T(8,128)(2,1)S(1)}, u32[]{:S(2)}, u32[]{:S(2)}) %all-to-all-start.1) | async-done | bytes 786464 | tf_op jit(solution)/shard_map/t_gate/all_to_all | solution.py:235
  66.1 3.5 all-to-all-start.2
  74.0 11.0 %collective-permute-done.10.refs_13_.refs_5_ = bf16[512,256]{1,0:T(8,128)(2,1)S(1)} collective-permute-done((bf16[512,256]{1,0:T(8,128)(2,1)S(1)}, bf16[512,256]{1,0:T(8,128)(2,1)S(1)}, u32[]{:S(2)}, u32[]{:S(2)}) %collective-permute-start.10) | collective-permute-done | bytes 262176 | tf_op jit(solution)/shard_map/s_kv/swap4/ppermute | solution.py:227
  93.1 5.0 collective-permute-done.9.refs_11_.refs_3_
  98.8 5.3 %project.1 = (bf16[512,2048]{1,0:T(8,128)(2,1)}, bf16[512,256]{1,0:T(8,128)(2,1)}, bf16[512,256]{1,0:T(8,128)(2,1)}, f32[512,256]{1,0:T(8,128)}, f32[512,128]{1,0:T(8,128)}) custom-call(bf16[64,2048]{1,0:T(8,128)(2,1)} %get-tuple-element.83.refs_0_, bf16[64,2048]{1,0:T(8,128)(2,1)} %copy-done.15, bf16[64,2048]{1,0:T(8,128)(2,1)} %copy-done.79, ...), custom_call_target="tpu_custom_call" | custom-call | tf_op jit(solution)/shard_map/project/pallas_call | solution.py:121
  108.3 4.1 collective-permute-done.14.refs_2_.refs_10_
  113.0 3.7 all-to-all-start.3
  118.2 9.5 %collective-permute-done.18.refs_7_.refs_15_ = bf16[512,256]{1,0:T(8,128)(2,1)S(1)} collective-permute-done((bf16[512,256]{1,0:T(8,128)(2,1)S(1)}, bf16[512,256]{1,0:T(8,128)(2,1)S(1)}, u32[]{:S(2)}, u32[]{:S(2)}) %collective-permute-start.18) | collective-permute-done | bytes 262176 | tf_op jit(solution)/shard_map/s_o/swap4/ppermute | solution.py:227
  127.7 7.0 %collective-permute-done.13.refs_1_.refs_9_ = bf16[512,256]{1,0:T(8,128)(2,1)S(1)} collective-permute-done((bf16[512,256]{1,0:T(8,128)(2,1)}, bf16[512,256]{1,0:T(8,128)(2,1)S(1)}, u32[]{:S(2)}, u32[]{:S(2)}) %collective-permute-start.13) | collective-permute-done | bytes 262176 | tf_op jit(solution)/shard_map/s_keys/swap4/ppermute | solution.py:227
  134.8 4.0 collective-permute-done.15.refs_3_.refs_11_
  139.5 7.4 %attend.1 = (f32[512,256]{1,0:T(8,128)}, f32[2,512,1]{2,1,0:T(8,128)}, bf16[2,128,2048]{2,1,0:T(8,128)(2,1)}, bf16[2,128,2048]{2,1,0:T(8,128)(2,1)}) custom-call(bf16[512,256]{1,0:T(8,128)(2,1)} %get-tuple-element.84.refs_0_.refs_8_, bf16[512,256]{1,0:T(8,128)(2,1)} %copy-done.71, bf16[512,256]{1,0:T(8,128)(2,1)} %copy-done.68, bf16[512,256]{1,0:T(8,128)(2,1)} %copy-done.72, ...), custom_call_target="tpu_custom_call" | custom-call | tf_op jit(solution)/shard_map/attend/pallas_call | solution.py:121
  149.0 7.0 %collective-permute-done.25.refs_6_.refs_10_ = bf16[64,2048]{1,0:T(8,128)(2,1)} collective-permute-done((bf16[64,2048]{1,0:T(8,128)(2,1)S(1)}, bf16[64,2048]{1,0:T(8,128)(2,1)}, u32[]{:S(2)}, u32[]{:S(2)}) %collective-permute-start.25) | collective-permute-done | bytes 262176 | tf_op jit(solution)/shard_map/g_cot/swaptp/ppermute | solution.py:231
  156.0 6.7 %collective-permute-done.22.refs_3_.refs_5_.refs_9_ = bf16[64,2048]{1,0:T(8,128)(2,1)} collective-permute-done((bf16[64,2048]{1,0:T(8,128)(2,1)S(1)}, bf16[64,2048]{1,0:T(8,128)(2,1)}, u32[]{:S(2)}, u32[]{:S(2)}) %collective-permute-start.22) | collective-permute-done | bytes 262176 | tf_op jit(solution)/shard_map/g_cot/swap8/ppermute | solution.py:227
  162.6 4.2 collective-permute-done.20.refs_2_.refs_14_.refs_18_
  173.4 2.7 collective-permute-done.26.refs_7_.refs_11_
  176.2 10.9 %collective-permute-done.21.refs_1_ = bf16[2,64,2048]{2,1,0:T(8,128)(2,1)S(1)} collective-permute-done((bf16[2,64,2048]{2,1,0:T(8,128)(2,1)}, bf16[2,64,2048]{2,1,0:T(8,128)(2,1)S(1)}, u32[]{:S(2)}, u32[]{:S(2)}) %collective-permute-start.21) | collective-permute-done | bytes 524320 | tf_op jit(solution)/shard_map/rs1/swaptp/ppermute | solution.py:231
  191.9 6.9 %collective-permute-done.31.refs_15_.refs_19_ = bf16[512,768]{1,0:T(8,128)(2,1)S(1)} collective-permute-done((bf16[512,768]{1,0:T(8,128)(2,1)S(1)}, bf16[512,768]{1,0:T(8,128)(2,1)S(1)}, u32[]{:S(2)}, u32[]{:S(2)}) %collective-permute-start.31) | collective-permute-done | bytes 786464 | tf_op jit(solution)/shard_map/s_gate/swap4/ppermute | solution.py:227
  200.4 15.3 %collective-permute-done.32.refs_16_.refs_21_ = bf16[512,768]{1,0:T(8,128)(2,1)S(1)} collective-permute-done((bf16[512,768]{1,0:T(8,128)(2,1)}, bf16[512,768]{1,0:T(8,128)(2,1)S(1)}, u32[]{:S(2)}, u32[]{:S(2)}) %collective-permute-start.32) | collective-permute-done | bytes 786464 | tf_op jit(solution)/shard_map/s_up/swap4/ppermute | solution.py:227
  217.2 12.8 %collective-permute-done.24 = bf16[2,32,2048]{2,1,0:T(8,128)(2,1)S(1)} collective-permute-done((bf16[2,32,2048]{2,1,0:T(8,128)(2,1)S(1)}, bf16[2,32,2048]{2,1,0:T(8,128)(2,1)S(1)}, u32[]{:S(2)}, u32[]{:S(2)}) %collective-permute-start.24) | collective-permute-done | bytes 262176 | tf_op jit(solution)/shard_map/rs1/swap8/ppermute | solution.py:227
  230.4 3.5 collective-permute-start.36
  234.4 17.4 %collective-permute-done.36.refs_1_ = bf16[64,2048]{1,0:T(8,128)(2,1)S(1)} collective-permute-done((bf16[64,2048]{1,0:T(8,128)(2,1)S(1)}, bf16[64,2048]{1,0:T(8,128)(2,1)S(1)}, u32[]{:S(2)}, u32[]{:S(2)}) %collective-permute-start.36) | collective-permute-done | bytes 262176 | tf_op jit(solution)/shard_map/g_norm2/swap8/ppermute | solution.py:227
  254.5 4.7 collective-permute-done.38.refs_3_
  261.6 15.7 %feed.1 = (bf16[512,2048]{1,0:T(8,128)(2,1)}, bf16[512,2048]{1,0:T(8,128)(2,1)}, bf16[512,768]{1,0:T(8,128)(2,1)}, bf16[512,768]{1,0:T(8,128)(2,1)}, bf16[512,76...) custom-call(bf16[64,2048]{1,0:T(8,128)(2,1)} %copy-done.45, ...), custom_call_target="tpu_custom_call" | custom-call | tf_op jit(solution)/shard_map/feed/pallas_call | solution.py:121
  277.9 7.3 %w_gate_up.1 = (bf16[2,512,768]{2,1,0:T(8,128)(2,1)}, bf16[2,512,768]{2,1,0:T(8,128)(2,1)}, bf16[2,512,768]{2,1,0:T(8,128)(2,1)}, bf16[2,512,768]{2,1,0:T(8,128)(2,1)}) custom-call(bf16[512,2048]{1,0:T(8,128)(2,1)} %get-tuple-element.107.refs_0_, bf16[512,768]{1,0:T(8,128)(2,1)} %get-tuple-element.108.refs_1_, bf16[512,768]{1,0:T(8,128)(2,1)} %get-tuple-element.109.refs_2_), custom_call_target="tpu_custom_call" | custom-call | tf_op jit(solution)/shard_map/w_gate_up/pallas_call | solution.py:121
  289.0 5.4 %feed_out.1 = (bf16[2,128,2048]{2,1,0:T(8,128)(2,1)}, bf16[2,128,2048]{2,1,0:T(8,128)(2,1)}) custom-call(bf16[4,768,128]{2,1,0:T(8,128)(2,1)} %copy-done.2, bf16[4,768,128]{2,1,0:T(8,128)(2,1)} %copy-done.55, bf16[4,768,128]{2,1,0:T(8,128)(2,1)} %copy-done.54, bf16[4,768,128]{2,1,0:T(8,128)(2,1)} %copy-done.56, ...), custom_call_target="tpu_custom_call" | custom-call | tf_op jit(solution)/shard_map/feed_out/pallas_call | solution.py:121
  294.4 5.5 %w_down.1 = (bf16[2,4,768,128]{3,2,1,0:T(8,128)(2,1)}, bf16[2,4,768,128]{3,2,1,0:T(8,128)(2,1)}) custom-call(bf16[512,768]{1,0:T(8,128)(2,1)} %get-tuple-element.96.refs_4_.refs_0_, bf16[512,2048]{1,0:T(8,128)(2,1)} %get-tuple-element.111.refs_1_), custom_call_target="tpu_custom_call" | custom-call | tf_op jit(solution)/shard_map/w_down/pallas_call | solution.py:121
  301.9 2.5 collective-permute-start.49
  304.4 23.2 %collective-permute-done.64 = bf16[2,512,768]{2,1,0:T(8,128)(2,1)} collective-permute-done((bf16[2,512,768]{2,1,0:T(8,128)(2,1)}, bf16[2,512,768]{2,1,0:T(8,128)(2,1)}, u32[]{:S(2)}, u32[]{:S(2)}) %collective-permute-start.64) | collective-permute-done | bytes 1572896 | tf_op jit(solution)/shard_map/r_up/swap4/ppermute | solution.py:227
  336.4 11.5 %collective-permute-done.50.refs_1_ = bf16[64,2048]{1,0:T(8,128)(2,1)S(1)} collective-permute-done((bf16[64,2048]{1,0:T(8,128)(2,1)S(1)}, bf16[64,2048]{1,0:T(8,128)(2,1)S(1)}, u32[]{:S(2)}, u32[]{:S(2)}) %collective-permute-start.50) | collective-permute-done | bytes 262176 | tf_op jit(solution)/shard_map/g_branch/swap8/ppermute | solution.py:227
  353.3 3.4 collective-permute-done.52.refs_3_
  362.0 11.6 %attend_back.1 = (bf16[512,2048]{1,0:T(8,128)(2,1)}, bf16[512,256]{1,0:T(8,128)(2,1)}, f32[1,128]{1,0:T(1,128)}, bf16[2,512,128]{2,1,0:T(8,128)(2,1)}, bf16[2,51...) custom-call(bf16[64,2048]{1,0:T(8,128)(2,1)} %copy-done.36, ...), custom_call_target="tpu_custom_call" | custom-call | tf_op jit(solution)/shard_map/attend_back/pallas_call | solution.py:121
  385.0 3.5 collective-permute-done.61
  388.5 13.5 %collective-permute-done.59 = bf16[1,512,128]{2,1,0:T(8,128)(2,1)S(1)} collective-permute-done((bf16[1,512,128]{2,1,0:T(8,128)(2,1)S(1)}, bf16[1,512,128]{2,1,0:T(8,128)(2,1)S(1)}, u32[]{:S(2)}, u32[]{:S(2)}) %collective-permute-start.59) | collective-permute-done | bytes 131104 | tf_op jit(solution)/shard_map/r_k/swap4/ppermute | solution.py:227
  403.1 7.2 %project_back.1 = (bf16[2,128,2048]{2,1,0:T(8,128)(2,1)}, bf16[2,128,2048]{2,1,0:T(8,128)(2,1)}, f32[1,2048]{1,0:T(1,128)}, bf16[2,512,256]{2,1,0:T(8,128)(2,1)}...) custom-call(bf16[512,256]{1,0:T(8,128)(2,1)} %copy-done.58, ...), custom_call_target="tpu_custom_call" | custom-call | tf_op jit(solution)/shard_map/project_back/pallas_call | solution.py:121
  414.5 4.2 all-to-all-start.6
  420.8 13.4 %collective-permute-done.57 = bf16[2,32,2048]{2,1,0:T(8,128)(2,1)S(1)} collective-permute-done((bf16[2,32,2048]{2,1,0:T(8,128)(2,1)S(1)}, bf16[2,32,2048]{2,1,0:T(8,128)(2,1)S(1)}, u32[]{:S(2)}, u32[]{:S(2)}) %collective-permute-start.57) | collective-permute-done | bytes 262176 | tf_op jit(solution)/shard_map/rs3/swap8/ppermute | solution.py:227
  436.5 2.9 collective-permute-start.68
  440.3 13.5 %collective-permute-done.68 = bf16[2,32,2048]{2,1,0:T(8,128)(2,1)S(1)} collective-permute-done((bf16[2,32,2048]{2,1,0:T(8,128)(2,1)S(1)}, bf16[2,32,2048]{2,1,0:T(8,128)(2,1)S(1)}, u32[]{:S(2)}, u32[]{:S(2)}) %collective-permute-start.68) | collective-permute-done | bytes 262176 | tf_op jit(solution)/shard_map/rs4/swap8/ppermute | solution.py:227
  453.9 4.9 all-to-all-start.4
  467.4 15.5 %collective-permute-done.79 = f32[34,128]{1,0:T(8,128)S(1)} collective-permute-done((f32[34,128]{1,0:T(8,128)S(1)}, f32[34,128]{1,0:T(8,128)S(1)}, u32[]{:S(2)}, u32[]{:S(2)}) %collective-permute-start.79) | collective-permute-done | bytes 17440 | tf_op jit(solution)/shard_map/swap4/ppermute | solution.py:227
  486.7 5.3 %collective-permute-start.81 = (f32[34,128]{1,0:T(8,128)S(1)}, f32[34,128]{1,0:T(8,128)S(1)}, u32[]{:S(2)}, u32[]{:S(2)}) collective-permute-start(f32[34,128]{1,0:T(8,128)S(1)} %add.564), channel_id=1, source_target_pairs={{0,8},{1,9},{2,10},{3,11},{4,12},{5,13},{6,14},{7,15},{8,0},{9,1},... | collective-permute-start | bytes 52232 | tf_op jit(solution)/shard_map/swap8/ppermute | solution.py:227
  502.6 3.5 all-to-all-start.5
  509.9 16.1 %all-to-all-done.5 = bf16[4,128,768]{2,1,0:T(8,128)(2,1)S(1)} async-done(((bf16[4,128,768]{2,1,0:T(8,128)(2,1)}), bf16[4,128,768]{2,1,0:T(8,128)(2,1)S(1)}, u32[]{:S(2)}, u32[]{:S(2)}) %all-to-all-start.5) | async-done | bytes 786464 | tf_op jit(solution)/shard_map/t_dqkv/all_to_all | solution.py:235
  (406 shorter events, 129.0 us)
Async XLA Ops:
  2.8 37.7 %all-to-all-start = ((bf16[4,128,768]{2,1,0:T(8,128)(2,1)}), bf16[4,128,768]{2,1,0:T(8,128)(2,1)S(1)}, u32[]{:S(2)}, u32[]{:S(2)}) async-start(bf16[4,128,768]{2,1,0:T(8,128)(2,1)} %pack1.1.refs_5_), calls=%async_computation | async-start | bytes 1572864 | tf_op jit(solution)/shard_map/t_first/all_to_all | solution.py:235
  10.4 30.1 %collective-permute-start = (bf16[64,2048]{1,0:T(8,128)(2,1)}, bf16[64,2048]{1,0:T(8,128)(2,1)S(1)}, u32[]{:S(2)}, u32[]{:S(2)}) collective-permute-start(bf16[64,2048]{1,0:T(8,128)(2,1)} %get-tuple-element.83.refs_0_), channel_id=1, source_target_pairs={{0,8},{1,9},{2,10},{3,11},{4,12},{5,13},{6,14},{7,15},{8,0},{9,1},... | collective-permute-start | bytes 786440 | tf_op jit(solution)/shard_map/g_norm1/swap8/ppermute | solution.py:227
  41.5 23.5 %all-to-all-start.1 = ((bf16[4,128,768]{2,1,0:T(8,128)(2,1)}), bf16[4,128,768]{2,1,0:T(8,128)(2,1)S(1)}, u32[]{:S(2)}, u32[]{:S(2)}) async-start(bf16[4,128,768]{2,1,0:T(8,128)(2,1)} %pack2.1), calls=%async_computation.1 | async-start | bytes 1572864 | tf_op jit(solution)/shard_map/t_gate/all_to_all | solution.py:235
  46.5 23.3 %collective-permute-start.3 = (bf16[64,2048]{1,0:T(8,128)(2,1)S(1)}, bf16[64,2048]{1,0:T(8,128)(2,1)}, u32[]{:S(2)}, u32[]{:S(2)}) collective-permute-start(bf16[64,2048]{1,0:T(8,128)(2,1)S(1)} %copy-done.78), channel_id=1, source_target_pairs={{0,1},{1,0},{2,3},{3,2},{4,5},{5,4},{6,7},{7,6},{8,9},{9,8},{10,11... | collective-permute-start | bytes 786440 | tf_op jit(solution)/shard_map/g_norm1/swap1/ppermute | solution.py:227
  46.7 25.5 %collective-permute-start.4 = (bf16[64,2048]{1,0:T(8,128)(2,1)S(1)}, bf16[64,2048]{1,0:T(8,128)(2,1)}, u32[]{:S(2)}, u32[]{:S(2)}) collective-permute-start(bf16[64,2048]{1,0:T(8,128)(2,1)S(1)} %collective-permute-done.refs_2_.refs_1_), channel_id=1, source_target_pairs={{0,1},{1,0},{2,3},{3,2},{4,5},{5,4},{6,7},{7,6},{8,9},{9,8},{10,11... | collective-permute-start | bytes 786440 | tf_op jit(solution)/shard_map/g_norm1/swap1/ppermute | solution.py:227
  47.1 24.4 %collective-permute-start.2 = (bf16[64,2048]{1,0:T(8,128)(2,1)S(1)}, bf16[64,2048]{1,0:T(8,128)(2,1)}, u32[]{:S(2)}, u32[]{:S(2)}) collective-permute-start(bf16[64,2048]{1,0:T(8,128)(2,1)S(1)} %collective-permute-done.refs_2_.refs_1_), channel_id=1, source_target_pairs={{0,16},{16,0},{1,17},{17,1},{2,18},{18,2},{3,19},{19,3},{4,20},{20... | collective-permute-start | bytes 786440 | tf_op jit(solution)/shard_map/g_norm1/swaptp/ppermute | solution.py:231
  54.2 17.5 %collective-permute-start.5 = (bf16[64,2048]{1,0:T(8,128)(2,1)S(1)}, bf16[64,2048]{1,0:T(8,128)(2,1)}, u32[]{:S(2)}, u32[]{:S(2)}) collective-permute-start(bf16[64,2048]{1,0:T(8,128)(2,1)S(1)} %collective-permute-done.1.refs_2_), channel_id=1, source_target_pairs={{0,1},{1,0},{2,3},{3,2},{4,5},{5,4},{6,7},{7,6},{8,9},{9,8},{10,11... | collective-permute-start | bytes 786440 | tf_op jit(solution)/shard_map/g_norm1/swap1/ppermute | solution.py:227
  66.1 46.8 %all-to-all-start.2 = ((bf16[4,128,768]{2,1,0:T(8,128)(2,1)}), bf16[4,128,768]{2,1,0:T(8,128)(2,1)S(1)}, u32[]{:S(2)}, u32[]{:S(2)}) async-start(bf16[4,128,768]{2,1,0:T(8,128)(2,1)} %pack3.1), calls=%async_computation.2 | async-start | bytes 1572864 | tf_op jit(solution)/shard_map/t_up/all_to_all | solution.py:235
  71.4 19.5 %collective-permute-start.6 = (bf16[64,2048]{1,0:T(8,128)(2,1)}, bf16[64,2048]{1,0:T(8,128)(2,1)S(1)}, u32[]{:S(2)}, u32[]{:S(2)}) collective-permute-start(bf16[64,2048]{1,0:T(8,128)(2,1)} %collective-permute-done.2.refs_3_), channel_id=1, source_target_pairs={{0,1},{1,0},{2,3},{3,2},{4,5},{5,4},{6,7},{7,6},{8,9},{9,8},{10,11... | collective-permute-start | bytes 786440 | tf_op jit(solution)/shard_map/g_norm1/swap1/ppermute | solution.py:227
  71.7 19.8 %collective-permute-start.11 = (bf16[512,256]{1,0:T(8,128)(2,1)S(1)}, bf16[512,256]{1,0:T(8,128)(2,1)S(1)}, u32[]{:S(2)}, u32[]{:S(2)}) collective-permute-start(bf16[512,256]{1,0:T(8,128)(2,1)S(1)} %get-tuple-element.189.refs_12_.refs_4_), channel_id=1, source_target_pairs={{0,2},{1,3},{2,0},{3,1},{4,6},{5,7},{6,4},{7,5},{8,10},{9,11},{10,... | collective-permute-start | bytes 786440 | tf_op jit(solution)/shard_map/s_kv/swap2/ppermute | solution.py:227
  72.2 20.7 %collective-permute-start.7 = (bf16[512,256]{1,0:T(8,128)(2,1)S(1)}, bf16[512,256]{1,0:T(8,128)(2,1)S(1)}, u32[]{:S(2)}, u32[]{:S(2)}) collective-permute-start(bf16[512,256]{1,0:T(8,128)(2,1)S(1)} %get-tuple-element.190.refs_8_.refs_0_), channel_id=1, source_target_pairs={{0,4},{1,5},{2,6},{3,7},{4,0},{5,1},{6,2},{7,3},{8,12},{9,13},{10,... | collective-permute-start | bytes 786440 | tf_op jit(solution)/shard_map/s_q/swap4/ppermute | solution.py:227
  106.2 21.5 %collective-permute-start.18 = (bf16[512,256]{1,0:T(8,128)(2,1)S(1)}, bf16[512,256]{1,0:T(8,128)(2,1)S(1)}, u32[]{:S(2)}, u32[]{:S(2)}) collective-permute-start(bf16[512,256]{1,0:T(8,128)(2,1)S(1)} %collective-permute-done.17.refs_6_.refs_14_), channel_id=1, source_target_pairs={{0,4},{1,5},{2,6},{3,7},{4,0},{5,1},{6,2},{7,3},{8,12},{9,13},{10,... | collective-permute-start | bytes 786440 | tf_op jit(solution)/shard_map/s_o/swap4/ppermute | solution.py:227
  107.9 26.9 %collective-permute-start.13 = (bf16[512,256]{1,0:T(8,128)(2,1)}, bf16[512,256]{1,0:T(8,128)(2,1)S(1)}, u32[]{:S(2)}, u32[]{:S(2)}) collective-permute-start(bf16[512,256]{1,0:T(8,128)(2,1)} %get-tuple-element.84.refs_0_.refs_8_), channel_id=1, source_target_pairs={{0,4},{1,5},{2,6},{3,7},{4,0},{5,1},{6,2},{7,3},{8,12},{9,13},{10,... | collective-permute-start | bytes 786440 | tf_op jit(solution)/shard_map/s_keys/swap4/ppermute | solution.py:227
  112.3 26.4 %collective-permute-start.15 = (bf16[512,256]{1,0:T(8,128)(2,1)S(1)}, bf16[512,256]{1,0:T(8,128)(2,1)S(1)}, u32[]{:S(2)}, u32[]{:S(2)}) collective-permute-start(bf16[512,256]{1,0:T(8,128)(2,1)S(1)} %collective-permute-done.14.refs_2_.refs_10_), channel_id=1, source_target_pairs={{0,4},{1,5},{2,6},{3,7},{4,0},{5,1},{6,2},{7,3},{8,12},{9,13},{10,... | collective-permute-start | bytes 786440 | tf_op jit(solution)/shard_map/s_keys/swap4/ppermute | solution.py:227
  113.0 59.2 %all-to-all-start.3 = ((bf16[4,768,128]{2,1,0:T(8,128)(2,1)}), bf16[4,768,128]{2,1,0:T(8,128)(2,1)S(1)}, u32[]{:S(2)}, u32[]{:S(2)}) async-start(bf16[4,768,128]{2,1,0:T(8,128)(2,1)} %bitcast.119), calls=%async_computation.3 | async-start | bytes 1572864 | tf_op jit(solution)/shard_map/t_down/all_to_all | solution.py:235
  146.8 20.0 %collective-permute-start.19 = (bf16[2,128,2048]{2,1,0:T(8,128)(2,1)}, bf16[2,128,2048]{2,1,0:T(8,128)(2,1)S(1)}, u32[]{:S(2)}, u32[]{:S(2)}) collective-permute-start(bf16[2,128,2048]{2,1,0:T(8,128)(2,1)} %get-tuple-element.87), channel_id=1, source_target_pairs={{0,1},{1,0},{2,3},{3,2},{4,5},{5,4},{6,7},{7,6},{8,9},{9,8},{10,11... | collective-permute-start | bytes 3145736 | tf_op jit(solution)/shard_map/rs1/swap1/ppermute | solution.py:227
  146.9 20.0 %collective-permute-start.20 = (bf16[512,768]{1,0:T(8,128)(2,1)S(1)}, bf16[512,768]{1,0:T(8,128)(2,1)S(1)}, u32[]{:S(2)}, u32[]{:S(2)}) collective-permute-start(bf16[512,768]{1,0:T(8,128)(2,1)S(1)} %bitcast.101), channel_id=1, source_target_pairs={{0,2},{1,3},{2,0},{3,1},{4,6},{5,7},{6,4},{7,5},{8,10},{9,11},{10,... | collective-permute-start | bytes 2359304 | tf_op jit(solution)/shard_map/s_gate/swap2/ppermute | solution.py:227
  149.0 27.1 %collective-permute-start.23 = (bf16[512,768]{1,0:T(8,128)(2,1)S(1)}, bf16[512,768]{1,0:T(8,128)(2,1)S(1)}, u32[]{:S(2)}, u32[]{:S(2)}) collective-permute-start(bf16[512,768]{1,0:T(8,128)(2,1)S(1)} %bitcast.102), channel_id=1, source_target_pairs={{0,4},{1,5},{2,6},{3,7},{4,0},{5,1},{6,2},{7,3},{8,12},{9,13},{10,... | collective-permute-start | bytes 2359304 | tf_op jit(solution)/shard_map/s_gate/swap4/ppermute | solution.py:227
  172.2 19.7 %collective-permute-start.34 = (bf16[4,768,128]{2,1,0:T(8,128)(2,1)S(1)}, bf16[4,768,128]{2,1,0:T(8,128)(2,1)S(1)}, u32[]{:S(2)}, u32[]{:S(2)}) collective-permute-start(bf16[4,768,128]{2,1,0:T(8,128)(2,1)S(1)} %all-to-all-done.3.refs_2_.refs_24_.refs_0_), channel_id=1, source_target_pairs={{0,2},{1,3},{2,0},{3,1},{4,6},{5,7},{6,4},{7,5},{8,10},{9,11},{10,... | collective-permute-start | bytes 2359304 | tf_op jit(solution)/shard_map/s_down/swap2/ppermute | solution.py:227
  172.8 26.0 %collective-permute-start.31 = (bf16[512,768]{1,0:T(8,128)(2,1)S(1)}, bf16[512,768]{1,0:T(8,128)(2,1)S(1)}, u32[]{:S(2)}, u32[]{:S(2)}) collective-permute-start(bf16[512,768]{1,0:T(8,128)(2,1)S(1)} %collective-permute-done.20.refs_2_.refs_14_.refs_18_), channel_id=1, source_target_pairs={{0,4},{1,5},{2,6},{3,7},{4,0},{5,1},{6,2},{7,3},{8,12},{9,13},{10,... | collective-permute-start | bytes 2359304 | tf_op jit(solution)/shard_map/s_gate/swap4/ppermute | solution.py:227
  176.1 39.6 %collective-permute-start.32 = (bf16[512,768]{1,0:T(8,128)(2,1)}, bf16[512,768]{1,0:T(8,128)(2,1)S(1)}, u32[]{:S(2)}, u32[]{:S(2)}) collective-permute-start(bf16[512,768]{1,0:T(8,128)(2,1)} %bitcast.116), channel_id=1, source_target_pairs={{0,4},{1,5},{2,6},{3,7},{4,0},{5,1},{6,2},{7,3},{8,12},{9,13},{10,... | collective-permute-start | bytes 2359304 | tf_op jit(solution)/shard_map/s_up/swap4/ppermute | solution.py:227
  187.1 46.8 %collective-permute-start.33 = (bf16[4,768,128]{2,1,0:T(8,128)(2,1)S(1)}, bf16[4,768,128]{2,1,0:T(8,128)(2,1)S(1)}, u32[]{:S(2)}, u32[]{:S(2)}) collective-permute-start(bf16[4,768,128]{2,1,0:T(8,128)(2,1)S(1)} %all-to-all-done.3.refs_2_.refs_24_.refs_0_), channel_id=1, source_target_pairs={{0,4},{1,5},{2,6},{3,7},{4,0},{5,1},{6,2},{7,3},{8,12},{9,13},{10,... | collective-permute-start | bytes 2359304 | tf_op jit(solution)/shard_map/s_down/swap4/ppermute | solution.py:227
  189.7 40.4 %collective-permute-start.24 = (bf16[2,32,2048]{2,1,0:T(8,128)(2,1)S(1)}, bf16[2,32,2048]{2,1,0:T(8,128)(2,1)S(1)}, u32[]{:S(2)}, u32[]{:S(2)}) collective-permute-start(bf16[2,32,2048]{2,1,0:T(8,128)(2,1)S(1)} %get-tuple-element.92), channel_id=1, source_target_pairs={{0,8},{1,9},{2,10},{3,11},{4,12},{5,13},{6,14},{7,15},{8,0},{9,1},... | collective-permute-start | bytes 786440 | tf_op jit(solution)/shard_map/rs1/swap8/ppermute | solution.py:227
  191.9 62.0 %collective-permute-start.35 = (bf16[4,768,128]{2,1,0:T(8,128)(2,1)S(1)}, bf16[4,768,128]{2,1,0:T(8,128)(2,1)S(1)}, u32[]{:S(2)}, u32[]{:S(2)}) collective-permute-start(bf16[4,768,128]{2,1,0:T(8,128)(2,1)S(1)} %collective-permute-done.34.refs_26_.refs_2_), channel_id=1, source_target_pairs={{0,4},{1,5},{2,6},{3,7},{4,0},{5,1},{6,2},{7,3},{8,12},{9,13},{10,... | collective-permute-start | bytes 2359304 | tf_op jit(solution)/shard_map/s_down/swap4/ppermute | solution.py:227
  198.9 55.1 %collective-permute-start.43 = (bf16[512,768]{1,0:T(8,128)(2,1)S(1)}, bf16[512,768]{1,0:T(8,128)(2,1)S(1)}, u32[]{:S(2)}, u32[]{:S(2)}) collective-permute-start(bf16[512,768]{1,0:T(8,128)(2,1)S(1)} %bitcast.118), channel_id=1, source_target_pairs={{0,2},{1,3},{2,0},{3,1},{4,6},{5,7},{6,4},{7,5},{8,10},{9,11},{10,... | collective-permute-start | bytes 2359304 | tf_op jit(solution)/shard_map/s_up/swap2/ppermute | solution.py:227
  215.7 43.6 %collective-permute-start.44 = (bf16[512,768]{1,0:T(8,128)(2,1)S(1)}, bf16[512,768]{1,0:T(8,128)(2,1)S(1)}, u32[]{:S(2)}, u32[]{:S(2)}) collective-permute-start(bf16[512,768]{1,0:T(8,128)(2,1)S(1)} %collective-permute-done.32.refs_16_.refs_21_), channel_id=1, source_target_pairs={{0,2},{1,3},{2,0},{3,1},{4,6},{5,7},{6,4},{7,5},{8,10},{9,11},{10,... | collective-permute-start | bytes 2359304 | tf_op jit(solution)/shard_map/s_up/swap2/ppermute | solution.py:227
  230.4 21.4 %collective-permute-start.36 = (bf16[64,2048]{1,0:T(8,128)(2,1)S(1)}, bf16[64,2048]{1,0:T(8,128)(2,1)S(1)}, u32[]{:S(2)}, u32[]{:S(2)}) collective-permute-start(bf16[64,2048]{1,0:T(8,128)(2,1)S(1)} %get-tuple-element.95.refs_0_), channel_id=1, source_target_pairs={{0,8},{1,9},{2,10},{3,11},{4,12},{5,13},{6,14},{7,15},{8,0},{9,1},... | collective-permute-start | bytes 786440 | tf_op jit(solution)/shard_map/g_norm2/swap8/ppermute | solution.py:227
  233.8 20.6 %collective-permute-start.37 = (bf16[64,2048]{1,0:T(8,128)(2,1)S(1)}, bf16[64,2048]{1,0:T(8,128)(2,1)S(1)}, u32[]{:S(2)}, u32[]{:S(2)}) collective-permute-start(bf16[64,2048]{1,0:T(8,128)(2,1)S(1)} %get-tuple-element.95.refs_0_), channel_id=1, source_target_pairs={{0,16},{16,0},{1,17},{17,1},{2,18},{18,2},{3,19},{19,3},{4,20},{20... | collective-permute-start | bytes 786440 | tf_op jit(solution)/shard_map/g_norm2/swaptp/ppermute | solution.py:231
  285.3 42.3 %collective-permute-start.64 = (bf16[2,512,768]{2,1,0:T(8,128)(2,1)}, bf16[2,512,768]{2,1,0:T(8,128)(2,1)}, u32[]{:S(2)}, u32[]{:S(2)}) collective-permute-start(bf16[2,512,768]{2,1,0:T(8,128)(2,1)} %get-tuple-element.128), channel_id=1, source_target_pairs={{0,4},{1,5},{2,6},{3,7},{4,0},{5,1},{6,2},{7,3},{8,12},{9,13},{10,... | collective-permute-start | bytes 4718600 | tf_op jit(solution)/shard_map/r_up/swap4/ppermute | solution.py:227
  286.6 43.4 %collective-permute-start.62 = (bf16[2,512,768]{2,1,0:T(8,128)(2,1)}, bf16[2,512,768]{2,1,0:T(8,128)(2,1)}, u32[]{:S(2)}, u32[]{:S(2)}) collective-permute-start(bf16[2,512,768]{2,1,0:T(8,128)(2,1)} %get-tuple-element.110.refs_5_), channel_id=1, source_target_pairs={{0,2},{1,3},{2,0},{3,1},{4,6},{5,7},{6,4},{7,5},{8,10},{9,11},{10,... | collective-permute-start | bytes 4718600 | tf_op jit(solution)/shard_map/r_gate/swap2/ppermute | solution.py:227
  294.4 53.5 %collective-permute-start.45 = (bf16[2,128,2048]{2,1,0:T(8,128)(2,1)}, bf16[2,128,2048]{2,1,0:T(8,128)(2,1)}, u32[]{:S(2)}, u32[]{:S(2)}) collective-permute-start(bf16[2,128,2048]{2,1,0:T(8,128)(2,1)} %get-tuple-element.98), channel_id=1, source_target_pairs={{0,1},{1,0},{2,3},{3,2},{4,5},{5,4},{6,7},{7,6},{8,9},{9,8},{10,11... | collective-permute-start | bytes 3145736 | tf_op jit(solution)/shard_map/rs3/swap1/ppermute | solution.py:227
  299.9 73.8 %collective-permute-start.75 = (bf16[2,4,768,128]{3,2,1,0:T(8,128)(2,1)}, bf16[2,4,768,128]{3,2,1,0:T(8,128)(2,1)}, u32[]{:S(2)}, u32[]{:S(2)}) collective-permute-start(bf16[2,4,768,128]{3,2,1,0:T(8,128)(2,1)} %get-tuple-element.112.refs_6_), channel_id=1, source_target_pairs={{0,2},{1,3},{2,0},{3,1},{4,6},{5,7},{6,4},{7,5},{8,10},{9,11},{10,... | collective-permute-start | bytes 4718600 | tf_op jit(solution)/shard_map/r_down/swap2/ppermute | solution.py:227
  301.9 30.2 %collective-permute-start.49 = (bf16[2,32,2048]{2,1,0:T(8,128)(2,1)S(1)}, bf16[2,32,2048]{2,1,0:T(8,128)(2,1)S(1)}, u32[]{:S(2)}, u32[]{:S(2)}) collective-permute-start(bf16[2,32,2048]{2,1,0:T(8,128)(2,1)S(1)} %get-tuple-element.106), channel_id=1, source_target_pairs={{0,8},{1,9},{2,10},{3,11},{4,12},{5,13},{6,14},{7,15},{8,0},{9,1},... | collective-permute-start | bytes 786440 | tf_op jit(solution)/shard_map/rs2/swap8/ppermute | solution.py:227
  351.8 30.0 %collective-permute-start.65 = (bf16[1,512,768]{2,1,0:T(8,128)(2,1)}, bf16[1,512,768]{2,1,0:T(8,128)(2,1)S(1)}, u32[]{:S(2)}, u32[]{:S(2)}) collective-permute-start(bf16[1,512,768]{2,1,0:T(8,128)(2,1)} %get-tuple-element.184), channel_id=1, source_target_pairs={{0,2},{1,3},{2,0},{3,1},{4,6},{5,7},{6,4},{7,5},{8,10},{9,11},{10,... | collective-permute-start | bytes 2359304 | tf_op jit(solution)/shard_map/r_up/swap2/ppermute | solution.py:227
  353.3 28.5 %collective-permute-start.63 = (bf16[1,512,768]{2,1,0:T(8,128)(2,1)}, bf16[1,512,768]{2,1,0:T(8,128)(2,1)S(1)}, u32[]{:S(2)}, u32[]{:S(2)}) collective-permute-start(bf16[1,512,768]{2,1,0:T(8,128)(2,1)} %get-tuple-element.186), channel_id=1, source_target_pairs={{0,4},{1,5},{2,6},{3,7},{4,0},{5,1},{6,2},{7,3},{8,12},{9,13},{10,... | collective-permute-start | bytes 2359304 | tf_op jit(solution)/shard_map/r_gate/swap4/ppermute | solution.py:227
  359.8 18.8 %collective-permute-start.46 = (bf16[2,64,2048]{2,1,0:T(8,128)(2,1)S(1)}, bf16[2,64,2048]{2,1,0:T(8,128)(2,1)}, u32[]{:S(2)}, u32[]{:S(2)}) collective-permute-start(bf16[2,64,2048]{2,1,0:T(8,128)(2,1)S(1)} %get-tuple-element.100.refs_25_), channel_id=1, source_target_pairs={{0,16},{16,0},{1,17},{17,1},{2,18},{18,2},{3,19},{19,3},{4,20},{20... | collective-permute-start | bytes 1572872 | tf_op jit(solution)/shard_map/rs3/swaptp/ppermute | solution.py:231
  378.6 33.4 %collective-permute-start.76 = (bf16[1,4,768,128]{3,2,1,0:T(8,128)(2,1)}, bf16[1,4,768,128]{3,2,1,0:T(8,128)(2,1)}, u32[]{:S(2)}, u32[]{:S(2)}) collective-permute-start(bf16[1,4,768,128]{3,2,1,0:T(8,128)(2,1)} %slice.247), channel_id=1, source_target_pairs={{0,4},{1,5},{2,6},{3,7},{4,0},{5,1},{6,2},{7,3},{8,12},{9,13},{10,... | collective-permute-start | bytes 2359304 | tf_op jit(solution)/shard_map/r_down/swap4/ppermute | solution.py:227
  410.4 23.9 %collective-permute-start.57 = (bf16[2,32,2048]{2,1,0:T(8,128)(2,1)S(1)}, bf16[2,32,2048]{2,1,0:T(8,128)(2,1)S(1)}, u32[]{:S(2)}, u32[]{:S(2)}) collective-permute-start(bf16[2,32,2048]{2,1,0:T(8,128)(2,1)S(1)} %get-tuple-element.119.refs_7_), channel_id=1, source_target_pairs={{0,8},{1,9},{2,10},{3,11},{4,12},{5,13},{6,14},{7,15},{8,0},{9,1},... | collective-permute-start | bytes 786440 | tf_op jit(solution)/shard_map/rs3/swap8/ppermute | solution.py:227
  414.5 39.4 %all-to-all-start.6 = ((bf16[4,768,128]{2,1,0:T(8,128)(2,1)}), bf16[4,768,128]{2,1,0:T(8,128)(2,1)}, u32[]{:S(2)}, u32[]{:S(2)}) async-start(bf16[4,768,128]{2,1,0:T(8,128)(2,1)} %fusion), calls=%async_computation.6 | async-start | bytes 1572864 | tf_op jit(solution)/shard_map/t_ddown/all_to_all | solution.py:235
  418.7 20.6 %collective-permute-start.73 = (bf16[2,512,256]{2,1,0:T(8,128)(2,1)S(1)}, bf16[2,512,256]{2,1,0:T(8,128)(2,1)S(1)}, u32[]{:S(2)}, u32[]{:S(2)}) collective-permute-start(bf16[2,512,256]{2,1,0:T(8,128)(2,1)S(1)} %copy-done.33), channel_id=1, source_target_pairs={{0,2},{1,3},{2,0},{3,1},{4,6},{5,7},{6,4},{7,5},{8,10},{9,11},{10,... | collective-permute-start | bytes 1572872 | tf_op jit(solution)/shard_map/r_out/swap2/ppermute | solution.py:227
  434.3 24.5 %collective-permute-start.69 = (bf16[2,512,256]{2,1,0:T(8,128)(2,1)}, bf16[2,512,256]{2,1,0:T(8,128)(2,1)}, u32[]{:S(2)}, u32[]{:S(2)}) collective-permute-start(bf16[2,512,256]{2,1,0:T(8,128)(2,1)} %get-tuple-element.140), channel_id=1, source_target_pairs={{0,2},{1,3},{2,0},{3,1},{4,6},{5,7},{6,4},{7,5},{8,10},{9,11},{10,... | collective-permute-start | bytes 1572872 | tf_op jit(solution)/shard_map/r_q/swap2/ppermute | solution.py:227
  435.5 30.7 %collective-permute-start.71 = (bf16[2,512,256]{2,1,0:T(8,128)(2,1)}, bf16[2,512,256]{2,1,0:T(8,128)(2,1)}, u32[]{:S(2)}, u32[]{:S(2)}) collective-permute-start(bf16[2,512,256]{2,1,0:T(8,128)(2,1)} %get-tuple-element.142), channel_id=1, source_target_pairs={{0,4},{1,5},{2,6},{3,7},{4,0},{5,1},{6,2},{7,3},{8,12},{9,13},{10,... | collective-permute-start | bytes 1572872 | tf_op jit(solution)/shard_map/r_kv/swap4/ppermute | solution.py:227
  436.5 17.3 %collective-permute-start.68 = (bf16[2,32,2048]{2,1,0:T(8,128)(2,1)S(1)}, bf16[2,32,2048]{2,1,0:T(8,128)(2,1)S(1)}, u32[]{:S(2)}, u32[]{:S(2)}) collective-permute-start(bf16[2,32,2048]{2,1,0:T(8,128)(2,1)S(1)} %get-tuple-element.136.refs_2_.refs_6_), channel_id=1, source_target_pairs={{0,8},{1,9},{2,10},{3,11},{4,12},{5,13},{6,14},{7,15},{8,0},{9,1},... | collective-permute-start | bytes 786440 | tf_op jit(solution)/shard_map/rs4/swap8/ppermute | solution.py:227
  440.3 57.9 %collective-permute-start.74 = (bf16[1,512,256]{2,1,0:T(8,128)(2,1)}, bf16[1,512,256]{2,1,0:T(8,128)(2,1)S(1)}, u32[]{:S(2)}, u32[]{:S(2)}) collective-permute-start(bf16[1,512,256]{2,1,0:T(8,128)(2,1)} %get-tuple-element.191), channel_id=1, source_target_pairs={{0,4},{1,5},{2,6},{3,7},{4,0},{5,1},{6,2},{7,3},{8,12},{9,13},{10,... | collective-permute-start | bytes 786440 | tf_op jit(solution)/shard_map/r_out/swap4/ppermute | solution.py:227
  453.9 45.7 %all-to-all-start.4 = ((bf16[4,128,1536]{2,1,0:T(8,128)(2,1)}), bf16[4,128,1536]{2,1,0:T(8,128)(2,1)S(1)}, u32[]{:S(2)}, u32[]{:S(2)}) async-start(bf16[4,128,1536]{2,1,0:T(8,128)(2,1)} %bitcast.24), calls=%async_computation.4 | async-start | bytes 3145728 | tf_op jit(solution)/shard_map/t_dgu/all_to_all | solution.py:235
  461.2 37.0 %collective-permute-start.70 = (bf16[1,512,256]{2,1,0:T(8,128)(2,1)S(1)}, bf16[1,512,256]{2,1,0:T(8,128)(2,1)S(1)}, u32[]{:S(2)}, u32[]{:S(2)}) collective-permute-start(bf16[1,512,256]{2,1,0:T(8,128)(2,1)S(1)} %get-tuple-element.195), channel_id=1, source_target_pairs={{0,4},{1,5},{2,6},{3,7},{4,0},{5,1},{6,2},{7,3},{8,12},{9,13},{10,... | collective-permute-start | bytes 786440 | tf_op jit(solution)/shard_map/r_q/swap4/ppermute | solution.py:227
  463.9 18.9 %collective-permute-start.79 = (f32[34,128]{1,0:T(8,128)S(1)}, f32[34,128]{1,0:T(8,128)S(1)}, u32[]{:S(2)}, u32[]{:S(2)}) collective-permute-start(f32[34,128]{1,0:T(8,128)S(1)} %fusion.38), channel_id=1, source_target_pairs={{0,4},{1,5},{2,6},{3,7},{4,0},{5,1},{6,2},{7,3},{8,12},{9,13},{10,... | collective-permute-start | bytes 52232 | tf_op jit(solution)/shard_map/swap4/ppermute | solution.py:227
  502.6 23.5 %all-to-all-start.5 = ((bf16[4,128,768]{2,1,0:T(8,128)(2,1)}), bf16[4,128,768]{2,1,0:T(8,128)(2,1)S(1)}, u32[]{:S(2)}, u32[]{:S(2)}) async-start(bf16[4,128,768]{2,1,0:T(8,128)(2,1)} %bitcast.25), calls=%async_computation.5 | async-start | bytes 1572864 | tf_op jit(solution)/shard_map/t_dqkv/all_to_all | solution.py:235
  (139 other events, 1754.6 us)
